TPU v7x, 32 devices: a whole 2x2x4 slice. The times are simulated.
32 devices in a mesh: grp: 2 (over y), basin: 4 (over z), chain: 2 (over x), mem: 2 (over core).
Axes of the slice: x: 2, y: 2, z: 4, core: 2. Of those that a mesh axis runs over, the one named last changes fastest.
Arguments:
- runoff: float32 [2, 64, 32, 2, 2048], P('mem', 'basin', 'grp', 'chain'), parts along dimension 2, may hold values from 0.002 to 0.02
- directions: int32 [32, 2, 2048], P(('grp', 'basin'), 'chain'), parts along dimension 0, may hold values from 0 to 2
Outputs:
- accumulation: float32 [128, 32, 2, 2048], P('mem', ('grp', 'basin'), 'chain'), parts along dimension 1
There are 2 independent parts, one for each index of `grp`. A program takes and returns all parts, laid end to end along the dimension named above; each array names one. Nothing has to cross between parts.
Inputs may be any that keep to these rules, and one draw needn't show every extreme that they name: `directions`: direction codes of forward three-direction routing: 0 east, 1 north-east, 2 south-east along the flow.
All inputs are finite; a program needn't handle non-finite values.
Results may differ from a plain program's by a relative error of at most 0.0003.
Values sent between devices are 32-bit elements; how exact they have to be, the bound alone decides.
No kernel may reach another device: no remote copies, remote signals or barrier semaphores. Data moves between devices by JAX's collectives and lax.ppermute only.
A program may use at most 128 MiB of HBM per device.

v0:
```python
import jax
import jax.numpy as jnp
from jax import lax
from jax.sharding import PartitionSpec as P

ROWS = 128


def from_behind(value, axis, by):
    count = lax.axis_size(axis)
    pairs = [(i, i + by) for i in range(count) if 0 <= i + by < count]
    return lax.ppermute(value, axis, pairs)


def target_rows(directions):
    cell_count = directions.shape[-1]
    row_ids = jnp.arange(cell_count, dtype=jnp.int32) % ROWS
    offsets = jnp.where(directions == 1, -1, jnp.where(directions == 2, 1, 0)).astype(jnp.int32)
    return jnp.clip(row_ids + offsets, 0, ROWS - 1)


def column_onehot(target_col, kind):
    lane_ids = jnp.arange(ROWS, dtype=jnp.int32)
    return (target_col[..., None] == lane_ids).astype(kind)


def sweep_tile(water_cols, targets, inflow):

    def advance(carried, column_data):
        water_col, target_col = column_data
        summed = water_col + carried
        passed = jnp.einsum(
            "mtj,tji->mti",
            summed,
            column_onehot(target_col, jnp.float32),
            precision=lax.Precision.HIGHEST,
        )
        return (passed, summed)

    return lax.scan(advance, inflow, (jnp.moveaxis(water_cols, 2, 0), jnp.moveaxis(targets, 1, 0)))


def section_matrix(targets):
    tile_count = targets.shape[0]
    start_map = jnp.broadcast_to(jnp.eye(ROWS, dtype=jnp.bfloat16), (tile_count, ROWS, ROWS))

    def chain_step(product, target_col):
        advanced = jnp.einsum(
            "tij,tjk->tik",
            product,
            column_onehot(target_col, jnp.bfloat16),
            preferred_element_type=jnp.float32,
        )
        return (advanced.astype(jnp.bfloat16), None)

    final_map, _ = lax.scan(chain_step, start_map, jnp.moveaxis(targets, 1, 0))
    return final_map.astype(jnp.float32)


def route_chain(water_cols, targets):
    member_count, tile_count = (water_cols.shape[0], water_cols.shape[1])
    no_inflow = jnp.zeros((member_count, tile_count, ROWS), jnp.float32)
    local_flow, _ = sweep_tile(water_cols, targets, no_inflow)
    panel_map = section_matrix(targets)

    def relay_step(counter, state):
        total_out, received = state
        received = from_behind(total_out, "chain", 1)
        total_out = local_flow + jnp.einsum(
            "mtj,tjk->mtk", received, panel_map, precision=lax.Precision.HIGHEST
        )
        return (total_out, received)

    _, inflow = lax.fori_loop(0, lax.axis_size("chain") - 1, relay_step, (local_flow, no_inflow))
    _, columns_out = sweep_tile(water_cols, targets, inflow)
    return columns_out


def local(runoff, directions):
    cell_count = runoff.shape[4]
    col_count = cell_count // ROWS
    regrouped = lax.all_to_all(runoff, "basin", split_axis=2, concat_axis=1, tiled=True)
    member_count, tile_count = (regrouped.shape[1], regrouped.shape[2])
    water_cols = regrouped.reshape(member_count, tile_count, col_count, ROWS)
    targets = target_rows(directions).reshape(tile_count, col_count, ROWS)
    columns_out = route_chain(water_cols, targets)
    return jnp.transpose(columns_out, (1, 2, 0, 3)).reshape(member_count, tile_count, 1, cell_count)


def solution(mesh):
    return jax.shard_map(
        local,
        mesh=mesh,
        in_specs=(P("mem", "basin", "grp", "chain", None), P(("grp", "basin"), "chain", None)),
        out_specs=P("mem", ("grp", "basin"), "chain", None),
        check_vma=False,
    )
```

profile of v0, /device:TPU:0, one launch (start us, length us, event | category | flops | bytes accessed | tf_op | source)
XLA Modules:
  0.0 95.5 jit_solution(6588446960508231606)
XLA Ops:
  0.0 5.1 %copy.10 = f32[1,16,16,1,2048]{4,3,1,0,2:T(1,128)} copy(f32[1,16,16,1,2048]{4,3,2,1,0:T(1,128)} %param.6) | data formatting | bytes 4194304 | tf_op args[0]
  5.1 6.4 %all-to-all-start = ((f32[1,16,16,1,2048]{4,3,1,0,2:T(1,128)}), f32[1,16,16,1,2048]{4,3,1,0,2:T(1,128)S(1)}, u32[]{:S(2)}, u32[]{:S(2)}) async-start(f32[1,16,16,1,2048]{4,3,1,0,2:T(1,128)} %copy.10), calls=%async_computation | async-start | bytes 4194304 | tf_op jit(solution)/shard_map/all_to_all | solution.py:82
  11.7 48.1 %all-to-all-done = f32[1,16,16,1,2048]{4,3,1,0,2:T(1,128)S(1)} async-done(((f32[1,16,16,1,2048]{4,3,1,0,2:T(1,128)}), f32[1,16,16,1,2048]{4,3,1,0,2:T(1,128)S(1)}, u32[]{:S(2)}, u32[]{:S(2)}) %all-to-all-start) | async-done | bytes 2097184 | tf_op jit(solution)/shard_map/all_to_all | solution.py:82
  59.8 0.9 copy.17
  60.9 0.4 copy.18
  61.3 0.7 copy.13
  62.0 6.4 %while.4 = (s32[]{:T(128)}, f32[64,4,128]{2,0,1:T(8,128)S(1)}, s32[16,4,128]{2,1,0:T(4,128)S(1)}, f32[16,64,4,128]{3,1,2,0:T(8,128)S(1)}, s32[]{:T(128)}) while((s32[]{:T(128)}, f32[64,4,128]{2,0,1:T(8,128)S(1)}, s32[16,4,128]{2,1,0:T(4,128)S(1)}, f32[16,64,4,128]{3,1,2,0:T(8,128)S(1)}, s32[]{:T(128)}) %tuple.38), condition=%wide.region_1.2_spmd, body=%wide.region_0.1_spmd.sunk | while | flops 50429952 | bytes 661581 | solution.py:40
  62.0 0.3 convolution_bitcast_fusion.4
  62.4 0.3 convolution_bitcast_fusion.4
  62.8 0.3 convolution_bitcast_fusion.4
  63.2 0.3 convolution_bitcast_fusion.4
  63.6 0.3 convolution_bitcast_fusion.4
  64.0 0.3 convolution_bitcast_fusion.4
  64.4 0.3 convolution_bitcast_fusion.4
  64.8 0.3 convolution_bitcast_fusion.4
  65.2 0.3 convolution_bitcast_fusion.4
  65.6 0.3 convolution_bitcast_fusion.4
  66.0 0.3 convolution_bitcast_fusion.4
  66.4 0.3 convolution_bitcast_fusion.4
  66.8 0.3 convolution_bitcast_fusion.4
  67.2 0.3 convolution_bitcast_fusion.4
  67.6 0.3 convolution_bitcast_fusion.4
  68.0 0.3 convolution_bitcast_fusion.4
  68.4 3.4 %collective-permute-start = (f32[64,4,128]{2,0,1:T(8,128)S(1)}, f32[64,4,128]{2,0,1:T(8,128)S(1)}, u32[]{:S(2)}, u32[]{:S(2)}) collective-permute-start(f32[64,4,128]{2,0,1:T(8,128)S(1)} %get-tuple-element.74), channel_id=1, source_target_pairs={{0,2},{1,3},{4,6},{5,7},{8,10},{9,11},{12,14},{13,15},{16,18},{17,... | collective-permute-start | bytes 393224 | tf_op jit(solution)/shard_map/while/body/eval_jaxpr/ppermute | solution.py:12
  71.8 2.5 %collective-permute-done = f32[64,4,128]{2,0,1:T(8,128)S(1)} collective-permute-done((f32[64,4,128]{2,0,1:T(8,128)S(1)}, f32[64,4,128]{2,0,1:T(8,128)S(1)}, u32[]{:S(2)}, u32[]{:S(2)}) %collective-permute-start) | collective-permute-done | bytes 131104 | tf_op jit(solution)/shard_map/while/body/eval_jaxpr/ppermute | solution.py:12
  74.3 17.1 %while.5 = (s32[]{:T(128)}, f32[64,4,128]{2,0,1:T(8,128)S(1)}, f32[16,64,4,128]{3,1,2,0:T(8,128)}, s32[16,4,128]{2,1,0:T(4,128)S(1)}, f32[16,64,4,128]{3,1,2,0:T(8,128)S(1)}, /*index=5*/s32[]{:T(128)}) while((s32[]{:T(128)}, f32[64,4,128]{2,0,1:T(8,128)S(1)}, f32[16,64,4,128]{3,1,2,0:T(8,128)}, s32[16,4,128]{2,1,0:T(4,128)S(1)}, ...), condition=%wide.region_3.4_spmd, body=%wide.region_2.3_spmd.sunk | while | flops 50462720 | bytes 1054809 | solution.py:40
  74.3 0.7 bitcast_dynamic-update-slice_fusion.2
  75.4 0.7 bitcast_dynamic-update-slice_fusion.2
  76.5 0.7 bitcast_dynamic-update-slice_fusion.2
  77.1 0.3 convolution_bitcast_fusion.5
  77.5 0.7 bitcast_dynamic-update-slice_fusion.2
  78.6 0.7 bitcast_dynamic-update-slice_fusion.2
  79.3 0.3 convolution_bitcast_fusion.5
  79.7 0.7 bitcast_dynamic-update-slice_fusion.2
  80.7 0.7 bitcast_dynamic-update-slice_fusion.2
  81.4 0.3 convolution_bitcast_fusion.5
  81.8 0.7 bitcast_dynamic-update-slice_fusion.2
  82.9 0.7 bitcast_dynamic-update-slice_fusion.2
  83.5 0.3 convolution_bitcast_fusion.5
  83.9 0.7 bitcast_dynamic-update-slice_fusion.2
  85.0 0.7 bitcast_dynamic-update-slice_fusion.2
  86.1 0.7 bitcast_dynamic-update-slice_fusion.2
  87.1 0.7 bitcast_dynamic-update-slice_fusion.2
  88.2 0.7 bitcast_dynamic-update-slice_fusion.2
  89.3 0.7 bitcast_dynamic-update-slice_fusion.2
  90.3 0.7 bitcast_dynamic-update-slice_fusion.2
  91.0 0.3 convolution_bitcast_fusion.5
  91.4 4.1 %copy.16 = f32[64,4,16,128]{3,2,1,0:T(8,128)} copy(f32[64,4,16,128]{3,0,1,2:T(8,128)} %bitcast.53) | data formatting | bytes 4194304 | tf_op jit(solution)/shard_map/transpose | solution.py:87
  (83 shorter events, 4.7 us)
Async XLA Ops:
  5.1 6.5 %copy-start = (s32[4,1,2048]{2,1,0:T(1,128)S(1)}, s32[4,1,2048]{2,1,0:T(1,128)}, u32[]{:S(2)}) copy-start(s32[4,1,2048]{2,1,0:T(1,128)} %param.7) | copy-start | bytes 98308
  5.1 54.6 %all-to-all-start = ((f32[1,16,16,1,2048]{4,3,1,0,2:T(1,128)}), f32[1,16,16,1,2048]{4,3,1,0,2:T(1,128)S(1)}, u32[]{:S(2)}, u32[]{:S(2)}) async-start(f32[1,16,16,1,2048]{4,3,1,0,2:T(1,128)} %copy.10), calls=%async_computation | async-start | bytes 4194304 | tf_op jit(solution)/shard_map/all_to_all | solution.py:82
  68.4 5.9 %collective-permute-start = (f32[64,4,128]{2,0,1:T(8,128)S(1)}, f32[64,4,128]{2,0,1:T(8,128)S(1)}, u32[]{:S(2)}, u32[]{:S(2)}) collective-permute-start(f32[64,4,128]{2,0,1:T(8,128)S(1)} %get-tuple-element.74), channel_id=1, source_target_pairs={{0,2},{1,3},{4,6},{5,7},{8,10},{9,11},{12,14},{13,15},{16,18},{17,... | collective-permute-start | bytes 393224 | tf_op jit(solution)/shard_map/while/body/eval_jaxpr/ppermute | solution.py:12
where the time goes:
time: 95.8 us; the launch traced here: 95.5 us
  waiting for transfers between devices  50.6 us (53%)
  local copies, waits for them, and re-layouts  12.1 us (13%)
  matrix products  10.9 us (11%)
  other arithmetic  10.8 us (11%)
  starting transfers between devices  9.85 us (10%)
  loops' own time  1.22 us (1%)
    all_to_all x1, waiting for transfers between devices, local(): lax.all_to_all(runoff, 'basin', split_axis=2, concat_axis=1, tiled=True)  48.1 us
    dot_general x32, matrix products, advance(): jnp.einsum('mtj,tji->mti', summed, column_onehot(target_col, jnp.float32)...  10.9 us
    dynamic_update_slice x16, other arithmetic, sweep_tile(): lax.scan(advance, inflow, (jnp.moveaxis(water_cols, 2, 0), jnp.moveaxis(t...  10.7 us
    all_to_all x1, starting transfers between devices, local(): lax.all_to_all(runoff, 'basin', split_axis=2, concat_axis=1, tiled=True)  6.45 us
    unnamed x5, local copies, waits for them, and re-layouts  6.37 us
    transpose x1, local copies, waits for them, and re-layouts, local(): jnp.transpose(columns_out, (1, 2, 0, 3))  4.13 us
    ppermute x1, starting transfers between devices, from_behind(): return lax.ppermute(value, axis, pairs)  3.4 us
    ppermute x1, waiting for transfers between devices, from_behind(): return lax.ppermute(value, axis, pairs)  2.49 us
  transfers between devices with their start and end apart: 2, of which 2 were waited for; matrix products, arithmetic and copies ran while one was open for 0% of the time, Pallas kernels for 0%

commit v1 on v0

v1 whole, which is shorter than its diff:
```python
import functools

import jax
import jax.numpy as jnp
from jax import lax
from jax.experimental import pallas as pl
from jax.experimental.pallas import tpu as pltpu
from jax.sharding import PartitionSpec as P

ROWS = 128
SUB = 8


def exchange_pairs(count, k):
    if count & (count - 1) == 0:
        return [(i, i ^ k) for i in range(count)]
    return [(i, (i + k) % count) for i in range(count)]


def reversed_pairs(pairs):
    return [(target, source) for source, target in pairs]


def looked_up(pairs, index):
    table = [0] * len(pairs)
    for source, target in pairs:
        table[source] = target
    return jnp.array(table, jnp.int32)[index]


def from_behind(value, axis):
    count = lax.axis_size(axis)
    return lax.ppermute(value, axis, [(i, i + 1) for i in range(count - 1)])


def column_masks(d_ref, col, tile_count, col_count):
    codes = d_ref[pl.ds(col, tile_count, col_count), :]
    codes = jnp.concatenate([codes] * (SUB // tile_count), axis=0)
    lane = lax.broadcasted_iota(jnp.int32, codes.shape, 1)
    north = (codes == 1) & (lane > 0)
    south = (codes == 2) & (lane < ROWS - 1)
    return north, south


def advance(summed, north, south):
    zero = jnp.zeros_like(summed)
    up = pltpu.roll(jnp.where(north, summed, zero), ROWS - 1, 1)
    down = pltpu.roll(jnp.where(south, summed, zero), 1, 1)
    return jnp.where(north | south, zero, summed) + (up + down)


def sweep_rows(x_ref, d_ref, carried, o_ref, tile_count, col_count):
    groups = len(carried)
    for col in range(col_count):
        masks = column_masks(d_ref, col, tile_count, col_count)
        for g in range(groups):
            rows = pl.ds(g * SUB * col_count + col, SUB, col_count)
            summed = x_ref[rows, :]
            if carried[g] is not None:
                summed = summed + carried[g]
            if o_ref is not None:
                o_ref[rows, :] = summed
            if o_ref is None or col < col_count - 1:
                carried[g] = advance(summed, *masks)
    return carried


def pack(x, block, tile_count):
    members, _, col_count, _ = x.shape
    parts = 4 if members % 4 == 0 else 1
    step = members // parts

    def body(block_ref, x_ref, o_ref, sems):
        tiles = pl.ds(block_ref[0] * tile_count, tile_count)
        copies = [
            pltpu.make_async_copy(
                x_ref.at[pl.ds(i * step, step), tiles], o_ref.at[pl.ds(i * step, step)], sems.at[i]
            )
            for i in range(parts)
        ]
        for copy in copies:
            copy.start()
        for copy in copies:
            copy.wait()

    out = pl.pallas_call(
        body,
        out_shape=jax.ShapeDtypeStruct((members, tile_count, col_count, ROWS), x.dtype),
        grid_spec=pltpu.PrefetchScalarGridSpec(
            num_scalar_prefetch=1,
            grid=(1,),
            in_specs=[pl.BlockSpec(memory_space=pl.ANY)],
            out_specs=pl.BlockSpec(memory_space=pl.ANY),
            scratch_shapes=[pltpu.SemaphoreType.DMA((parts,))],
        ),
        name="pack",
    )(block, x)
    return out.reshape(members * tile_count * col_count, ROWS)


def pack_with_inflow(x, block, inflow, tile_count):
    members, _, col_count, _ = x.shape
    count = members * tile_count

    def body(block_ref, x_ref, in_ref, o_ref):
        o_ref[...] = x_ref[...].reshape(o_ref.shape)
        rows = pl.ds(0, count, col_count)
        o_ref[rows, :] = o_ref[rows, :] + in_ref[...]

    return pl.pallas_call(
        body,
        out_shape=jax.ShapeDtypeStruct((count * col_count, ROWS), x.dtype),
        grid_spec=pltpu.PrefetchScalarGridSpec(
            num_scalar_prefetch=1,
            grid=(1,),
            in_specs=[
                pl.BlockSpec((members, tile_count, col_count, ROWS), lambda i, b: (0, b[0], 0, 0)),
                pl.BlockSpec((count, ROWS), lambda i, b: (0, 0)),
            ],
            out_specs=pl.BlockSpec((count * col_count, ROWS), lambda i, b: (0, 0)),
        ),
        name="pack_with_inflow",
    )(block, x, inflow)


def source_panels(x, blocks, dirs, inflow, tile_count):
    members, _, col_count, _ = x.shape
    count = members * tile_count
    listed = blocks.shape[0]

    def body(blocks_ref, x_ref, d_ref, in_ref, o_ref):
        flat = x_ref.reshape(count * col_count, ROWS)
        codes = d_ref.reshape(tile_count * col_count, ROWS)
        carried = [in_ref[0, pl.ds(g * SUB, SUB), :] for g in range(count // SUB)]
        carried = sweep_rows(flat, codes, carried, None, tile_count, col_count)
        for g in range(count // SUB):
            o_ref[0, pl.ds(g * SUB, SUB), :] = carried[g]

    return pl.pallas_call(
        body,
        out_shape=jax.ShapeDtypeStruct((listed, count, ROWS), x.dtype),
        grid_spec=pltpu.PrefetchScalarGridSpec(
            num_scalar_prefetch=1,
            grid=(listed,),
            in_specs=[
                pl.BlockSpec((members, tile_count, col_count, ROWS), lambda i, b: (0, b[i], 0, 0)),
                pl.BlockSpec((1, tile_count, col_count, ROWS), lambda i, b: (i, 0, 0, 0)),
                pl.BlockSpec((1, count, ROWS), lambda i, b: (i, 0, 0)),
            ],
            out_specs=pl.BlockSpec((1, count, ROWS), lambda i, b: (i, 0, 0)),
        ),
        name="source_panels",
    )(blocks, x, dirs, inflow)


def chunk_panel(chunk, codes, inflow, tile_count):
    count = inflow.shape[0]
    col_count = chunk.shape[0] // count

    def body(x_ref, d_ref, in_ref, o_ref):
        carried = [in_ref[pl.ds(g * SUB, SUB), :] for g in range(count // SUB)]
        carried = sweep_rows(x_ref, d_ref, carried, None, tile_count, col_count)
        for g in range(count // SUB):
            o_ref[pl.ds(g * SUB, SUB), :] = carried[g]

    return pl.pallas_call(
        body, out_shape=jax.ShapeDtypeStruct(inflow.shape, chunk.dtype), name="chunk_panel"
    )(chunk, codes, inflow)


def chunk_result(chunk, codes, inflow, result, block, tile_count, shape):
    col_count = codes.shape[0] // tile_count
    rows = chunk.shape[0]
    groups = rows // (col_count * SUB)
    aliases = {}
    operands = [block, chunk, codes]
    specs = [
        pl.BlockSpec((rows, ROWS), lambda i, b: (0, 0)),
        pl.BlockSpec(codes.shape, lambda i, b: (0, 0)),
    ]
    if inflow is not None:
        operands.append(inflow)
        specs.append(pl.BlockSpec(inflow.shape, lambda i, b: (0, 0)))
    if result is not None:
        aliases = {len(operands): 0}
        operands.append(result)
        specs.append(pl.BlockSpec(memory_space=pl.ANY))

    def body(block_ref, x_ref, d_ref, *rest):
        o_ref = rest[-1]
        carried = [None] * groups
        if inflow is not None:
            carried = [rest[0][pl.ds(g * SUB, SUB), :] for g in range(groups)]
        sweep_rows(x_ref, d_ref, carried, o_ref, tile_count, col_count)

    return pl.pallas_call(
        body,
        out_shape=jax.ShapeDtypeStruct(shape, chunk.dtype),
        grid_spec=pltpu.PrefetchScalarGridSpec(
            num_scalar_prefetch=1,
            grid=(1,),
            in_specs=specs,
            out_specs=pl.BlockSpec((rows, ROWS), lambda i, b: (b[0], 0)),
        ),
        input_output_aliases=aliases,
        name="chunk_result",
    )(*operands)


def local(runoff, directions):
    basins, chain = lax.axis_size("basin"), lax.axis_size("chain")
    _, members, all_tiles, _, cell_count = runoff.shape
    tile_count = directions.shape[0]
    col_count = cell_count // ROWS
    count = members * tile_count
    x = runoff.reshape(members, all_tiles, col_count, ROWS)
    d = directions.reshape(tile_count, col_count, ROWS)
    codes = d.reshape(tile_count * col_count, ROWS)
    me = lax.axis_index("basin")

    first = basins // 2
    late = [k for k in range(basins - 1, 0, -1) if k != first]
    pairs = {k: exchange_pairs(basins, k) for k in range(basins)}
    target = {k: looked_up(pairs[k], me)[None] for k in pairs}
    origin = {k: looked_up(reversed_pairs(pairs[k]), me)[None] for k in pairs}

    listed = [0] + late
    dirs = jnp.stack([d] + [lax.ppermute(d, "basin", reversed_pairs(pairs[k])) for k in late])
    blocks = jnp.concatenate([target[k] for k in listed])

    arrived = {first: lax.ppermute(pack(x, target[first], tile_count), "basin", pairs[first])}

    inflows = jnp.zeros((len(listed), count, ROWS), jnp.float32)
    for _ in range(chain - 1):
        inflows = from_behind(source_panels(x, blocks, dirs, inflows, tile_count), "chain")
    for i, k in enumerate(listed):
        chunk = pack_with_inflow(x, target[k], inflows[i], tile_count)
        arrived[k] = lax.ppermute(chunk, "basin", pairs[k]) if k else chunk

    inflow = jnp.zeros((count, ROWS), jnp.float32)
    for _ in range(chain - 1):
        inflow = from_behind(chunk_panel(arrived[first], codes, inflow, tile_count), "chain")

    shape = (basins * count * col_count, ROWS)
    result = None
    for k in [0, first] + late:
        result = chunk_result(
            arrived[k], codes, inflow if k == first else None, result, origin[k], tile_count, shape
        )
    return result.reshape(basins * members, tile_count, 1, cell_count)


def solution(mesh):
    return jax.shard_map(
        local,
        mesh=mesh,
        in_specs=(P("mem", "basin", "grp", "chain", None), P(("grp", "basin"), "chain", None)),
        out_specs=P("mem", ("grp", "basin"), "chain", None),
        check_vma=False,
    )
```

time: 95.8 us -> 101 us (1.054)
  Pallas kernels: 0 us -> 47.3 us
  waiting for transfers between devices: 50.6 us -> 27.9 us
  matrix products: 10.9 us -> 0 us
  other arithmetic: 10.8 us -> 3.31 us
  starting transfers between devices: 9.85 us -> 14.4 us
  local copies, waits for them, and re-layouts: 12.1 us -> 7.58 us
  loops' own time: 1.22 us -> 0 us
    all_to_all x1 -> x0, waiting for transfers between devices: 48.1 us -> none  [local(): lax.all_to_all(runoff, 'basin', split_axis=2, concat_axis=1, tiled=True)]
    pallas_call x0 -> x10, Pallas kernels: none -> 47.3 us  [the longest x1 17.7 us: pack(): pl.pallas_call(body, out_shape=jax.ShapeDtypeStruct((members, tile_count,...]
    ppermute x1 -> x7, waiting for transfers between devices: 2.49 us -> 27.9 us  [the longest x1 27.9 us: local(): lax.ppermute(pack(x, target[first], tile_count), 'basin', pairs[first])]
    ppermute x1 -> x7, starting transfers between devices: 3.4 us -> 14.4 us  [the longest x2 5.05 us: local(): lax.ppermute(d, 'basin', reversed_pairs(pairs[k]))]
    dot_general x32 -> x0, matrix products: 10.9 us -> none  [advance(): jnp.einsum('mtj,tji->mti', summed, column_onehot(target_col, jnp.float32)...]
    dynamic_update_slice x16 -> x0, other arithmetic: 10.7 us -> none  [sweep_tile(): lax.scan(advance, inflow, (jnp.moveaxis(water_cols, 2, 0), jnp.moveaxis(t...]
    all_to_all x1 -> x0, starting transfers between devices: 6.45 us -> none  [local(): lax.all_to_all(runoff, 'basin', split_axis=2, concat_axis=1, tiled=True)]
    transpose x1 -> x0, local copies, waits for them, and re-layouts: 4.13 us -> none  [local(): jnp.transpose(columns_out, (1, 2, 0, 3))]
  transfers between devices with their start and end apart: 2 -> 7, of which waited for: 2 -> 1; matrix products, arithmetic and copies ran while one was open for 0% -> 6% of each run, Pallas kernels for 0% -> 38%
where the time goes in v1:
time: 101 us
  Pallas kernels  47.3 us (47%)
  waiting for transfers between devices  27.9 us (28%)
  starting transfers between devices  14.4 us (14%)
  local copies, waits for them, and re-layouts  7.58 us (8%)
  other arithmetic  3.31 us (3%)
    ppermute x1, waiting for transfers between devices, local(): lax.ppermute(pack(x, target[first], tile_count), 'basin', pairs[first])  27.9 us
    pallas_call x1, Pallas kernels, pack(): pl.pallas_call(body, out_shape=jax.ShapeDtypeStruct((members, tile_count,...  17.7 us
    pallas_call x4, Pallas kernels, chunk_result(): pl.pallas_call(body, out_shape=jax.ShapeDtypeStruct(shape, chunk.dtype),...  13.8 us
    pallas_call x3, Pallas kernels, pack_with_inflow(): pl.pallas_call(body, out_shape=jax.ShapeDtypeStruct((count * col_count, R...  7.05 us
    pallas_call x1, Pallas kernels, source_panels(): pl.pallas_call(body, out_shape=jax.ShapeDtypeStruct((listed, count, ROWS)...  5.88 us
    ppermute x2, starting transfers between devices, local(): lax.ppermute(d, 'basin', reversed_pairs(pairs[k]))  5.05 us
    ppermute x2, starting transfers between devices, from_behind(): return lax.ppermute(value, axis, [(i, i + 1) for i in range(count - 1)])  4.93 us
    ppermute x2, starting transfers between devices, local(): arrived[k] = lax.ppermute(chunk, 'basin', pairs[k]) if k else chunk  3.6 us
  transfers between devices with their start and end apart: 7, of which 1 were waited for; matrix products, arithmetic and copies ran while one was open for 6% of the time, Pallas kernels for 38%

profile of v1, /device:TPU:0, one launch (start us, length us, event | category | flops | bytes accessed | tf_op | source)
XLA Modules:
  0.0 100.6 jit_solution(16176081089624784550)
XLA Ops:
  0.0 0.0 copy-start.4
  0.0 5.0 %collective-permute-start = (s32[4,16,128]{2,1,0:T(8,128)}, s32[4,16,128]{2,1,0:T(8,128)S(1)}, u32[]{:S(2)}, u32[]{:S(2)}) collective-permute-start(s32[4,16,128]{2,1,0:T(8,128)} %bitcast.20), channel_id=1, source_target_pairs={{12,0},{8,4},{4,8},{0,12},{13,1},{9,5},{5,9},{1,13},{14,2},{10,6},... | collective-permute-start | bytes 98312 | tf_op jit(solution)/shard_map/ppermute | solution.py:228
  5.1 0.0 collective-permute-start.1
  5.1 1.2 %dynamic_slice.24.block_ref = s32[1]{0:T(128)} dynamic-slice(s32[4]{0:T(128)} %constant.20.clone, s32[]{:T(128)S(6)} %select_n.2), dynamic_slice_sizes={1} | dynamic-slice | bytes 12 | tf_op jit(solution)/shard_map/dynamic_slice | solution.py:28
  6.3 1.3 %dynamic_slice.27.block_ref = s32[1]{0:T(128)} dynamic-slice(s32[4]{0:T(128)} %constant.22.clone, s32[]{:T(128)S(6)} %select_n.2), dynamic_slice_sizes={1} | dynamic-slice | bytes 12 | tf_op jit(solution)/shard_map/dynamic_slice | solution.py:28
  7.6 1.9 %pad_add_fusion.1.blocks_ref = s32[3]{0:T(128)} fusion(s32[1]{0:T(128)} %dynamic_slice.24.block_ref, s32[1]{0:T(128)} %dynamic_slice.27.block_ref, s32[1]{0:T(128)} %bitcast.1.block_ref), kind=kLoop, calls=%fused_computation.4 | loop fusion | flops 6 | bytes 24 | tf_op jit(solution)/shard_map/concatenate | solution.py:229
  9.5 0.0 collective-permute-done
  9.5 0.0 collective-permute-done.1
  9.5 1.4 %pad_add_fusion.d_ref = s32[3,4,16,128]{3,2,1,0:T(8,128)} fusion(s32[1,4,16,128]{3,2,1,0:T(8,128)S(1)} %bitcast.30, s32[1,4,16,128]{3,2,1,0:T(8,128)S(1)} %bitcast.29, s32[1,4,16,128]{3,2,1,0:T(8,128)} %bitcast.22), kind=kLoop, calls=%fused_computation | loop fusion | flops 49152 | bytes 196608 | tf_op jit(solution)/shard_map/stack | solution.py:228
  10.9 0.7 broadcast_in_dim.6.in_ref
  11.6 5.9 %source_panels.1 = f32[3,64,128]{2,1,0:T(8,128)} custom-call(s32[3]{0:T(128)} %pad_add_fusion.1.blocks_ref, f32[16,16,16,128]{3,2,1,0:T(8,128)} %bitcast.15, s32[3,4,16,128]{3,2,1,0:T(8,128)} %pad_add_fusion.d_ref, f32[3,64,128]{2,1,0:T(8,128)} %broadcast_in_dim.6.in_ref), custom_call_target="tpu_custom_call" | custom-call | tf_op jit(solution)/shard_map/source_panels/pallas_call | solution.py:139
  17.5 3.4 %collective-permute-start.2 = (f32[3,64,128]{2,1,0:T(8,128)}, f32[3,64,128]{2,1,0:T(8,128)S(1)}, u32[]{:S(2)}, u32[]{:S(2)}) collective-permute-start(f32[3,64,128]{2,1,0:T(8,128)} %source_panels.1), channel_id=1, source_target_pairs={{0,2},{1,3},{4,6},{5,7},{8,10},{9,11},{12,14},{13,15},{16,18},{17,... | collective-permute-start | bytes 294920 | tf_op jit(solution)/shard_map/ppermute | solution.py:33
  20.9 0.0 copy-done.4
  20.9 0.7 dynamic_slice.29.block_ref
  21.5 17.7 %pack.1 = f32[16,4,16,128]{3,2,1,0:T(8,128)} custom-call(s32[1]{0:T(128)} %dynamic_slice.29.block_ref, f32[16,16,16,128]{3,2,1,0:T(8,128)} %bitcast.16), custom_call_target="tpu_custom_call" | custom-call | tf_op jit(solution)/shard_map/pack/pallas_call | solution.py:86
  39.2 0.8 collective-permute-start.5
  40.1 0.0 collective-permute-done.2
  40.1 0.7 slice_bitcast_fusion
  40.7 2.6 %pack_with_inflow.4 = f32[1024,128]{1,0:T(8,128)} custom-call(s32[1]{0:T(128)} %dynamic_slice.27.block_ref, f32[16,16,16,128]{3,2,1,0:T(8,128)} %bitcast.17, f32[64,128]{1,0:T(8,128)} %get-tuple-element.6.in_ref), custom_call_target="tpu_custom_call" | custom-call | tf_op jit(solution)/shard_map/pack_with_inflow/pallas_call | solution.py:110
  43.3 3.6 %collective-permute-start.4 = (f32[1024,128]{1,0:T(8,128)}, f32[1024,128]{1,0:T(8,128)S(1)}, u32[]{:S(2)}, u32[]{:S(2)}) collective-permute-start(f32[1024,128]{1,0:T(8,128)} %pack_with_inflow.4), channel_id=1, source_target_pairs={{0,12},{4,8},{8,4},{12,0},{1,13},{5,9},{9,5},{13,1},{2,14},{6,10},... | collective-permute-start | bytes 1572872 | tf_op jit(solution)/shard_map/ppermute | solution.py:238
  46.9 2.5 %pack_with_inflow.3 = f32[1024,128]{1,0:T(8,128)} custom-call(s32[1]{0:T(128)} %dynamic_slice.24.block_ref, f32[16,16,16,128]{3,2,1,0:T(8,128)} %bitcast.18, f32[64,128]{1,0:T(8,128)} %get-tuple-element.7.in_ref), custom_call_target="tpu_custom_call" | custom-call | tf_op jit(solution)/shard_map/pack_with_inflow/pallas_call | solution.py:110
  49.5 0.0 collective-permute-start.3
  49.5 27.9 %collective-permute-done.5.x_ref = f32[1024,128]{1,0:T(8,128)S(1)} collective-permute-done((f32[1024,128]{1,0:T(8,128)}, f32[1024,128]{1,0:T(8,128)S(1)}, u32[]{:S(2)}, u32[]{:S(2)}) %collective-permute-start.5) | collective-permute-done | bytes 524320 | tf_op jit(solution)/shard_map/ppermute | solution.py:231
  77.4 0.0 copy-start
  77.4 0.7 broadcast_in_dim.7.in_ref
  78.0 0.2 copy-done
  78.2 2.8 %chunk_panel.1 = f32[64,128]{1,0:T(8,128)} custom-call(f32[1024,128]{1,0:T(8,128)} %copy-done, s32[64,128]{1,0:T(8,128)} %bitcast.23, f32[64,128]{1,0:T(8,128)} %broadcast_in_dim.7.in_ref), custom_call_target="tpu_custom_call" | custom-call | tf_op jit(solution)/shard_map/chunk_panel/pallas_call | solution.py:166
  81.0 1.5 %collective-permute-start.6 = (f32[64,128]{1,0:T(8,128)}, f32[64,128]{1,0:T(8,128)S(1)}, u32[]{:S(2)}, u32[]{:S(2)}) collective-permute-start(f32[64,128]{1,0:T(8,128)} %chunk_panel.1), channel_id=1, source_target_pairs={{0,2},{1,3},{4,6},{5,7},{8,10},{9,11},{12,14},{13,15},{16,18},{17,... | collective-permute-start | bytes 98312 | tf_op jit(solution)/shard_map/ppermute | solution.py:33
  82.6 1.9 %pack_with_inflow.5.x_ref = f32[1024,128]{1,0:T(8,128)} custom-call(s32[1]{0:T(128)} %bitcast.1.block_ref, f32[16,16,16,128]{3,2,1,0:T(8,128)} %bitcast.19, f32[64,128]{1,0:T(8,128)} %get-tuple-element.5.in_ref), custom_call_target="tpu_custom_call" | custom-call | tf_op jit(solution)/shard_map/pack_with_inflow/pallas_call | solution.py:110
  84.5 3.0 %chunk_result.4.rest_1_ = f32[4096,128]{1,0:T(8,128)} custom-call(s32[1]{0:T(128)} %bitcast.1.block_ref, f32[1024,128]{1,0:T(8,128)} %pack_with_inflow.5.x_ref, s32[64,128]{1,0:T(8,128)} %bitcast.24), custom_call_target="tpu_custom_call" | custom-call | tf_op jit(solution)/shard_map/chunk_result/pallas_call | solution.py:196
  87.5 0.0 collective-permute-done.6.rest_0_
  87.5 0.0 copy-start.3
  87.5 0.6 copy-done.3
  88.1 3.6 %chunk_result.5.rest_0_ = f32[4096,128]{1,0:T(8,128)} custom-call(s32[1]{0:T(128)} %dynamic_slice.29.block_ref, f32[1024,128]{1,0:T(8,128)} %copy-done, s32[64,128]{1,0:T(8,128)} %bitcast.25, f32[64,128]{1,0:T(8,128)} %copy-done.3, f32[4096,128]{1,0:T(8,128)} %chunk_result.4.rest_1_), custom_call_target="tpu_custom_call", output_to_operand_aliasing={{}: (4, {})} | custom-call | tf_op jit(solution)/shard_map/chunk_result/pallas_call | solution.py:196
  91.7 0.0 collective-permute-done.4.x_ref
  91.7 0.0 copy-start.2
  91.7 0.8 copy-done.2
  92.5 3.6 %chunk_result.6.rest_0_ = f32[4096,128]{1,0:T(8,128)} custom-call(s32[1]{0:T(128)} %dynamic_slice.27.block_ref, f32[1024,128]{1,0:T(8,128)} %copy-done.2, s32[64,128]{1,0:T(8,128)} %bitcast.26, f32[4096,128]{1,0:T(8,128)} %chunk_result.5.rest_0_), custom_call_target="tpu_custom_call", output_to_operand_aliasing={{}: (3, {})} | custom-call | tf_op jit(solution)/shard_map/chunk_result/pallas_call | solution.py:196
  96.2 0.0 collective-permute-done.3.x_ref
  96.2 0.0 copy-start.1
  96.2 0.8 copy-done.1
  97.0 3.6 %chunk_result.7 = f32[4096,128]{1,0:T(8,128)} custom-call(s32[1]{0:T(128)} %dynamic_slice.24.block_ref, f32[1024,128]{1,0:T(8,128)} %copy-done.1, s32[64,128]{1,0:T(8,128)} %bitcast.27, f32[4096,128]{1,0:T(8,128)} %chunk_result.6.rest_0_), custom_call_target="tpu_custom_call", output_to_operand_aliasing={{}: (3, {})} | custom-call | tf_op jit(solution)/shard_map/chunk_result/pallas_call | solution.py:196
Async XLA Ops:
  0.0 20.9 %copy-start.4 = (s32[4]{0:T(128)S(1)}, s32[4]{0:T(128)}, u32[]{:S(2)}) copy-start(s32[4]{0:T(128)} %constant.21.clone) | copy-start | bytes 52
  0.0 9.5 %collective-permute-start = (s32[4,16,128]{2,1,0:T(8,128)}, s32[4,16,128]{2,1,0:T(8,128)S(1)}, u32[]{:S(2)}, u32[]{:S(2)}) collective-permute-start(s32[4,16,128]{2,1,0:T(8,128)} %bitcast.20), channel_id=1, source_target_pairs={{12,0},{8,4},{4,8},{0,12},{13,1},{9,5},{5,9},{1,13},{14,2},{10,6},... | collective-permute-start | bytes 98312 | tf_op jit(solution)/shard_map/ppermute | solution.py:228
  5.1 4.5 %collective-permute-start.1 = (s32[4,16,128]{2,1,0:T(8,128)}, s32[4,16,128]{2,1,0:T(8,128)S(1)}, u32[]{:S(2)}, u32[]{:S(2)}) collective-permute-start(s32[4,16,128]{2,1,0:T(8,128)} %bitcast.21), channel_id=1, source_target_pairs={{4,0},{0,4},{12,8},{8,12},{5,1},{1,5},{13,9},{9,13},{6,2},{2,6},{1... | collective-permute-start | bytes 98312 | tf_op jit(solution)/shard_map/ppermute | solution.py:228
  17.5 22.6 %collective-permute-start.2 = (f32[3,64,128]{2,1,0:T(8,128)}, f32[3,64,128]{2,1,0:T(8,128)S(1)}, u32[]{:S(2)}, u32[]{:S(2)}) collective-permute-start(f32[3,64,128]{2,1,0:T(8,128)} %source_panels.1), channel_id=1, source_target_pairs={{0,2},{1,3},{4,6},{5,7},{8,10},{9,11},{12,14},{13,15},{16,18},{17,... | collective-permute-start | bytes 294920 | tf_op jit(solution)/shard_map/ppermute | solution.py:33
  39.2 38.1 %collective-permute-start.5 = (f32[1024,128]{1,0:T(8,128)}, f32[1024,128]{1,0:T(8,128)S(1)}, u32[]{:S(2)}, u32[]{:S(2)}) collective-permute-start(f32[1024,128]{1,0:T(8,128)} %bitcast.28), channel_id=1, source_target_pairs={{0,8},{4,12},{8,0},{12,4},{1,9},{5,13},{9,1},{13,5},{2,10},{6,14},... | collective-permute-start | bytes 1572872 | tf_op jit(solution)/shard_map/ppermute | solution.py:231
  43.3 48.4 %collective-permute-start.4 = (f32[1024,128]{1,0:T(8,128)}, f32[1024,128]{1,0:T(8,128)S(1)}, u32[]{:S(2)}, u32[]{:S(2)}) collective-permute-start(f32[1024,128]{1,0:T(8,128)} %pack_with_inflow.4), channel_id=1, source_target_pairs={{0,12},{4,8},{8,4},{12,0},{1,13},{5,9},{9,5},{13,1},{2,14},{6,10},... | collective-permute-start | bytes 1572872 | tf_op jit(solution)/shard_map/ppermute | solution.py:238
  49.5 46.7 %collective-permute-start.3 = (f32[1024,128]{1,0:T(8,128)}, f32[1024,128]{1,0:T(8,128)S(1)}, u32[]{:S(2)}, u32[]{:S(2)}) collective-permute-start(f32[1024,128]{1,0:T(8,128)} %pack_with_inflow.3), channel_id=1, source_target_pairs={{0,4},{4,0},{8,12},{12,8},{1,5},{5,1},{9,13},{13,9},{2,6},{6,2},{1... | collective-permute-start | bytes 1572872 | tf_op jit(solution)/shard_map/ppermute | solution.py:238
  77.4 0.8 copy-start
  81.0 6.4 %collective-permute-start.6 = (f32[64,128]{1,0:T(8,128)}, f32[64,128]{1,0:T(8,128)S(1)}, u32[]{:S(2)}, u32[]{:S(2)}) collective-permute-start(f32[64,128]{1,0:T(8,128)} %chunk_panel.1), channel_id=1, source_target_pairs={{0,2},{1,3},{4,6},{5,7},{8,10},{9,11},{12,14},{13,15},{16,18},{17,... | collective-permute-start | bytes 98312 | tf_op jit(solution)/shard_map/ppermute | solution.py:33
  87.5 0.6 copy-start.3
  91.7 0.8 copy-start.2
  96.2 0.8 copy-start.1

commit v2 on v0

v2 whole, which is shorter than its diff:
```python
import jax
import jax.numpy as jnp
from jax import lax
from jax.experimental import pallas as pl
from jax.experimental.pallas import tpu as pltpu
from jax.sharding import PartitionSpec as P

ROWS = 128
SUB = 8
HBM = pl.BlockSpec(memory_space=pl.ANY)
VMEM = pl.BlockSpec(memory_space=pltpu.VMEM)


def exchange_pairs(count, k):
    if count & (count - 1) == 0:
        return [(i, i ^ k) for i in range(count)]
    return [(i, (i + k) % count) for i in range(count)]


def reversed_pairs(pairs):
    return [(target, source) for source, target in pairs]


def target_of(k, count):
    me = lax.axis_index("basin")
    return me ^ k if count & (count - 1) == 0 else lax.rem(me + k, count)


def origin_of(k, count):
    me = lax.axis_index("basin")
    return me ^ k if count & (count - 1) == 0 else lax.rem(me + count - k, count)


def from_behind(value, axis):
    count = lax.axis_size(axis)
    return lax.ppermute(value, axis, [(i, i + 1) for i in range(count - 1)])


class Sizes:
    def __init__(self, members, tiles, columns, basins):
        self.members, self.tiles, self.columns, self.basins = members, tiles, columns, basins
        self.per_member = tiles * columns
        self.count = members * tiles
        self.rows = members * tiles * columns
        self.groups = self.count // SUB


def column_masks(d_ref, col, sizes):
    codes = d_ref[pl.ds(col, sizes.tiles, sizes.columns), :]
    codes = jnp.concatenate([codes] * (SUB // sizes.tiles), axis=0)
    lane = lax.broadcasted_iota(jnp.int32, codes.shape, 1)
    north = (codes == 1) & (lane > 0)
    south = (codes == 2) & (lane < ROWS - 1)
    return north, south


def advance(summed, north, south):
    zero = jnp.zeros_like(summed)
    up = pltpu.roll(jnp.where(north, summed, zero), ROWS - 1, 1)
    down = pltpu.roll(jnp.where(south, summed, zero), 1, 1)
    return jnp.where(north | south, zero, summed) + (up + down)


def sweep(x_ref, d_ref, carried, o_ref, sizes):
    for col in range(sizes.columns):
        north, south = column_masks(d_ref, col, sizes)
        for g in range(sizes.groups):
            rows = pl.ds(g * SUB * sizes.columns + col, SUB, sizes.columns)
            summed = x_ref[rows, :]
            if carried[g] is not None:
                summed = summed + carried[g]
            if o_ref is not None:
                o_ref[rows, :] = summed
            if o_ref is None or col < sizes.columns - 1:
                carried[g] = advance(summed, north, south)
    return carried


def registers(in_ref, i, sizes):
    if in_ref is None:
        return [None] * sizes.groups
    return [in_ref[i, pl.ds(g * SUB, SUB), :] for g in range(sizes.groups)]


def store_registers(o_ref, i, carried):
    for g, value in enumerate(carried):
        o_ref[i, pl.ds(g * SUB, SUB), :] = value


def gather_copies(x_ref, buf_ref, sem, block, sizes):
    size = sizes.per_member
    return [
        pltpu.make_async_copy(
            x_ref.at[m, pl.ds(block * size, size)], buf_ref.at[pl.ds(m * size, size)], sem.at[m]
        )
        for m in range(sizes.members)
    ]


def start_all(copies):
    for copy in copies:
        copy.start()


def wait_all(copies):
    for copy in copies:
        copy.wait()


def chunk_shape(sizes):
    return jax.ShapeDtypeStruct((sizes.rows, ROWS), jnp.float32)


def panel_shape(listed, sizes):
    return jax.ShapeDtypeStruct((listed, sizes.count, ROWS), jnp.float32)


def result_shape(sizes):
    return jax.ShapeDtypeStruct((sizes.basins * sizes.rows, ROWS), jnp.float32)


def params(sizes, chunks):
    return pltpu.CompilerParams(vmem_limit_bytes=(chunks * sizes.rows + 4096) * ROWS * 4)


def cost(chunks):
    return pl.CostEstimate(flops=chunks * (1 << 20), bytes_accessed=chunks * (1 << 20), transcendentals=0)


def pack(x, k, sizes):
    def body(x_ref, o_ref, sem):
        copies = gather_copies(x_ref, o_ref, sem, target_of(k, sizes.basins), sizes)
        start_all(copies)
        wait_all(copies)

    return pl.pallas_call(
        body,
        out_shape=chunk_shape(sizes),
        in_specs=[HBM],
        out_specs=VMEM,
        scratch_shapes=[pltpu.SemaphoreType.DMA((sizes.members,))],
        cost_estimate=cost(1),
        compiler_params=params(sizes, 2),
        name="pack",
    )(x)


def source_panels(x, ks, codes, inflow, sizes):
    listed = len(ks)

    def body(x_ref, *rest):
        d_refs, rest = rest[:listed], rest[listed:]
        in_ref = rest[0] if inflow is not None else None
        o_ref, buf, sem = rest[-3:]
        copies = [
            gather_copies(x_ref, buf.at[i], sem.at[i], target_of(k, sizes.basins), sizes)
            for i, k in enumerate(ks)
        ]
        for c in copies:
            start_all(c)
        for i in range(listed):
            wait_all(copies[i])
            store_registers(
                o_ref, i, sweep(buf.at[i], d_refs[i], registers(in_ref, i, sizes), None, sizes)
            )

    return pl.pallas_call(
        body,
        out_shape=panel_shape(listed, sizes),
        in_specs=[HBM] + [VMEM] * (listed + (inflow is not None)),
        out_specs=VMEM,
        scratch_shapes=[
            pltpu.VMEM((listed, sizes.rows, ROWS), jnp.float32),
            pltpu.SemaphoreType.DMA((listed, sizes.members)),
        ],
        cost_estimate=cost(listed),
        compiler_params=params(sizes, 2 * listed),
        name="source_panels",
    )(x, *codes, *([inflow] if inflow is not None else []))


def source_chunk(x, k, codes, inflow, i, sizes):
    def body(x_ref, d_ref, in_ref, o_ref, buf, sem):
        copies = gather_copies(x_ref, buf, sem, target_of(k, sizes.basins), sizes)
        start_all(copies)
        wait_all(copies)
        sweep(buf, d_ref, registers(in_ref, i, sizes), o_ref, sizes)

    return pl.pallas_call(
        body,
        out_shape=chunk_shape(sizes),
        in_specs=[HBM, VMEM, VMEM],
        out_specs=VMEM,
        scratch_shapes=[
            pltpu.VMEM((sizes.rows, ROWS), jnp.float32),
            pltpu.SemaphoreType.DMA((sizes.members,)),
        ],
        cost_estimate=cost(1),
        compiler_params=params(sizes, 3),
        name="source_chunk",
    )(x, codes, inflow)


def own_result(x, codes, inflow, sizes):
    def body(x_ref, d_ref, in_ref, o_ref, buf, out, sem, out_sem):
        copies = gather_copies(x_ref, buf, sem, lax.axis_index("basin"), sizes)
        start_all(copies)
        wait_all(copies)
        sweep(buf, d_ref, registers(in_ref, 0, sizes), out, sizes)
        place = o_ref.at[pl.ds(lax.axis_index("basin") * sizes.rows, sizes.rows)]
        copy = pltpu.make_async_copy(out, place, out_sem)
        copy.start()
        copy.wait()

    return pl.pallas_call(
        body,
        out_shape=result_shape(sizes),
        in_specs=[HBM, VMEM, VMEM],
        out_specs=HBM,
        scratch_shapes=[
            pltpu.VMEM((sizes.rows, ROWS), jnp.float32),
            pltpu.VMEM((sizes.rows, ROWS), jnp.float32),
            pltpu.SemaphoreType.DMA((sizes.members,)),
            pltpu.SemaphoreType.DMA,
        ],
        cost_estimate=cost(1),
        compiler_params=params(sizes, 3),
        name="own_result",
    )(x, codes, inflow)


def arrived_panels(chunks, codes, inflow, sizes):
    listed = len(chunks)

    def body(*refs):
        x_refs, d_ref, o_ref = refs[:listed], refs[listed], refs[-1]
        in_ref = refs[listed + 1] if inflow is not None else None
        for i in range(listed):
            store_registers(
                o_ref, i, sweep(x_refs[i], d_ref, registers(in_ref, i, sizes), None, sizes)
            )

    return pl.pallas_call(
        body,
        out_shape=panel_shape(listed, sizes),
        in_specs=[VMEM] * (listed + 1 + (inflow is not None)),
        out_specs=VMEM,
        cost_estimate=cost(listed),
        compiler_params=params(sizes, 2 * listed),
        name="arrived_panels",
    )(*chunks, codes, *([inflow] if inflow is not None else []))


def arrived_result(chunks, ks, codes, inflow, result, sizes):
    listed = len(chunks)

    def body(*refs):
        x_refs, d_ref, in_ref = refs[:listed], refs[listed], refs[listed + 1]
        o_ref, out, sem = refs[-3:]
        copies = []
        for i, k in enumerate(ks):
            sweep(x_refs[i], d_ref, registers(in_ref, i, sizes), out.at[i], sizes)
            place = o_ref.at[pl.ds(origin_of(k, sizes.basins) * sizes.rows, sizes.rows)]
            copies.append(pltpu.make_async_copy(out.at[i], place, sem.at[i]))
            copies[i].start()
        wait_all(copies)

    return pl.pallas_call(
        body,
        out_shape=result_shape(sizes),
        in_specs=[VMEM] * (listed + 2) + [HBM],
        out_specs=HBM,
        scratch_shapes=[
            pltpu.VMEM((listed, sizes.rows, ROWS), jnp.float32),
            pltpu.SemaphoreType.DMA((listed,)),
        ],
        input_output_aliases={listed + 2: 0},
        cost_estimate=cost(listed),
        compiler_params=params(sizes, 3 * listed),
        name="arrived_result",
    )(*chunks, codes, inflow, result)


def place_chunk(chunk, k, result, sizes):
    def body(x_ref, _, o_ref, sem):
        place = o_ref.at[pl.ds(origin_of(k, sizes.basins) * sizes.rows, sizes.rows)]
        copy = pltpu.make_async_copy(x_ref, place, sem)
        copy.start()
        copy.wait()

    return pl.pallas_call(
        body,
        out_shape=result_shape(sizes),
        in_specs=[VMEM, HBM],
        out_specs=HBM,
        scratch_shapes=[pltpu.SemaphoreType.DMA],
        input_output_aliases={1: 0},
        cost_estimate=cost(1),
        compiler_params=params(sizes, 2),
        name="place_chunk",
    )(chunk, result)


def local(runoff, directions):
    basins, chain = lax.axis_size("basin"), lax.axis_size("chain")
    _, members, all_tiles, _, cell_count = runoff.shape
    sizes = Sizes(members, directions.shape[0], cell_count // ROWS, basins)
    x = runoff.reshape(members, all_tiles * sizes.columns, ROWS)
    codes = directions.reshape(sizes.per_member, ROWS)

    early = sorted({basins // 2, 1}, reverse=True)
    late = [k for k in range(basins - 1, 0, -1) if k not in early]
    pairs = {k: exchange_pairs(basins, k) for k in range(basins)}
    listed = [0] + late

    arrived = {k: lax.ppermute(pack(x, k, sizes), "basin", pairs[k]) for k in early}
    dirs = [codes] + [lax.ppermute(codes, "basin", reversed_pairs(pairs[k])) for k in late]

    inflow = None
    for _ in range(chain - 1):
        inflow = from_behind(source_panels(x, listed, dirs, inflow, sizes), "chain")
    if inflow is None:
        inflow = jnp.zeros((len(listed), sizes.count, ROWS), jnp.float32)
    for i, k in enumerate(listed):
        if k:
            arrived[k] = lax.ppermute(source_chunk(x, k, dirs[i], inflow, i, sizes), "basin", pairs[k])
    result = own_result(x, codes, inflow, sizes)

    chunks = [arrived[k] for k in early]
    inflow = None
    for _ in range(chain - 1):
        inflow = from_behind(arrived_panels(chunks, codes, inflow, sizes), "chain")
    if inflow is None:
        inflow = jnp.zeros((len(early), sizes.count, ROWS), jnp.float32)
    result = arrived_result(chunks, early, codes, inflow, result, sizes)
    for k in late:
        result = place_chunk(arrived[k], k, result, sizes)
    return result.reshape(basins * members, sizes.tiles, 1, cell_count)


def solution(mesh):
    return jax.shard_map(
        local,
        mesh=mesh,
        in_specs=(P("mem", "basin", "grp", "chain", None), P(("grp", "basin"), "chain", None)),
        out_specs=P("mem", ("grp", "basin"), "chain", None),
        check_vma=False,
    )
```

time: 95.8 us -> 54.9 us (0.57)
  waiting for transfers between devices: 50.6 us -> 22.1 us
  Pallas kernels: 0 us -> 14.6 us
  matrix products: 10.9 us -> 0 us
  other arithmetic: 10.8 us -> 0 us
  local copies, waits for them, and re-layouts: 12.1 us -> 1.6 us
  starting transfers between devices: 9.85 us -> 16.4 us
  loops' own time: 1.22 us -> 0 us
    all_to_all x1 -> x0, waiting for transfers between devices: 48.1 us -> none  [local(): lax.all_to_all(runoff, 'basin', split_axis=2, concat_axis=1, tiled=True)]
    ppermute x1 -> x6, waiting for transfers between devices: 2.49 us -> 22.1 us  [the longest x2 20.2 us: local(): lax.ppermute(pack(x, k, sizes), 'basin', pairs[k])]
    pallas_call x0 -> x8, Pallas kernels: none -> 14.6 us  [the longest x1 4.03 us: source_panels(): pl.pallas_call(body, out_shape=panel_shape(listed, sizes), in_specs=[HBM]...]
    ppermute x1 -> x6, starting transfers between devices: 3.4 us -> 16.4 us  [the longest x2 7.02 us: from_behind(): return lax.ppermute(value, axis, [(i, i + 1) for i in range(count - 1)])]
    dot_general x32 -> x0, matrix products: 10.9 us -> none  [advance(): jnp.einsum('mtj,tji->mti', summed, column_onehot(target_col, jnp.float32)...]
    dynamic_update_slice x16 -> x0, other arithmetic: 10.7 us -> none  [sweep_tile(): lax.scan(advance, inflow, (jnp.moveaxis(water_cols, 2, 0), jnp.moveaxis(t...]
    all_to_all x1 -> x0, starting transfers between devices: 6.45 us -> none  [local(): lax.all_to_all(runoff, 'basin', split_axis=2, concat_axis=1, tiled=True)]
    unnamed x5 -> x6, local copies, waits for them, and re-layouts: 6.37 us -> 1.6 us
  transfers between devices with their start and end apart: 2 -> 6, of which waited for: 2 -> 3; matrix products, arithmetic and copies ran while one was open for 0% -> 0% of each run, Pallas kernels for 0% -> 25%
where the time goes in v2:
time: 54.9 us; the launch traced here: 54.8 us
  waiting for transfers between devices  22.1 us (40%)
  starting transfers between devices  16.4 us (30%)
  Pallas kernels  14.6 us (27%)
  local copies, waits for them, and re-layouts  1.6 us (3%)
    ppermute x2, waiting for transfers between devices, local(): lax.ppermute(pack(x, k, sizes), 'basin', pairs[k])  20.2 us
    ppermute x2, starting transfers between devices, from_behind(): return lax.ppermute(value, axis, [(i, i + 1) for i in range(count - 1)])  7.02 us
    ppermute x1, starting transfers between devices, local(): lax.ppermute(codes, 'basin', reversed_pairs(pairs[k]))  5.05 us
    pallas_call x1, Pallas kernels, source_panels(): pl.pallas_call(body, out_shape=panel_shape(listed, sizes), in_specs=[HBM]...  4.03 us
    ppermute x1, starting transfers between devices, local(): lax.ppermute(source_chunk(x, k, dirs[i], inflow, i, sizes), 'basin', pair...  3.67 us
    pallas_call x1, Pallas kernels, own_result(): pl.pallas_call(body, out_shape=result_shape(sizes), in_specs=[HBM, VMEM,...  2.78 us
    pallas_call x1, Pallas kernels, arrived_result(): pl.pallas_call(body, out_shape=result_shape(sizes), in_specs=[VMEM] * (li...  2.18 us
    pallas_call x1, Pallas kernels, source_chunk(): pl.pallas_call(body, out_shape=chunk_shape(sizes), in_specs=[HBM, VMEM, V...  1.93 us
  transfers between devices with their start and end apart: 6, of which 3 were waited for; matrix products, arithmetic and copies ran while one was open for 0% of the time, Pallas kernels for 25%

profile of v2, /device:TPU:0, one launch (start us, length us, event | category | flops | bytes accessed | tf_op | source)
XLA Modules:
  0.0 54.8 jit_solution(10403033759521332913)
XLA Ops:
  0.0 5.0 %collective-permute-start = (s32[64,128]{1,0:T(8,128)}, s32[64,128]{1,0:T(8,128)S(1)}, u32[]{:S(2)}, u32[]{:S(2)}) collective-permute-start(s32[64,128]{1,0:T(8,128)} %bitcast.8), channel_id=1, source_target_pairs={{12,0},{8,4},{4,8},{0,12},{13,1},{9,5},{5,9},{1,13},{14,2},{10,6},... | collective-permute-start | bytes 98312 | tf_op jit(solution)/shard_map/ppermute | solution.py:317
  5.0 0.0 copy-start
  5.1 1.6 %copy-done = f32[1,16,16,1,2048]{4,3,2,1,0:T(1,128)S(1)} copy-done((f32[1,16,16,1,2048]{4,3,2,1,0:T(1,128)S(1)}, f32[1,16,16,1,2048]{4,3,2,1,0:T(1,128)}, u32[]{:S(2)}) %copy-start) | copy-done | bytes 2097176
  6.6 0.0 copy-start.1
  6.6 0.0 copy-start.2
  6.6 0.8 %pack.2 = f32[1024,128]{1,0:T(8,128)S(1)} custom-call(f32[16,256,128]{2,1,0:T(8,128)S(1)} %bitcast.3), custom_call_target="tpu_custom_call" | custom-call | flops 1048576 | bytes 1048576 | tf_op jit(solution)/shard_map/pack/pallas_call | solution.py:136
  7.5 0.1 collective-permute-start.3
  7.6 0.9 %pack.3 = f32[1024,128]{1,0:T(8,128)S(1)} custom-call(f32[16,256,128]{2,1,0:T(8,128)S(1)} %bitcast.4), custom_call_target="tpu_custom_call" | custom-call | flops 1048576 | bytes 1048576 | tf_op jit(solution)/shard_map/pack/pallas_call | solution.py:136
  8.4 0.6 %collective-permute-start.4 = (f32[1024,128]{1,0:T(8,128)S(1)}, f32[1024,128]{1,0:T(8,128)S(1)}, u32[]{:S(2)}, u32[]{:S(2)}) collective-permute-start(f32[1024,128]{1,0:T(8,128)S(1)} %pack.3), channel_id=1, source_target_pairs={{0,4},{4,0},{8,12},{12,8},{1,5},{5,1},{9,13},{13,9},{2,6},{6,2},{1... | collective-permute-start | bytes 1572872 | tf_op jit(solution)/shard_map/ppermute | solution.py:316
  9.0 0.0 collective-permute-done.rest_1_.d_ref
  9.0 0.0 copy-done.1
  9.0 0.0 copy-done.2
  9.0 4.0 %source_panels.1 = f32[2,64,128]{2,1,0:T(8,128)S(1)} custom-call(f32[16,256,128]{2,1,0:T(8,128)S(1)} %bitcast.5, s32[64,128]{1,0:T(8,128)S(1)} %bitcast.9, s32[64,128]{1,0:T(8,128)S(1)} %collective-permute-done.rest_1_.d_ref), custom_call_target="tpu_custom_call" | custom-call | flops 2097152 | bytes 2097152 | tf_op jit(solution)/shard_map/source_panels/pallas_call | solution.py:167
  13.1 3.6 %collective-permute-start.1 = (f32[2,64,128]{2,1,0:T(8,128)S(1)}, f32[2,64,128]{2,1,0:T(8,128)S(1)}, u32[]{:S(2)}, u32[]{:S(2)}) collective-permute-start(f32[2,64,128]{2,1,0:T(8,128)S(1)} %source_panels.1), channel_id=1, source_target_pairs={{0,2},{1,3},{4,6},{5,7},{8,10},{9,11},{12,14},{13,15},{16,18},{17,... | collective-permute-start | bytes 196616 | tf_op jit(solution)/shard_map/ppermute | solution.py:36
  16.7 1.9 %collective-permute-done.1.in_ref = f32[2,64,128]{2,1,0:T(8,128)S(1)} collective-permute-done((f32[2,64,128]{2,1,0:T(8,128)S(1)}, f32[2,64,128]{2,1,0:T(8,128)S(1)}, u32[]{:S(2)}, u32[]{:S(2)}) %collective-permute-start.1) | collective-permute-done | bytes 65568 | tf_op jit(solution)/shard_map/ppermute | solution.py:36
  18.6 1.9 %source_chunk.1 = f32[1024,128]{1,0:T(8,128)S(1)} custom-call(f32[16,256,128]{2,1,0:T(8,128)S(1)} %bitcast.6, s32[64,128]{1,0:T(8,128)S(1)} %collective-permute-done.rest_1_.d_ref, f32[2,64,128]{2,1,0:T(8,128)S(1)} %collective-permute-done.1.in_ref), custom_call_target="tpu_custom_call" | custom-call | flops 1048576 | bytes 1048576 | tf_op jit(solution)/shard_map/source_chunk/pallas_call | solution.py:189
  20.5 3.7 %collective-permute-start.2 = (f32[1024,128]{1,0:T(8,128)S(1)}, f32[1024,128]{1,0:T(8,128)S(1)}, u32[]{:S(2)}, u32[]{:S(2)}) collective-permute-start(f32[1024,128]{1,0:T(8,128)S(1)} %source_chunk.1), channel_id=1, source_target_pairs={{0,12},{4,8},{8,4},{12,0},{1,13},{5,9},{9,5},{13,1},{2,14},{6,10},... | collective-permute-start | bytes 1572872 | tf_op jit(solution)/shard_map/ppermute | solution.py:326
  24.2 9.5 %collective-permute-done.3.refs_0_ = f32[1024,128]{1,0:T(8,128)S(1)} collective-permute-done((f32[1024,128]{1,0:T(8,128)S(1)}, f32[1024,128]{1,0:T(8,128)S(1)}, u32[]{:S(2)}, u32[]{:S(2)}) %collective-permute-start.3) | collective-permute-done | bytes 524320 | tf_op jit(solution)/shard_map/ppermute | solution.py:316
  33.7 10.7 %collective-permute-done.4.refs_1_ = f32[1024,128]{1,0:T(8,128)S(1)} collective-permute-done((f32[1024,128]{1,0:T(8,128)S(1)}, f32[1024,128]{1,0:T(8,128)S(1)}, u32[]{:S(2)}, u32[]{:S(2)}) %collective-permute-start.4) | collective-permute-done | bytes 524320 | tf_op jit(solution)/shard_map/ppermute | solution.py:316
  44.4 1.2 %arrived_panels.1 = f32[2,64,128]{2,1,0:T(8,128)S(1)} custom-call(f32[1024,128]{1,0:T(8,128)S(1)} %collective-permute-done.3.refs_0_, f32[1024,128]{1,0:T(8,128)S(1)} %collective-permute-done.4.refs_1_, s32[64,128]{1,0:T(8,128)S(1)} %bitcast.10), custom_call_target="tpu_custom_call" | custom-call | flops 2097152 | bytes 2097152 | tf_op jit(solution)/shard_map/arrived_panels/pallas_call | solution.py:243
  45.5 3.4 %collective-permute-start.5 = (f32[2,64,128]{2,1,0:T(8,128)S(1)}, f32[2,64,128]{2,1,0:T(8,128)S(1)}, u32[]{:S(2)}, u32[]{:S(2)}) collective-permute-start(f32[2,64,128]{2,1,0:T(8,128)S(1)} %arrived_panels.1), channel_id=1, source_target_pairs={{0,2},{1,3},{4,6},{5,7},{8,10},{9,11},{12,14},{13,15},{16,18},{17,... | collective-permute-start | bytes 196616 | tf_op jit(solution)/shard_map/ppermute | solution.py:36
  48.9 2.8 %own_result.1.refs_4_ = f32[4096,128]{1,0:T(8,128)} custom-call(f32[16,256,128]{2,1,0:T(8,128)S(1)} %bitcast.7, s32[64,128]{1,0:T(8,128)S(1)} %bitcast.11, f32[2,64,128]{2,1,0:T(8,128)S(1)} %collective-permute-done.1.in_ref), custom_call_target="tpu_custom_call" | custom-call | flops 1048576 | bytes 1048576 | tf_op jit(solution)/shard_map/own_result/pallas_call | solution.py:215
  51.7 0.0 collective-permute-done.5.refs_3_
  51.7 2.2 %arrived_result.1._ = f32[4096,128]{1,0:T(8,128)} custom-call(f32[1024,128]{1,0:T(8,128)S(1)} %collective-permute-done.3.refs_0_, f32[1024,128]{1,0:T(8,128)S(1)} %collective-permute-done.4.refs_1_, s32[64,128]{1,0:T(8,128)S(1)} %bitcast.12, f32[2,64,128]{2,1,0:T(8,128)S(1)} %collective-permute-done.5.refs_3_, ...), custom_call_target="tpu_custom_call", output_to_operand_aliasing={{}: (4, {})} | custom-call | flops 2097152 | bytes 2097152 | tf_op jit(solution)/shard_map/arrived_result/pallas_call | solution.py:268
  53.9 0.0 collective-permute-done.2.x_ref
  53.9 0.8 %place_chunk.1 = f32[4096,128]{1,0:T(8,128)} custom-call(f32[1024,128]{1,0:T(8,128)S(1)} %collective-permute-done.2.x_ref, f32[4096,128]{1,0:T(8,128)} %arrived_result.1._), custom_call_target="tpu_custom_call", output_to_operand_aliasing={{}: (1, {})} | custom-call | flops 1048576 | bytes 1048576 | tf_op jit(solution)/shard_map/place_chunk/pallas_call | solution.py:291
Async XLA Ops:
  0.0 9.0 %collective-permute-start = (s32[64,128]{1,0:T(8,128)}, s32[64,128]{1,0:T(8,128)S(1)}, u32[]{:S(2)}, u32[]{:S(2)}) collective-permute-start(s32[64,128]{1,0:T(8,128)} %bitcast.8), channel_id=1, source_target_pairs={{12,0},{8,4},{4,8},{0,12},{13,1},{9,5},{5,9},{1,13},{14,2},{10,6},... | collective-permute-start | bytes 98312 | tf_op jit(solution)/shard_map/ppermute | solution.py:317
  5.0 1.6 %copy-start = (f32[1,16,16,1,2048]{4,3,2,1,0:T(1,128)S(1)}, f32[1,16,16,1,2048]{4,3,2,1,0:T(1,128)}, u32[]{:S(2)}) copy-start(f32[1,16,16,1,2048]{4,3,2,1,0:T(1,128)} %param.2) | copy-start | bytes 6291460
  6.6 2.4 %copy-start.1 = (f32[1,16,16,1,2048]{4,3,2,1,0:T(1,128)S(1)}, f32[1,16,16,1,2048]{4,3,2,1,0:T(1,128)}, u32[]{:S(2)}) copy-start(f32[1,16,16,1,2048]{4,3,2,1,0:T(1,128)} %param.2) | copy-start | bytes 6291460
  6.6 2.4 %copy-start.2 = (s32[4,1,2048]{2,1,0:T(1,128)S(1)}, s32[4,1,2048]{2,1,0:T(1,128)}, u32[]{:S(2)}) copy-start(s32[4,1,2048]{2,1,0:T(1,128)} %param.3) | copy-start | bytes 98308
  7.5 26.2 %collective-permute-start.3 = (f32[1024,128]{1,0:T(8,128)S(1)}, f32[1024,128]{1,0:T(8,128)S(1)}, u32[]{:S(2)}, u32[]{:S(2)}) collective-permute-start(f32[1024,128]{1,0:T(8,128)S(1)} %pack.2), channel_id=1, source_target_pairs={{0,8},{4,12},{8,0},{12,4},{1,9},{5,13},{9,1},{13,5},{2,10},{6,14},... | collective-permute-start | bytes 1572872 | tf_op jit(solution)/shard_map/ppermute | solution.py:316
  8.4 35.9 %collective-permute-start.4 = (f32[1024,128]{1,0:T(8,128)S(1)}, f32[1024,128]{1,0:T(8,128)S(1)}, u32[]{:S(2)}, u32[]{:S(2)}) collective-permute-start(f32[1024,128]{1,0:T(8,128)S(1)} %pack.3), channel_id=1, source_target_pairs={{0,4},{4,0},{8,12},{12,8},{1,5},{5,1},{9,13},{13,9},{2,6},{6,2},{1... | collective-permute-start | bytes 1572872 | tf_op jit(solution)/shard_map/ppermute | solution.py:316
  13.1 5.5 %collective-permute-start.1 = (f32[2,64,128]{2,1,0:T(8,128)S(1)}, f32[2,64,128]{2,1,0:T(8,128)S(1)}, u32[]{:S(2)}, u32[]{:S(2)}) collective-permute-start(f32[2,64,128]{2,1,0:T(8,128)S(1)} %source_panels.1), channel_id=1, source_target_pairs={{0,2},{1,3},{4,6},{5,7},{8,10},{9,11},{12,14},{13,15},{16,18},{17,... | collective-permute-start | bytes 196616 | tf_op jit(solution)/shard_map/ppermute | solution.py:36
  20.5 33.4 %collective-permute-start.2 = (f32[1024,128]{1,0:T(8,128)S(1)}, f32[1024,128]{1,0:T(8,128)S(1)}, u32[]{:S(2)}, u32[]{:S(2)}) collective-permute-start(f32[1024,128]{1,0:T(8,128)S(1)} %source_chunk.1), channel_id=1, source_target_pairs={{0,12},{4,8},{8,4},{12,0},{1,13},{5,9},{9,5},{13,1},{2,14},{6,10},... | collective-permute-start | bytes 1572872 | tf_op jit(solution)/shard_map/ppermute | solution.py:326
  45.5 6.2 %collective-permute-start.5 = (f32[2,64,128]{2,1,0:T(8,128)S(1)}, f32[2,64,128]{2,1,0:T(8,128)S(1)}, u32[]{:S(2)}, u32[]{:S(2)}) collective-permute-start(f32[2,64,128]{2,1,0:T(8,128)S(1)} %arrived_panels.1), channel_id=1, source_target_pairs={{0,2},{1,3},{4,6},{5,7},{8,10},{9,11},{12,14},{13,15},{16,18},{17,... | collective-permute-start | bytes 196616 | tf_op jit(solution)/shard_map/ppermute | solution.py:36

commit v3 on v2

--- a/solution.py
+++ b/solution.py
@@ -7,7 +7,7 @@
 
 ROWS = 128
 SUB = 8
-HBM = pl.BlockSpec(memory_space=pl.ANY)
+HBM = pl.BlockSpec(memory_space=pltpu.HBM)
 VMEM = pl.BlockSpec(memory_space=pltpu.VMEM)
 
 
@@ -124,7 +124,7 @@
 
 
 def cost(chunks):
-    return pl.CostEstimate(flops=chunks * (1 << 20), bytes_accessed=chunks * (1 << 20), transcendentals=0)
+    return pl.CostEstimate(flops=chunks, bytes_accessed=chunks, transcendentals=0)
 
 
 def pack(x, k, sizes):
@@ -179,54 +179,35 @@
     )(x, *codes, *([inflow] if inflow is not None else []))
 
 
-def source_chunk(x, k, codes, inflow, i, sizes):
-    def body(x_ref, d_ref, in_ref, o_ref, buf, sem):
-        copies = gather_copies(x_ref, buf, sem, target_of(k, sizes.basins), sizes)
-        start_all(copies)
-        wait_all(copies)
-        sweep(buf, d_ref, registers(in_ref, i, sizes), o_ref, sizes)
-
-    return pl.pallas_call(
-        body,
-        out_shape=chunk_shape(sizes),
-        in_specs=[HBM, VMEM, VMEM],
-        out_specs=VMEM,
+def source_chunks(x, ks, codes, inflow, sizes):
+    listed = len(ks)
+
+    def body(x_ref, *rest):
+        d_refs, in_ref, o_refs = rest[:listed], rest[listed], rest[listed + 1 : 2 * listed + 1]
+        buf, sem = rest[-2:]
+        copies = [
+            gather_copies(x_ref, buf.at[i], sem.at[i], target_of(k, sizes.basins), sizes)
+            for i, k in enumerate(ks)
+        ]
+        for c in copies:
+            start_all(c)
+        for i in range(listed):
+            wait_all(copies[i])
+            sweep(buf.at[i], d_refs[i], registers(in_ref, i, sizes), o_refs[i], sizes)
+
+    return pl.pallas_call(
+        body,
+        out_shape=[chunk_shape(sizes)] * listed,
+        in_specs=[HBM] + [VMEM] * (listed + 1),
+        out_specs=[VMEM] * listed,
         scratch_shapes=[
-            pltpu.VMEM((sizes.rows, ROWS), jnp.float32),
-            pltpu.SemaphoreType.DMA((sizes.members,)),
+            pltpu.VMEM((listed, sizes.rows, ROWS), jnp.float32),
+            pltpu.SemaphoreType.DMA((listed, sizes.members)),
         ],
-        cost_estimate=cost(1),
-        compiler_params=params(sizes, 3),
-        name="source_chunk",
-    )(x, codes, inflow)
-
-
-def own_result(x, codes, inflow, sizes):
-    def body(x_ref, d_ref, in_ref, o_ref, buf, out, sem, out_sem):
-        copies = gather_copies(x_ref, buf, sem, lax.axis_index("basin"), sizes)
-        start_all(copies)
-        wait_all(copies)
-        sweep(buf, d_ref, registers(in_ref, 0, sizes), out, sizes)
-        place = o_ref.at[pl.ds(lax.axis_index("basin") * sizes.rows, sizes.rows)]
-        copy = pltpu.make_async_copy(out, place, out_sem)
-        copy.start()
-        copy.wait()
-
-    return pl.pallas_call(
-        body,
-        out_shape=result_shape(sizes),
-        in_specs=[HBM, VMEM, VMEM],
-        out_specs=HBM,
-        scratch_shapes=[
-            pltpu.VMEM((sizes.rows, ROWS), jnp.float32),
-            pltpu.VMEM((sizes.rows, ROWS), jnp.float32),
-            pltpu.SemaphoreType.DMA((sizes.members,)),
-            pltpu.SemaphoreType.DMA,
-        ],
-        cost_estimate=cost(1),
-        compiler_params=params(sizes, 3),
-        name="own_result",
-    )(x, codes, inflow)
+        compiler_params=params(sizes, 3 * listed),
+        cost_estimate=cost(listed),
+        name="source_chunks",
+    )(x, *codes, inflow)
 
 
 def arrived_panels(chunks, codes, inflow, sizes):
@@ -251,7 +232,7 @@
     )(*chunks, codes, *([inflow] if inflow is not None else []))
 
 
-def arrived_result(chunks, ks, codes, inflow, result, sizes):
+def arrived_result(chunks, ks, codes, inflow, sizes):
     listed = len(chunks)
 
     def body(*refs):
@@ -268,17 +249,16 @@
     return pl.pallas_call(
         body,
         out_shape=result_shape(sizes),
-        in_specs=[VMEM] * (listed + 2) + [HBM],
+        in_specs=[VMEM] * (listed + 2),
         out_specs=HBM,
         scratch_shapes=[
             pltpu.VMEM((listed, sizes.rows, ROWS), jnp.float32),
             pltpu.SemaphoreType.DMA((listed,)),
         ],
-        input_output_aliases={listed + 2: 0},
         cost_estimate=cost(listed),
         compiler_params=params(sizes, 3 * listed),
         name="arrived_result",
-    )(*chunks, codes, inflow, result)
+    )(*chunks, codes, inflow)
 
 
 def place_chunk(chunk, k, result, sizes):
@@ -306,33 +286,34 @@
     _, members, all_tiles, _, cell_count = runoff.shape
     sizes = Sizes(members, directions.shape[0], cell_count // ROWS, basins)
     x = runoff.reshape(members, all_tiles * sizes.columns, ROWS)
+    x = pltpu.with_memory_space_constraint(x, pltpu.HBM)
     codes = directions.reshape(sizes.per_member, ROWS)
 
-    early = sorted({basins // 2, 1}, reverse=True)
+    early = [basins // 2]
     late = [k for k in range(basins - 1, 0, -1) if k not in early]
     pairs = {k: exchange_pairs(basins, k) for k in range(basins)}
-    listed = [0] + late
-
-    arrived = {k: lax.ppermute(pack(x, k, sizes), "basin", pairs[k]) for k in early}
-    dirs = [codes] + [lax.ppermute(codes, "basin", reversed_pairs(pairs[k])) for k in late]
+
+    packed = [pack(x, k, sizes) for k in early]
+    packed, codes = lax.optimization_barrier((packed, codes))
+    arrived = {k: lax.ppermute(value, "basin", pairs[k]) for k, value in zip(early, packed)}
+    dirs = [lax.ppermute(codes, "basin", reversed_pairs(pairs[k])) for k in late]
 
     inflow = None
     for _ in range(chain - 1):
-        inflow = from_behind(source_panels(x, listed, dirs, inflow, sizes), "chain")
+        inflow = from_behind(source_panels(x, late, dirs, inflow, sizes), "chain")
     if inflow is None:
-        inflow = jnp.zeros((len(listed), sizes.count, ROWS), jnp.float32)
-    for i, k in enumerate(listed):
-        if k:
-            arrived[k] = lax.ppermute(source_chunk(x, k, dirs[i], inflow, i, sizes), "basin", pairs[k])
-    result = own_result(x, codes, inflow, sizes)
-
-    chunks = [arrived[k] for k in early]
+        inflow = jnp.zeros((len(late), sizes.count, ROWS), jnp.float32)
+    chunks = source_chunks(x, late, dirs, inflow, sizes)
+    for k, chunk in zip(late, chunks):
+        arrived[k] = lax.ppermute(chunk, "basin", pairs[k])
+
+    chunks = [pack(x, 0, sizes)] + [arrived[k] for k in early]
     inflow = None
     for _ in range(chain - 1):
         inflow = from_behind(arrived_panels(chunks, codes, inflow, sizes), "chain")
     if inflow is None:
-        inflow = jnp.zeros((len(early), sizes.count, ROWS), jnp.float32)
-    result = arrived_result(chunks, early, codes, inflow, result, sizes)
+        inflow = jnp.zeros((len(chunks), sizes.count, ROWS), jnp.float32)
+    result = arrived_result(chunks, [0] + early, codes, inflow, sizes)
     for k in late:
         result = place_chunk(arrived[k], k, result, sizes)
     return result.reshape(basins * members, sizes.tiles, 1, cell_count)

time: 54.9 us -> 56.1 us (1.022)
  starting transfers between devices: 16.4 us -> 25.1 us
  waiting for transfers between devices: 22.1 us -> 15.9 us
  local copies, waits for them, and re-layouts: 1.6 us -> 0.01 us
    ppermute x3, waiting for transfers between devices: 20.2 us -> 8.6 us  [the longest x1 7.11 us: local(): lax.ppermute(value, 'basin', pairs[k])]
    ppermute x3, starting transfers between devices: 4.31 us -> 12.8 us  [the longest x2 12.7 us: local(): arrived[k] = lax.ppermute(chunk, 'basin', pairs[k])]
    ppermute x1 -> x2, waiting for transfers between devices: 0.01 us -> 3.57 us  [local(): lax.ppermute(codes, 'basin', reversed_pairs(pairs[k]))]
    ppermute x2, waiting for transfers between devices: 1.89 us -> 3.77 us  [from_behind(): return lax.ppermute(value, axis, [(i, i + 1) for i in range(count - 1)])]
    unnamed x6 -> x2, local copies, waits for them, and re-layouts: 1.6 us -> 0.01 us
    pallas_call x2 -> x1, Pallas kernels: 4.72 us -> 3.54 us  [source_chunks(): pl.pallas_call(body, out_shape=[chunk_shape(sizes)] * listed, in_specs=[H...]
    pallas_call x1 -> x2, Pallas kernels: 0.82 us -> 1.62 us  [place_chunk(): pl.pallas_call(body, out_shape=result_shape(sizes), in_specs=[VMEM, HBM],...]
    pallas_call x2, Pallas kernels: 1.69 us -> 2.27 us  [pack(): pl.pallas_call(body, out_shape=chunk_shape(sizes), in_specs=[HBM], out_sp...]
  transfers between devices with their start and end apart: 6 -> 7, of which waited for: 3 -> 5; matrix products, arithmetic and copies ran while one was open for 0% -> 0% of each run, Pallas kernels for 25% -> 22%
where the time goes in v3:
time: 56.1 us; the launch traced here: 55.6 us
  starting transfers between devices  25.1 us (45%)
  waiting for transfers between devices  15.9 us (28%)
  Pallas kernels  14.4 us (26%)
    ppermute x2, starting transfers between devices, local(): arrived[k] = lax.ppermute(chunk, 'basin', pairs[k])  12.7 us
    ppermute x1, waiting for transfers between devices, local(): lax.ppermute(value, 'basin', pairs[k])  7.11 us
    ppermute x2, starting transfers between devices, from_behind(): return lax.ppermute(value, axis, [(i, i + 1) for i in range(count - 1)])  6.8 us
    ppermute x2, starting transfers between devices, local(): lax.ppermute(codes, 'basin', reversed_pairs(pairs[k]))  5.56 us
    ppermute x2, waiting for transfers between devices, from_behind(): return lax.ppermute(value, axis, [(i, i + 1) for i in range(count - 1)])  3.77 us
    pallas_call x1, Pallas kernels, source_panels(): pl.pallas_call(body, out_shape=panel_shape(listed, sizes), in_specs=[HBM]...  3.62 us
    ppermute x2, waiting for transfers between devices, local(): lax.ppermute(codes, 'basin', reversed_pairs(pairs[k]))  3.57 us
    pallas_call x1, Pallas kernels, source_chunks(): pl.pallas_call(body, out_shape=[chunk_shape(sizes)] * listed, in_specs=[H...  3.54 us
  transfers between devices with their start and end apart: 7, of which 5 were waited for; matrix products, arithmetic and copies ran while one was open for 0% of the time, Pallas kernels for 22%

profile of v3, /device:TPU:0, one launch (start us, length us, event | category | flops | bytes accessed | tf_op | source)
XLA Modules:
  0.0 55.6 jit_solution(16271962192688339348)
XLA Ops:
  0.0 0.0 copy-start
  0.0 1.1 %pack.2 = f32[1024,128]{1,0:T(8,128)S(1)} custom-call(f32[16,256,128]{2,1,0:T(8,128)} %bitcast.7), custom_call_target="tpu_custom_call" | custom-call | flops 1 | bytes 1 | tf_op jit(solution)/shard_map/pack/pallas_call | solution.py:136
  1.1 0.0 copy-done
  1.2 3.1 %collective-permute-start.1 = (s32[64,128]{1,0:T(8,128)S(1)}, s32[64,128]{1,0:T(8,128)S(1)}, u32[]{:S(2)}, u32[]{:S(2)}) collective-permute-start(s32[64,128]{1,0:T(8,128)S(1)} %bitcast.3), channel_id=1, source_target_pairs={{4,0},{0,4},{12,8},{8,12},{5,1},{1,5},{13,9},{9,13},{6,2},{2,6},{1... | collective-permute-start | bytes 98312 | tf_op jit(solution)/shard_map/ppermute | solution.py:299
  4.2 2.5 %collective-permute-start = (s32[64,128]{1,0:T(8,128)S(1)}, s32[64,128]{1,0:T(8,128)S(1)}, u32[]{:S(2)}, u32[]{:S(2)}) collective-permute-start(s32[64,128]{1,0:T(8,128)S(1)} %bitcast.4), channel_id=1, source_target_pairs={{12,0},{8,4},{4,8},{0,12},{13,1},{9,5},{5,9},{1,13},{14,2},{10,6},... | collective-permute-start | bytes 98312 | tf_op jit(solution)/shard_map/ppermute | solution.py:299
  6.7 0.1 collective-permute-start.5
  6.8 0.0 collective-permute-done.1.rest_1_
  6.8 3.6 %collective-permute-done.rest_0_ = s32[64,128]{1,0:T(8,128)S(1)} collective-permute-done((s32[64,128]{1,0:T(8,128)S(1)}, s32[64,128]{1,0:T(8,128)S(1)}, u32[]{:S(2)}, u32[]{:S(2)}) %collective-permute-start) | collective-permute-done | bytes 32800 | tf_op jit(solution)/shard_map/ppermute | solution.py:299
  10.4 3.6 %source_panels.1 = f32[2,64,128]{2,1,0:T(8,128)S(1)} custom-call(f32[16,256,128]{2,1,0:T(8,128)} %bitcast.8, s32[64,128]{1,0:T(8,128)S(1)} %collective-permute-done.rest_0_, s32[64,128]{1,0:T(8,128)S(1)} %collective-permute-done.1.rest_1_), custom_call_target="tpu_custom_call" | custom-call | flops 2 | bytes 2 | tf_op jit(solution)/shard_map/source_panels/pallas_call | solution.py:167
  14.0 3.4 %collective-permute-start.2 = (f32[2,64,128]{2,1,0:T(8,128)S(1)}, f32[2,64,128]{2,1,0:T(8,128)S(1)}, u32[]{:S(2)}, u32[]{:S(2)}) collective-permute-start(f32[2,64,128]{2,1,0:T(8,128)S(1)} %source_panels.1), channel_id=1, source_target_pairs={{0,2},{1,3},{4,6},{5,7},{8,10},{9,11},{12,14},{13,15},{16,18},{17,... | collective-permute-start | bytes 196616 | tf_op jit(solution)/shard_map/ppermute | solution.py:36
  17.4 1.9 %collective-permute-done.2.rest_2_ = f32[2,64,128]{2,1,0:T(8,128)S(1)} collective-permute-done((f32[2,64,128]{2,1,0:T(8,128)S(1)}, f32[2,64,128]{2,1,0:T(8,128)S(1)}, u32[]{:S(2)}, u32[]{:S(2)}) %collective-permute-start.2) | collective-permute-done | bytes 65568 | tf_op jit(solution)/shard_map/ppermute | solution.py:36
  19.3 3.5 %source_chunks.1 = (f32[1024,128]{1,0:T(8,128)S(1)}, f32[1024,128]{1,0:T(8,128)S(1)}) custom-call(f32[16,256,128]{2,1,0:T(8,128)} %bitcast.9, s32[64,128]{1,0:T(8,128)S(1)} %collective-permute-done.rest_0_, s32[64,128]{1,0:T(8,128)S(1)} %collective-permute-done.1.rest_1_, f32[2,64,128]{2,1,0:T(8,128)S(1)} %collective-permute-done.2.rest_2_), custom_call_target="tpu_custom_call" | custom-call | flops 2 | bytes 2 | tf_op jit(solution)/shard_map/source_chunks/pallas_call | solution.py:198
  22.9 2.6 %collective-permute-start.4 = (f32[1024,128]{1,0:T(8,128)S(1)}, f32[1024,128]{1,0:T(8,128)S(1)}, u32[]{:S(2)}, u32[]{:S(2)}) collective-permute-start(f32[1024,128]{1,0:T(8,128)S(1)} %get-tuple-element.11), channel_id=1, source_target_pairs={{0,12},{4,8},{8,4},{12,0},{1,13},{5,9},{9,5},{13,1},{2,14},{6,10},... | collective-permute-start | bytes 1572872 | tf_op jit(solution)/shard_map/ppermute | solution.py:308
  25.5 10.1 %collective-permute-start.3 = (f32[1024,128]{1,0:T(8,128)S(1)}, f32[1024,128]{1,0:T(8,128)S(1)}, u32[]{:S(2)}, u32[]{:S(2)}) collective-permute-start(f32[1024,128]{1,0:T(8,128)S(1)} %get-tuple-element.10), channel_id=1, source_target_pairs={{0,4},{4,0},{8,12},{12,8},{1,5},{5,1},{9,13},{13,9},{2,6},{6,2},{1... | collective-permute-start | bytes 1572872 | tf_op jit(solution)/shard_map/ppermute | solution.py:308
  35.5 1.1 %pack.3.refs_0_ = f32[1024,128]{1,0:T(8,128)S(1)} custom-call(f32[16,256,128]{2,1,0:T(8,128)} %bitcast.10), custom_call_target="tpu_custom_call" | custom-call | flops 1 | bytes 1 | tf_op jit(solution)/shard_map/pack/pallas_call | solution.py:136
  36.7 7.1 %collective-permute-done.5.refs_1_ = f32[1024,128]{1,0:T(8,128)S(1)} collective-permute-done((f32[1024,128]{1,0:T(8,128)S(1)}, f32[1024,128]{1,0:T(8,128)S(1)}, u32[]{:S(2)}, u32[]{:S(2)}) %collective-permute-start.5) | collective-permute-done | bytes 524320 | tf_op jit(solution)/shard_map/ppermute | solution.py:298
  43.8 1.2 %arrived_panels.1 = f32[2,64,128]{2,1,0:T(8,128)S(1)} custom-call(f32[1024,128]{1,0:T(8,128)S(1)} %pack.3.refs_0_, f32[1024,128]{1,0:T(8,128)S(1)} %collective-permute-done.5.refs_1_, s32[64,128]{1,0:T(8,128)S(1)} %bitcast.5), custom_call_target="tpu_custom_call" | custom-call | flops 2 | bytes 2 | tf_op jit(solution)/shard_map/arrived_panels/pallas_call | solution.py:224
  45.0 3.4 %collective-permute-start.6 = (f32[2,64,128]{2,1,0:T(8,128)S(1)}, f32[2,64,128]{2,1,0:T(8,128)S(1)}, u32[]{:S(2)}, u32[]{:S(2)}) collective-permute-start(f32[2,64,128]{2,1,0:T(8,128)S(1)} %arrived_panels.1), channel_id=1, source_target_pairs={{0,2},{1,3},{4,6},{5,7},{8,10},{9,11},{12,14},{13,15},{16,18},{17,... | collective-permute-start | bytes 196616 | tf_op jit(solution)/shard_map/ppermute | solution.py:36
  48.4 1.9 %collective-permute-done.6.refs_3_ = f32[2,64,128]{2,1,0:T(8,128)S(1)} collective-permute-done((f32[2,64,128]{2,1,0:T(8,128)S(1)}, f32[2,64,128]{2,1,0:T(8,128)S(1)}, u32[]{:S(2)}, u32[]{:S(2)}) %collective-permute-start.6) | collective-permute-done | bytes 65568 | tf_op jit(solution)/shard_map/ppermute | solution.py:36
  50.3 2.2 %arrived_result.1._ = f32[4096,128]{1,0:T(8,128)} custom-call(f32[1024,128]{1,0:T(8,128)S(1)} %pack.3.refs_0_, f32[1024,128]{1,0:T(8,128)S(1)} %collective-permute-done.5.refs_1_, s32[64,128]{1,0:T(8,128)S(1)} %bitcast.6, f32[2,64,128]{2,1,0:T(8,128)S(1)} %collective-permute-done.6.refs_3_), custom_call_target="tpu_custom_call" | custom-call | flops 2 | bytes 2 | tf_op jit(solution)/shard_map/arrived_result/pallas_call | solution.py:249
  52.5 0.0 collective-permute-done.4.x_ref
  52.5 0.8 %place_chunk.2._ = f32[4096,128]{1,0:T(8,128)} custom-call(f32[1024,128]{1,0:T(8,128)S(1)} %collective-permute-done.4.x_ref, f32[4096,128]{1,0:T(8,128)} %arrived_result.1._), custom_call_target="tpu_custom_call", output_to_operand_aliasing={{}: (1, {})} | custom-call | flops 1 | bytes 1 | tf_op jit(solution)/shard_map/place_chunk/pallas_call | solution.py:271
  53.3 1.5 %collective-permute-done.3.x_ref = f32[1024,128]{1,0:T(8,128)S(1)} collective-permute-done((f32[1024,128]{1,0:T(8,128)S(1)}, f32[1024,128]{1,0:T(8,128)S(1)}, u32[]{:S(2)}, u32[]{:S(2)}) %collective-permute-start.3) | collective-permute-done | bytes 524320 | tf_op jit(solution)/shard_map/ppermute | solution.py:308
  54.8 0.8 %place_chunk.3 = f32[4096,128]{1,0:T(8,128)} custom-call(f32[1024,128]{1,0:T(8,128)S(1)} %collective-permute-done.3.x_ref, f32[4096,128]{1,0:T(8,128)} %place_chunk.2._), custom_call_target="tpu_custom_call", output_to_operand_aliasing={{}: (1, {})} | custom-call | flops 1 | bytes 1 | tf_op jit(solution)/shard_map/place_chunk/pallas_call | solution.py:271
Async XLA Ops:
  0.0 1.1 %copy-start = (s32[4,1,2048]{2,1,0:T(1,128)S(1)}, s32[4,1,2048]{2,1,0:T(1,128)}, u32[]{:S(2)}) copy-start(s32[4,1,2048]{2,1,0:T(1,128)} %param.3) | copy-start | bytes 98308
  1.2 5.7 %collective-permute-start.1 = (s32[64,128]{1,0:T(8,128)S(1)}, s32[64,128]{1,0:T(8,128)S(1)}, u32[]{:S(2)}, u32[]{:S(2)}) collective-permute-start(s32[64,128]{1,0:T(8,128)S(1)} %bitcast.3), channel_id=1, source_target_pairs={{4,0},{0,4},{12,8},{8,12},{5,1},{1,5},{13,9},{9,13},{6,2},{2,6},{1... | collective-permute-start | bytes 98312 | tf_op jit(solution)/shard_map/ppermute | solution.py:299
  4.2 6.2 %collective-permute-start = (s32[64,128]{1,0:T(8,128)S(1)}, s32[64,128]{1,0:T(8,128)S(1)}, u32[]{:S(2)}, u32[]{:S(2)}) collective-permute-start(s32[64,128]{1,0:T(8,128)S(1)} %bitcast.4), channel_id=1, source_target_pairs={{12,0},{8,4},{4,8},{0,12},{13,1},{9,5},{5,9},{1,13},{14,2},{10,6},... | collective-permute-start | bytes 98312 | tf_op jit(solution)/shard_map/ppermute | solution.py:299
  6.7 37.1 %collective-permute-start.5 = (f32[1024,128]{1,0:T(8,128)S(1)}, f32[1024,128]{1,0:T(8,128)S(1)}, u32[]{:S(2)}, u32[]{:S(2)}) collective-permute-start(f32[1024,128]{1,0:T(8,128)S(1)} %pack.2), channel_id=1, source_target_pairs={{0,8},{4,12},{8,0},{12,4},{1,9},{5,13},{9,1},{13,5},{2,10},{6,14},... | collective-permute-start | bytes 1572872 | tf_op jit(solution)/shard_map/ppermute | solution.py:298
  14.0 5.3 %collective-permute-start.2 = (f32[2,64,128]{2,1,0:T(8,128)S(1)}, f32[2,64,128]{2,1,0:T(8,128)S(1)}, u32[]{:S(2)}, u32[]{:S(2)}) collective-permute-start(f32[2,64,128]{2,1,0:T(8,128)S(1)} %source_panels.1), channel_id=1, source_target_pairs={{0,2},{1,3},{4,6},{5,7},{8,10},{9,11},{12,14},{13,15},{16,18},{17,... | collective-permute-start | bytes 196616 | tf_op jit(solution)/shard_map/ppermute | solution.py:36
  22.9 29.6 %collective-permute-start.4 = (f32[1024,128]{1,0:T(8,128)S(1)}, f32[1024,128]{1,0:T(8,128)S(1)}, u32[]{:S(2)}, u32[]{:S(2)}) collective-permute-start(f32[1024,128]{1,0:T(8,128)S(1)} %get-tuple-element.11), channel_id=1, source_target_pairs={{0,12},{4,8},{8,4},{12,0},{1,13},{5,9},{9,5},{13,1},{2,14},{6,10},... | collective-permute-start | bytes 1572872 | tf_op jit(solution)/shard_map/ppermute | solution.py:308
  25.5 29.3 %collective-permute-start.3 = (f32[1024,128]{1,0:T(8,128)S(1)}, f32[1024,128]{1,0:T(8,128)S(1)}, u32[]{:S(2)}, u32[]{:S(2)}) collective-permute-start(f32[1024,128]{1,0:T(8,128)S(1)} %get-tuple-element.10), channel_id=1, source_target_pairs={{0,4},{4,0},{8,12},{12,8},{1,5},{5,1},{9,13},{13,9},{2,6},{6,2},{1... | collective-permute-start | bytes 1572872 | tf_op jit(solution)/shard_map/ppermute | solution.py:308
  45.0 5.3 %collective-permute-start.6 = (f32[2,64,128]{2,1,0:T(8,128)S(1)}, f32[2,64,128]{2,1,0:T(8,128)S(1)}, u32[]{:S(2)}, u32[]{:S(2)}) collective-permute-start(f32[2,64,128]{2,1,0:T(8,128)S(1)} %arrived_panels.1), channel_id=1, source_target_pairs={{0,2},{1,3},{4,6},{5,7},{8,10},{9,11},{12,14},{13,15},{16,18},{17,... | collective-permute-start | bytes 196616 | tf_op jit(solution)/shard_map/ppermute | solution.py:36

commit v4 on v3

--- a/solution.py
+++ b/solution.py
@@ -34,6 +34,17 @@
 def from_behind(value, axis):
     count = lax.axis_size(axis)
     return lax.ppermute(value, axis, [(i, i + 1) for i in range(count - 1)])
+
+
+def fetched(codes, pairs):
+    cores = lax.axis_size("mem")
+    giver = cores - 1
+    steps = [(a * cores + giver, b * cores + giver) for a, b in pairs]
+    got = lax.ppermute(codes, ("basin", "mem"), steps)
+    total = got
+    for core in range(giver):
+        total = total + lax.ppermute(got, "mem", [(giver, core)])
+    return total
 
 
 class Sizes:
@@ -289,14 +300,15 @@
     x = pltpu.with_memory_space_constraint(x, pltpu.HBM)
     codes = directions.reshape(sizes.per_member, ROWS)
 
-    early = [basins // 2]
+    early = [basins - 1]
     late = [k for k in range(basins - 1, 0, -1) if k not in early]
     pairs = {k: exchange_pairs(basins, k) for k in range(basins)}
 
     packed = [pack(x, k, sizes) for k in early]
     packed, codes = lax.optimization_barrier((packed, codes))
     arrived = {k: lax.ppermute(value, "basin", pairs[k]) for k, value in zip(early, packed)}
-    dirs = [lax.ppermute(codes, "basin", reversed_pairs(pairs[k])) for k in late]
+    fetch = lambda value: [fetched(value, reversed_pairs(pairs[k])) for k in late]
+    dirs = lax.cond(directions[0, 0, 0] < 3, fetch, lambda value: [value] * len(late), codes)
 
     inflow = None
     for _ in range(chain - 1):

time: 56.1 us -> 70.2 us (1.25)
  waiting for transfers between devices: 15.9 us -> 34.3 us
  starting transfers between devices: 25.1 us -> 19.6 us
    ppermute x2 -> x4, waiting for transfers between devices: 3.57 us -> 19 us  [the longest x2 19 us: fetched(): total = total + lax.ppermute(got, 'mem', [(giver, core)])]
    ppermute x2, waiting for transfers between devices: 1.5 us -> 11.5 us  [local(): arrived[k] = lax.ppermute(chunk, 'basin', pairs[k])]
    ppermute x2, starting transfers between devices: 12.7 us -> 2.91 us  [local(): arrived[k] = lax.ppermute(chunk, 'basin', pairs[k])]
    ppermute x1, waiting for transfers between devices: 7.11 us -> 0.01 us  [local(): lax.ppermute(value, 'basin', pairs[k])]
    ppermute x1, starting transfers between devices: 0.12 us -> 5.11 us  [local(): lax.ppermute(value, 'basin', pairs[k])]
    ppermute x2 -> x4, starting transfers between devices: 5.56 us -> 3.91 us  [the longest x2 2.58 us: fetched(): total = total + lax.ppermute(got, 'mem', [(giver, core)])]
    ppermute x2, starting transfers between devices: 6.8 us -> 7.67 us  [from_behind(): return lax.ppermute(value, axis, [(i, i + 1) for i in range(count - 1)])]
  transfers between devices with their start and end apart: 7 -> 9, of which waited for: 5 -> 5; matrix products, arithmetic and copies ran while one was open for 0% -> 1% of each run, Pallas kernels for 22% -> 18%
where the time goes in v4:
time: 70.2 us; the launch traced here: 69.7 us
  waiting for transfers between devices  34.3 us (49%)
  starting transfers between devices  19.6 us (28%)
  Pallas kernels  14.4 us (21%)
  between operations  0.75 us (1%)
    ppermute x2, waiting for transfers between devices, fetched(): total = total + lax.ppermute(got, 'mem', [(giver, core)])  19 us
    ppermute x2, waiting for transfers between devices, local(): arrived[k] = lax.ppermute(chunk, 'basin', pairs[k])  11.5 us
    ppermute x2, starting transfers between devices, from_behind(): return lax.ppermute(value, axis, [(i, i + 1) for i in range(count - 1)])  7.67 us
    ppermute x1, starting transfers between devices, local(): lax.ppermute(value, 'basin', pairs[k])  5.11 us
    ppermute x2, waiting for transfers between devices, from_behind(): return lax.ppermute(value, axis, [(i, i + 1) for i in range(count - 1)])  3.77 us
    pallas_call x1, Pallas kernels, source_panels(): pl.pallas_call(body, out_shape=panel_shape(listed, sizes), in_specs=[HBM]...  3.62 us
    pallas_call x1, Pallas kernels, source_chunks(): pl.pallas_call(body, out_shape=[chunk_shape(sizes)] * listed, in_specs=[H...  3.54 us
    ppermute x2, starting transfers between devices, local(): arrived[k] = lax.ppermute(chunk, 'basin', pairs[k])  2.91 us
  transfers between devices with their start and end apart: 9, of which 5 were waited for; matrix products, arithmetic and copies ran while one was open for 1% of the time, Pallas kernels for 18%

profile of v4, /device:TPU:0, one launch (start us, length us, event | category | flops | bytes accessed | tf_op | source)
XLA Modules:
  0.0 69.7 jit_solution(5309027000402664060)
XLA Ops:
  0.0 0.0 copy-start
  0.0 1.1 %pack.2 = f32[1024,128]{1,0:T(8,128)S(1)} custom-call(f32[16,256,128]{2,1,0:T(8,128)} %bitcast.4), custom_call_target="tpu_custom_call" | custom-call | flops 1 | bytes 1 | tf_op jit(solution)/shard_map/pack/pallas_call | solution.py:147
  1.1 5.1 %collective-permute-start.7 = (f32[1024,128]{1,0:T(8,128)S(1)}, f32[1024,128]{1,0:T(8,128)S(1)}, u32[]{:S(2)}, u32[]{:S(2)}) collective-permute-start(f32[1024,128]{1,0:T(8,128)S(1)} %pack.2), channel_id=1, source_target_pairs={{0,12},{4,8},{8,4},{12,0},{1,13},{5,9},{9,5},{13,1},{2,14},{6,10},... | collective-permute-start | bytes 1572872 | tf_op jit(solution)/shard_map/ppermute | solution.py:309
  6.3 0.0 copy-done
  6.3 0.5 slice.3
  7.4 23.0 %conditional.1 = (s32[64,128]{1,0:T(8,128)S(1)}, s32[64,128]{1,0:T(8,128)S(1)}) conditional(s32[]{:T(128)} %bitcast.1, s32[64,128]{1,0:T(8,128)S(1)} %bitcast.8, s32[64,128]{1,0:T(8,128)S(1)} %bitcast.9), branch_computations={%region_0.0_spmd, %region_1.0_spmd} | conditional | flops 16384 | bytes 721072 | solution.py:311
  7.4 0.7 collective-permute-start.2
  8.1 0.7 collective-permute-start
  8.8 0.0 collective-permute-done.2
  8.8 1.3 %collective-permute-start.3 = (s32[64,128]{1,0:T(8,128)S(1)}, s32[64,128]{1,0:T(8,128)S(1)}, u32[]{:S(2)}, u32[]{:S(2)}) collective-permute-start(s32[64,128]{1,0:T(8,128)S(1)} %collective-permute-done.2), channel_id=1, source_target_pairs={{1,0},{3,2},{5,4},{7,6},{9,8},{11,10},{13,12},{15,14},{17,16},{19,... | collective-permute-start | bytes 98312 | tf_op jit(solution)/shard_map/cond/branch_1_fun/ppermute | solution.py:46
  10.1 0.0 collective-permute-done
  10.1 1.3 %collective-permute-start.1 = (s32[64,128]{1,0:T(8,128)S(1)}, s32[64,128]{1,0:T(8,128)S(1)}, u32[]{:S(2)}, u32[]{:S(2)}) collective-permute-start(s32[64,128]{1,0:T(8,128)S(1)} %collective-permute-done), channel_id=1, source_target_pairs={{1,0},{3,2},{5,4},{7,6},{9,8},{11,10},{13,12},{15,14},{17,16},{19,... | collective-permute-start | bytes 98312 | tf_op jit(solution)/shard_map/cond/branch_1_fun/ppermute | solution.py:46
  11.4 8.8 %collective-permute-done.3 = s32[64,128]{1,0:T(8,128)S(1)} collective-permute-done((s32[64,128]{1,0:T(8,128)S(1)}, s32[64,128]{1,0:T(8,128)S(1)}, u32[]{:S(2)}, u32[]{:S(2)}) %collective-permute-start.3) | collective-permute-done | bytes 32800 | tf_op jit(solution)/shard_map/cond/branch_1_fun/ppermute | solution.py:46
  20.3 10.2 %collective-permute-done.1 = s32[64,128]{1,0:T(8,128)S(1)} collective-permute-done((s32[64,128]{1,0:T(8,128)S(1)}, s32[64,128]{1,0:T(8,128)S(1)}, u32[]{:S(2)}, u32[]{:S(2)}) %collective-permute-start.1) | collective-permute-done | bytes 32800 | tf_op jit(solution)/shard_map/cond/branch_1_fun/ppermute | solution.py:46
  30.5 3.6 %source_panels.1 = f32[2,64,128]{2,1,0:T(8,128)S(1)} custom-call(f32[16,256,128]{2,1,0:T(8,128)} %bitcast.5, s32[64,128]{1,0:T(8,128)S(1)} %get-tuple-element.14.rest_0_, s32[64,128]{1,0:T(8,128)S(1)} %get-tuple-element.15.rest_1_), custom_call_target="tpu_custom_call" | custom-call | flops 2 | bytes 2 | tf_op jit(solution)/shard_map/source_panels/pallas_call | solution.py:178
  34.1 3.4 %collective-permute-start.4 = (f32[2,64,128]{2,1,0:T(8,128)S(1)}, f32[2,64,128]{2,1,0:T(8,128)S(1)}, u32[]{:S(2)}, u32[]{:S(2)}) collective-permute-start(f32[2,64,128]{2,1,0:T(8,128)S(1)} %source_panels.1), channel_id=1, source_target_pairs={{0,2},{1,3},{4,6},{5,7},{8,10},{9,11},{12,14},{13,15},{16,18},{17,... | collective-permute-start | bytes 196616 | tf_op jit(solution)/shard_map/ppermute | solution.py:36
  37.5 1.9 %collective-permute-done.4.rest_2_ = f32[2,64,128]{2,1,0:T(8,128)S(1)} collective-permute-done((f32[2,64,128]{2,1,0:T(8,128)S(1)}, f32[2,64,128]{2,1,0:T(8,128)S(1)}, u32[]{:S(2)}, u32[]{:S(2)}) %collective-permute-start.4) | collective-permute-done | bytes 65568 | tf_op jit(solution)/shard_map/ppermute | solution.py:36
  39.4 3.5 %source_chunks.1 = (f32[1024,128]{1,0:T(8,128)S(1)}, f32[1024,128]{1,0:T(8,128)S(1)}) custom-call(f32[16,256,128]{2,1,0:T(8,128)} %bitcast.6, s32[64,128]{1,0:T(8,128)S(1)} %get-tuple-element.14.rest_0_, s32[64,128]{1,0:T(8,128)S(1)} %get-tuple-element.15.rest_1_, f32[2,64,128]{2,1,0:T(8,128)S(1)} %collective-permute-done.4.rest_2_), custom_call_target="tpu_custom_call" | custom-call | flops 2 | bytes 2 | tf_op jit(solution)/shard_map/source_chunks/pallas_call | solution.py:209
  42.9 0.1 collective-permute-start.6
  43.0 2.8 %collective-permute-start.5 = (f32[1024,128]{1,0:T(8,128)S(1)}, f32[1024,128]{1,0:T(8,128)S(1)}, u32[]{:S(2)}, u32[]{:S(2)}) collective-permute-start(f32[1024,128]{1,0:T(8,128)S(1)} %get-tuple-element.16), channel_id=1, source_target_pairs={{0,4},{4,0},{8,12},{12,8},{1,5},{5,1},{9,13},{13,9},{2,6},{6,2},{1... | collective-permute-start | bytes 1572872 | tf_op jit(solution)/shard_map/ppermute | solution.py:320
  45.8 1.1 %pack.3.refs_0_ = f32[1024,128]{1,0:T(8,128)S(1)} custom-call(f32[16,256,128]{2,1,0:T(8,128)} %bitcast.7), custom_call_target="tpu_custom_call" | custom-call | flops 1 | bytes 1 | tf_op jit(solution)/shard_map/pack/pallas_call | solution.py:147
  47.0 0.0 collective-permute-done.7.refs_1_
  47.0 1.2 %arrived_panels.1 = f32[2,64,128]{2,1,0:T(8,128)S(1)} custom-call(f32[1024,128]{1,0:T(8,128)S(1)} %pack.3.refs_0_, f32[1024,128]{1,0:T(8,128)S(1)} %collective-permute-done.7.refs_1_, s32[64,128]{1,0:T(8,128)S(1)} %bitcast.10), custom_call_target="tpu_custom_call" | custom-call | flops 2 | bytes 2 | tf_op jit(solution)/shard_map/arrived_panels/pallas_call | solution.py:235
  48.2 4.3 %collective-permute-start.8 = (f32[2,64,128]{2,1,0:T(8,128)S(1)}, f32[2,64,128]{2,1,0:T(8,128)S(1)}, u32[]{:S(2)}, u32[]{:S(2)}) collective-permute-start(f32[2,64,128]{2,1,0:T(8,128)S(1)} %arrived_panels.1), channel_id=1, source_target_pairs={{0,2},{1,3},{4,6},{5,7},{8,10},{9,11},{12,14},{13,15},{16,18},{17,... | collective-permute-start | bytes 196616 | tf_op jit(solution)/shard_map/ppermute | solution.py:36
  52.5 1.9 %collective-permute-done.8.refs_3_ = f32[2,64,128]{2,1,0:T(8,128)S(1)} collective-permute-done((f32[2,64,128]{2,1,0:T(8,128)S(1)}, f32[2,64,128]{2,1,0:T(8,128)S(1)}, u32[]{:S(2)}, u32[]{:S(2)}) %collective-permute-start.8) | collective-permute-done | bytes 65568 | tf_op jit(solution)/shard_map/ppermute | solution.py:36
  54.3 2.2 %arrived_result.1._ = f32[4096,128]{1,0:T(8,128)} custom-call(f32[1024,128]{1,0:T(8,128)S(1)} %pack.3.refs_0_, f32[1024,128]{1,0:T(8,128)S(1)} %collective-permute-done.7.refs_1_, s32[64,128]{1,0:T(8,128)S(1)} %bitcast.11, f32[2,64,128]{2,1,0:T(8,128)S(1)} %collective-permute-done.8.refs_3_), custom_call_target="tpu_custom_call" | custom-call | flops 2 | bytes 2 | tf_op jit(solution)/shard_map/arrived_result/pallas_call | solution.py:260
  56.5 11.5 %collective-permute-done.6.x_ref = f32[1024,128]{1,0:T(8,128)S(1)} collective-permute-done((f32[1024,128]{1,0:T(8,128)S(1)}, f32[1024,128]{1,0:T(8,128)S(1)}, u32[]{:S(2)}, u32[]{:S(2)}) %collective-permute-start.6) | collective-permute-done | bytes 524320 | tf_op jit(solution)/shard_map/ppermute | solution.py:320
  68.0 0.8 %place_chunk.2._ = f32[4096,128]{1,0:T(8,128)} custom-call(f32[1024,128]{1,0:T(8,128)S(1)} %collective-permute-done.6.x_ref, f32[4096,128]{1,0:T(8,128)} %arrived_result.1._), custom_call_target="tpu_custom_call", output_to_operand_aliasing={{}: (1, {})} | custom-call | flops 1 | bytes 1 | tf_op jit(solution)/shard_map/place_chunk/pallas_call | solution.py:282
  68.8 0.0 collective-permute-done.5.x_ref
  68.8 0.8 %place_chunk.3 = f32[4096,128]{1,0:T(8,128)} custom-call(f32[1024,128]{1,0:T(8,128)S(1)} %collective-permute-done.5.x_ref, f32[4096,128]{1,0:T(8,128)} %place_chunk.2._), custom_call_target="tpu_custom_call", output_to_operand_aliasing={{}: (1, {})} | custom-call | flops 1 | bytes 1 | tf_op jit(solution)/shard_map/place_chunk/pallas_call | solution.py:282
  (2 shorter events, 0.0 us)
Async XLA Ops:
  0.0 6.3 %copy-start = (s32[4,1,2048]{2,1,0:T(1,128)S(1)}, s32[4,1,2048]{2,1,0:T(1,128)}, u32[]{:S(2)}) copy-start(s32[4,1,2048]{2,1,0:T(1,128)} %param.5) | copy-start | bytes 98308
  1.1 45.8 %collective-permute-start.7 = (f32[1024,128]{1,0:T(8,128)S(1)}, f32[1024,128]{1,0:T(8,128)S(1)}, u32[]{:S(2)}, u32[]{:S(2)}) collective-permute-start(f32[1024,128]{1,0:T(8,128)S(1)} %pack.2), channel_id=1, source_target_pairs={{0,12},{4,8},{8,4},{12,0},{1,13},{5,9},{9,5},{13,1},{2,14},{6,10},... | collective-permute-start | bytes 1572872 | tf_op jit(solution)/shard_map/ppermute | solution.py:309
  7.4 1.3 %collective-permute-start.2 = (s32[64,128]{1,0:T(8,128)S(1)}, s32[64,128]{1,0:T(8,128)S(1)}, u32[]{:S(2)}, u32[]{:S(2)}) collective-permute-start(s32[64,128]{1,0:T(8,128)S(1)} %param.1), channel_id=1, source_target_pairs={{5,1},{1,5},{13,9},{9,13},{7,3},{3,7},{15,11},{11,15},{21,17},{17,... | collective-permute-start | bytes 98312 | tf_op jit(solution)/shard_map/cond/branch_1_fun/ppermute | solution.py:43
  8.1 2.0 %collective-permute-start = (s32[64,128]{1,0:T(8,128)S(1)}, s32[64,128]{1,0:T(8,128)S(1)}, u32[]{:S(2)}, u32[]{:S(2)}) collective-permute-start(s32[64,128]{1,0:T(8,128)S(1)} %param.1), channel_id=1, source_target_pairs={{9,1},{13,5},{1,9},{5,13},{11,3},{15,7},{3,11},{7,15},{25,17},{29,... | collective-permute-start | bytes 98312 | tf_op jit(solution)/shard_map/cond/branch_1_fun/ppermute | solution.py:43
  8.8 11.4 %collective-permute-start.3 = (s32[64,128]{1,0:T(8,128)S(1)}, s32[64,128]{1,0:T(8,128)S(1)}, u32[]{:S(2)}, u32[]{:S(2)}) collective-permute-start(s32[64,128]{1,0:T(8,128)S(1)} %collective-permute-done.2), channel_id=1, source_target_pairs={{1,0},{3,2},{5,4},{7,6},{9,8},{11,10},{13,12},{15,14},{17,16},{19,... | collective-permute-start | bytes 98312 | tf_op jit(solution)/shard_map/cond/branch_1_fun/ppermute | solution.py:46
  10.1 20.3 %collective-permute-start.1 = (s32[64,128]{1,0:T(8,128)S(1)}, s32[64,128]{1,0:T(8,128)S(1)}, u32[]{:S(2)}, u32[]{:S(2)}) collective-permute-start(s32[64,128]{1,0:T(8,128)S(1)} %collective-permute-done), channel_id=1, source_target_pairs={{1,0},{3,2},{5,4},{7,6},{9,8},{11,10},{13,12},{15,14},{17,16},{19,... | collective-permute-start | bytes 98312 | tf_op jit(solution)/shard_map/cond/branch_1_fun/ppermute | solution.py:46
  34.1 5.3 %collective-permute-start.4 = (f32[2,64,128]{2,1,0:T(8,128)S(1)}, f32[2,64,128]{2,1,0:T(8,128)S(1)}, u32[]{:S(2)}, u32[]{:S(2)}) collective-permute-start(f32[2,64,128]{2,1,0:T(8,128)S(1)} %source_panels.1), channel_id=1, source_target_pairs={{0,2},{1,3},{4,6},{5,7},{8,10},{9,11},{12,14},{13,15},{16,18},{17,... | collective-permute-start | bytes 196616 | tf_op jit(solution)/shard_map/ppermute | solution.py:36
  42.9 25.1 %collective-permute-start.6 = (f32[1024,128]{1,0:T(8,128)S(1)}, f32[1024,128]{1,0:T(8,128)S(1)}, u32[]{:S(2)}, u32[]{:S(2)}) collective-permute-start(f32[1024,128]{1,0:T(8,128)S(1)} %get-tuple-element.17), channel_id=1, source_target_pairs={{0,8},{4,12},{8,0},{12,4},{1,9},{5,13},{9,1},{13,5},{2,10},{6,14},... | collective-permute-start | bytes 1572872 | tf_op jit(solution)/shard_map/ppermute | solution.py:320
  43.0 25.8 %collective-permute-start.5 = (f32[1024,128]{1,0:T(8,128)S(1)}, f32[1024,128]{1,0:T(8,128)S(1)}, u32[]{:S(2)}, u32[]{:S(2)}) collective-permute-start(f32[1024,128]{1,0:T(8,128)S(1)} %get-tuple-element.16), channel_id=1, source_target_pairs={{0,4},{4,0},{8,12},{12,8},{1,5},{5,1},{9,13},{13,9},{2,6},{6,2},{1... | collective-permute-start | bytes 1572872 | tf_op jit(solution)/shard_map/ppermute | solution.py:320
  48.2 6.2 %collective-permute-start.8 = (f32[2,64,128]{2,1,0:T(8,128)S(1)}, f32[2,64,128]{2,1,0:T(8,128)S(1)}, u32[]{:S(2)}, u32[]{:S(2)}) collective-permute-start(f32[2,64,128]{2,1,0:T(8,128)S(1)} %arrived_panels.1), channel_id=1, source_target_pairs={{0,2},{1,3},{4,6},{5,7},{8,10},{9,11},{12,14},{13,15},{16,18},{17,... | collective-permute-start | bytes 196616 | tf_op jit(solution)/shard_map/ppermute | solution.py:36

commit v5 on v3

v5 whole, which is shorter than its diff:
```python
import jax
import jax.numpy as jnp
from jax import lax
from jax.experimental import pallas as pl
from jax.experimental.pallas import tpu as pltpu
from jax.sharding import PartitionSpec as P

ROWS = 128
SUB = 8
HBM = pl.BlockSpec(memory_space=pltpu.HBM)
VMEM = pl.BlockSpec(memory_space=pltpu.VMEM)


def exchange_pairs(count, k):
    return [(i, i ^ k) for i in range(count)]


def partner(k):
    return lax.axis_index("basin") ^ k


def from_behind(value, axis):
    count = lax.axis_size(axis)
    return lax.ppermute(value, axis, [(i, i + 1) for i in range(count - 1)])


class Piece:
    def __init__(self, k, first, last, sizes):
        self.k, self.first, self.sizes = k, first, sizes
        self.members = last - first
        self.count = self.members * sizes.tiles
        self.rows = self.members * sizes.per_member
        self.groups = self.count // SUB

    def shape(self):
        return jax.ShapeDtypeStruct((self.rows, ROWS), jnp.float32)

    def panel(self):
        return jax.ShapeDtypeStruct((self.count, ROWS), jnp.float32)

    def gather(self, x_ref, buf_ref, sem):
        size = self.sizes.per_member
        block = partner(self.k)
        return [
            pltpu.make_async_copy(
                x_ref.at[self.first + m, pl.ds(block * size, size)],
                buf_ref.at[pl.ds(m * size, size)],
                sem.at[m],
            )
            for m in range(self.members)
        ]

    def place(self, o_ref):
        sizes = self.sizes
        start = (partner(self.k) * sizes.members + self.first) * sizes.per_member
        return o_ref.at[pl.ds(start, self.rows)]


class Sizes:
    def __init__(self, members, tiles, columns, basins):
        self.members, self.tiles, self.columns, self.basins = members, tiles, columns, basins
        self.per_member = tiles * columns

    def result(self):
        rows = self.basins * self.members * self.per_member
        return jax.ShapeDtypeStruct((rows, ROWS), jnp.float32)


def column_masks(d_ref, col, sizes):
    codes = d_ref[pl.ds(col, sizes.tiles, sizes.columns), :]
    codes = jnp.concatenate([codes] * (SUB // sizes.tiles), axis=0)
    lane = lax.broadcasted_iota(jnp.int32, codes.shape, 1)
    north = (codes == 1) & (lane > 0)
    south = (codes == 2) & (lane < ROWS - 1)
    return north, south


def advance(summed, north, south):
    zero = jnp.zeros_like(summed)
    up = pltpu.roll(jnp.where(north, summed, zero), ROWS - 1, 1)
    down = pltpu.roll(jnp.where(south, summed, zero), 1, 1)
    return jnp.where(north | south, zero, summed) + (up + down)


def sweep(x_ref, d_ref, carried, o_ref, sizes):
    for col in range(sizes.columns):
        north, south = column_masks(d_ref, col, sizes)
        for g in range(len(carried)):
            rows = pl.ds(g * SUB * sizes.columns + col, SUB, sizes.columns)
            summed = x_ref[rows, :]
            if carried[g] is not None:
                summed = summed + carried[g]
            if o_ref is not None:
                o_ref[rows, :] = summed
            if o_ref is None or col < sizes.columns - 1:
                carried[g] = advance(summed, north, south)
    return carried


def registers(in_ref, start, piece):
    if in_ref is None:
        return [None] * piece.groups
    return [in_ref[pl.ds(start + g * SUB, SUB), :] for g in range(piece.groups)]


def store_registers(o_ref, start, carried):
    for g, value in enumerate(carried):
        o_ref[pl.ds(start + g * SUB, SUB), :] = value


def start_all(copies):
    for copy in copies:
        copy.start()


def wait_all(copies):
    for copy in copies:
        copy.wait()


def params(rows):
    return pltpu.CompilerParams(vmem_limit_bytes=(rows + 4096) * ROWS * 4)


def cost(rows):
    return pl.CostEstimate(flops=rows * ROWS, bytes_accessed=rows * ROWS, transcendentals=0)


def pack(x, piece):
    def body(x_ref, o_ref, sem):
        copies = piece.gather(x_ref, o_ref, sem)
        start_all(copies)
        wait_all(copies)

    return pl.pallas_call(
        body,
        out_shape=piece.shape(),
        in_specs=[HBM],
        out_specs=VMEM,
        scratch_shapes=[pltpu.SemaphoreType.DMA((piece.members,))],
        compiler_params=params(piece.rows),
        cost_estimate=cost(piece.rows),
        name="pack",
    )(x)


def pack_with_codes(x, piece, codes):
    code_rows = codes.shape[0]

    def body(x_ref, d_ref, o_ref, buf, sem, code_sem):
        copies = piece.gather(x_ref, o_ref, sem)
        start_all(copies)
        copy = pltpu.make_async_copy(d_ref, buf, code_sem)
        copy.start()
        copy.wait()
        o_ref[pl.ds(piece.rows, code_rows), :] = buf[...].astype(jnp.float32)
        wait_all(copies)

    return pl.pallas_call(
        body,
        out_shape=jax.ShapeDtypeStruct((piece.rows + code_rows, ROWS), jnp.float32),
        in_specs=[HBM, HBM],
        out_specs=VMEM,
        scratch_shapes=[
            pltpu.VMEM(codes.shape, codes.dtype),
            pltpu.SemaphoreType.DMA((piece.members,)),
            pltpu.SemaphoreType.DMA,
        ],
        compiler_params=params(piece.rows),
        cost_estimate=cost(piece.rows),
        name="pack_with_codes",
    )(x, codes)


def source_panels(x, pieces, codes, inflow):
    listed, starts = len(pieces), panel_starts(pieces)
    rows = sum(piece.rows for piece in pieces)

    def body(x_ref, *refs):
        d_refs, in_ref = refs[:listed], refs[listed] if inflow is not None else None
        o_ref, bufs, sem = refs[-2 - listed], refs[-1 - listed : -1], refs[-1]
        copies = [piece.gather(x_ref, bufs[i], sem.at[i]) for i, piece in enumerate(pieces)]
        for c in copies:
            start_all(c)
        for i, piece in enumerate(pieces):
            wait_all(copies[i])
            size = piece.sizes.per_member
            codes_ref = d_refs[i].at[pl.ds(codes[i].shape[0] - size, size)]
            carried = registers(in_ref, starts[i], piece)
            store_registers(o_ref, starts[i], sweep(bufs[i], codes_ref, carried, None, piece.sizes))

    return pl.pallas_call(
        body,
        out_shape=jax.ShapeDtypeStruct((starts[-1], ROWS), jnp.float32),
        in_specs=[HBM] + [VMEM] * (listed + (inflow is not None)),
        out_specs=VMEM,
        scratch_shapes=[pltpu.VMEM((piece.rows, ROWS), jnp.float32) for piece in pieces]
        + [pltpu.SemaphoreType.DMA((listed, max(piece.members for piece in pieces)))],
        compiler_params=params(2 * rows),
        cost_estimate=cost(rows),
        name="source_panels",
    )(x, *codes, *([inflow] if inflow is not None else []))


def source_chunk(x, piece, codes, inflow):
    def body(x_ref, d_ref, in_ref, o_ref, buf, sem):
        copies = piece.gather(x_ref, buf, sem)
        start_all(copies)
        wait_all(copies)
        size = piece.sizes.per_member
        codes_ref = d_ref.at[pl.ds(codes.shape[0] - size, size)]
        sweep(buf, codes_ref, registers(in_ref, 0, piece), o_ref, piece.sizes)

    return pl.pallas_call(
        body,
        out_shape=piece.shape(),
        in_specs=[HBM, VMEM, VMEM],
        out_specs=VMEM,
        scratch_shapes=[
            pltpu.VMEM((piece.rows, ROWS), jnp.float32),
            pltpu.SemaphoreType.DMA((piece.members,)),
        ],
        compiler_params=params(3 * piece.rows),
        cost_estimate=cost(piece.rows),
        name="source_chunk",
    )(x, codes, inflow)


def panel_starts(pieces):
    starts = [0]
    for piece in pieces:
        starts.append(starts[-1] + piece.count)
    return starts


def arrived_panels(chunks, pieces, codes, inflow):
    listed, starts = len(pieces), panel_starts(pieces)
    rows = sum(piece.rows for piece in pieces)

    def body(*refs):
        x_refs, d_ref, o_ref = refs[:listed], refs[listed], refs[-1]
        in_ref = refs[listed + 1] if inflow is not None else None
        for x_ref, piece, start in zip(x_refs, pieces, starts):
            carried = registers(in_ref, start, piece)
            store_registers(o_ref, start, sweep(x_ref, d_ref, carried, None, piece.sizes))

    return pl.pallas_call(
        body,
        out_shape=jax.ShapeDtypeStruct((starts[-1], ROWS), jnp.float32),
        in_specs=[VMEM] * (listed + 1 + (inflow is not None)),
        out_specs=VMEM,
        compiler_params=params(2 * rows),
        cost_estimate=cost(rows),
        name="arrived_panels",
    )(*chunks, codes, *([inflow] if inflow is not None else []))


def arrived_result(chunks, pieces, codes, inflows, places, sizes):
    listed, given = len(pieces), len(inflows)
    rows = sum(piece.rows for piece in pieces)

    def body(*refs):
        x_refs, d_ref = refs[:listed], refs[listed]
        in_refs, o_ref = refs[listed + 1 : listed + 1 + given], refs[listed + 1 + given]
        outs, sem = refs[listed + 2 + given : -1], refs[-1]
        copies = []
        for i, piece in enumerate(pieces):
            which, start = places[i]
            sweep(x_refs[i], d_ref, registers(in_refs[which], start, piece), outs[i], sizes)
            copies.append(pltpu.make_async_copy(outs[i], piece.place(o_ref), sem.at[i]))
            copies[i].start()
        wait_all(copies)

    return pl.pallas_call(
        body,
        out_shape=sizes.result(),
        in_specs=[VMEM] * (listed + 1 + given),
        out_specs=HBM,
        scratch_shapes=[pltpu.VMEM((piece.rows, ROWS), jnp.float32) for piece in pieces]
        + [pltpu.SemaphoreType.DMA((listed,))],
        compiler_params=params(2 * rows),
        cost_estimate=cost(rows),
        name="arrived_result",
    )(*chunks, codes, *inflows)


def place_chunk(chunk, piece, result):
    def body(x_ref, _, o_ref, sem):
        copy = pltpu.make_async_copy(x_ref, piece.place(o_ref), sem)
        copy.start()
        copy.wait()

    return pl.pallas_call(
        body,
        out_shape=piece.sizes.result(),
        in_specs=[VMEM, HBM],
        out_specs=HBM,
        scratch_shapes=[pltpu.SemaphoreType.DMA],
        input_output_aliases={1: 0},
        compiler_params=params(piece.rows),
        cost_estimate=cost(piece.rows),
        name="place_chunk",
    )(chunk, result)


def local(runoff, directions):
    basins, chain = lax.axis_size("basin"), lax.axis_size("chain")
    _, members, all_tiles, _, cell_count = runoff.shape
    sizes = Sizes(members, directions.shape[0], cell_count // ROWS, basins)
    x = runoff.reshape(members, all_tiles * sizes.columns, ROWS)
    x = pltpu.with_memory_space_constraint(x, pltpu.HBM)
    codes = directions.reshape(sizes.per_member, ROWS)
    pairs = {k: exchange_pairs(basins, k) for k in range(basins)}

    far = basins - 1
    cut = max(SUB // sizes.tiles, members // 4)
    late = Piece(far, cut, members, sizes)
    early = [Piece(far, 0, cut, sizes)]
    early += [Piece(k, 0, members, sizes) for k in range(far - 1, 0, -1)]

    first = pack_with_codes(x, early[0], pltpu.with_memory_space_constraint(codes, pltpu.HBM))
    arrived = [lax.ppermute(first, "basin", pairs[far])]
    far_codes = arrived[0]
    arrived += [lax.ppermute(pack(x, piece), "basin", pairs[piece.k]) for piece in early[1:]]

    own = Piece(0, 0, members, sizes)
    source, source_codes, inflow = [late, own], [far_codes, codes], None
    for _ in range(chain - 1):
        inflow = from_behind(source_panels(x, source, source_codes, inflow), "chain")
    if inflow is None:
        inflow = jnp.zeros((panel_starts(source)[-1], ROWS), jnp.float32)
    finished = lax.ppermute(source_chunk(x, late, far_codes, inflow), "basin", pairs[far])

    late_inflow = None
    for _ in range(chain - 1):
        late_inflow = from_behind(arrived_panels(arrived, early, codes, late_inflow), "chain")
    if late_inflow is None:
        late_inflow = jnp.zeros((panel_starts(early)[-1], ROWS), jnp.float32)
    places = [(0, late.count)] + [(1, start) for start in panel_starts(early)[:-1]]
    result = arrived_result(
        [pack(x, own)] + arrived, [own] + early, codes, [inflow, late_inflow], places, sizes
    )
    result = place_chunk(finished, late, result)
    return result.reshape(basins * members, sizes.tiles, 1, cell_count)


def solution(mesh):
    return jax.shard_map(
        local,
        mesh=mesh,
        in_specs=(P("mem", "basin", "grp", "chain", None), P(("grp", "basin"), "chain", None)),
        out_specs=P("mem", ("grp", "basin"), "chain", None),
        check_vma=False,
    )
```

time: 56.1 us -> 55.2 us (0.984)
  starting transfers between devices: 25.1 us -> 16.5 us
  waiting for transfers between devices: 15.9 us -> 23.5 us
    ppermute x5 -> x4, starting transfers between devices: 18.4 us -> 9.59 us  [the longest x1 5.11 us: local(): arrived = [lax.ppermute(first, 'basin', pairs[far])]]
    ppermute x5 -> x4, waiting for transfers between devices: 12.2 us -> 20.9 us  [the longest x2 18.8 us: local(): lax.ppermute(pack(x, piece), 'basin', pairs[piece.k])]
    ppermute x2, waiting for transfers between devices: 3.77 us -> 2.61 us  [from_behind(): return lax.ppermute(value, axis, [(i, i + 1) for i in range(count - 1)])]
    pallas_call x8 -> x9, Pallas kernels: 14.4 us -> 14.4 us  [the longest x1 3.56 us: source_panels(): pl.pallas_call(body, out_shape=jax.ShapeDtypeStruct((starts[-1], ROWS), j...]
  transfers between devices with their start and end apart: 7 -> 6, of which waited for: 5 -> 4; matrix products, arithmetic and copies ran while one was open for 0% -> 0% of each run, Pallas kernels for 22% -> 23%
where the time goes in v5:
time: 55.2 us; the launch traced here: 54.5 us
  waiting for transfers between devices  23.5 us (43%)
  starting transfers between devices  16.5 us (30%)
  Pallas kernels  14.4 us (26%)
    ppermute x2, waiting for transfers between devices, local(): lax.ppermute(pack(x, piece), 'basin', pairs[piece.k])  18.8 us
    ppermute x2, starting transfers between devices, from_behind(): return lax.ppermute(value, axis, [(i, i + 1) for i in range(count - 1)])  6.9 us
    ppermute x1, starting transfers between devices, local(): arrived = [lax.ppermute(first, 'basin', pairs[far])]  5.11 us
    ppermute x1, starting transfers between devices, local(): lax.ppermute(source_chunk(x, late, far_codes, inflow), 'basin', pairs[far])  3.77 us
    pallas_call x1, Pallas kernels, source_panels(): pl.pallas_call(body, out_shape=jax.ShapeDtypeStruct((starts[-1], ROWS), j...  3.56 us
    pallas_call x3, Pallas kernels, pack(): pl.pallas_call(body, out_shape=piece.shape(), in_specs=[HBM], out_specs=V...  3.43 us
    ppermute x2, waiting for transfers between devices, from_behind(): return lax.ppermute(value, axis, [(i, i + 1) for i in range(count - 1)])  2.61 us
    pallas_call x1, Pallas kernels, arrived_result(): pl.pallas_call(body, out_shape=sizes.result(), in_specs=[VMEM] * (listed...  2.45 us
  transfers between devices with their start and end apart: 6, of which 4 were waited for; matrix products, arithmetic and copies ran while one was open for 0% of the time, Pallas kernels for 23%

profile of v5, /device:TPU:0, one launch (start us, length us, event | category | flops | bytes accessed | tf_op | source)
XLA Modules:
  0.0 54.5 jit_solution(5468849678265352893)
XLA Ops:
  0.0 0.9 %pack_with_codes.1 = f32[320,128]{1,0:T(8,128)S(1)} custom-call(f32[16,256,128]{2,1,0:T(8,128)} %bitcast.7, s32[64,128]{1,0:T(8,128)} %bitcast.3), custom_call_target="tpu_custom_call" | custom-call | flops 32768 | bytes 32768 | tf_op jit(solution)/shard_map/pack_with_codes/pallas_call | solution.py:159
  0.9 0.0 copy-start
  0.9 5.1 %collective-permute-start = (f32[320,128]{1,0:T(8,128)S(1)}, f32[320,128]{1,0:T(8,128)S(1)}, u32[]{:S(2)}, u32[]{:S(2)}) collective-permute-start(f32[320,128]{1,0:T(8,128)S(1)} %pack_with_codes.1), channel_id=1, source_target_pairs={{0,12},{4,8},{8,4},{12,0},{1,13},{5,9},{9,5},{13,1},{2,14},{6,10},... | collective-permute-start | bytes 491528 | tf_op jit(solution)/shard_map/ppermute | solution.py:322
  6.0 1.1 %pack.4 = f32[1024,128]{1,0:T(8,128)S(1)} custom-call(f32[16,256,128]{2,1,0:T(8,128)} %bitcast.8), custom_call_target="tpu_custom_call" | custom-call | flops 131072 | bytes 131072 | tf_op jit(solution)/shard_map/pack/pallas_call | solution.py:135
  7.1 0.1 collective-permute-start.3
  7.2 1.1 %pack.5 = f32[1024,128]{1,0:T(8,128)S(1)} custom-call(f32[16,256,128]{2,1,0:T(8,128)} %bitcast.9), custom_call_target="tpu_custom_call" | custom-call | flops 131072 | bytes 131072 | tf_op jit(solution)/shard_map/pack/pallas_call | solution.py:135
  8.4 0.6 %collective-permute-start.4 = (f32[1024,128]{1,0:T(8,128)S(1)}, f32[1024,128]{1,0:T(8,128)S(1)}, u32[]{:S(2)}, u32[]{:S(2)}) collective-permute-start(f32[1024,128]{1,0:T(8,128)S(1)} %pack.5), channel_id=1, source_target_pairs={{0,4},{4,0},{8,12},{12,8},{1,5},{5,1},{9,13},{13,9},{2,6},{6,2},{1... | collective-permute-start | bytes 1572872 | tf_op jit(solution)/shard_map/ppermute | solution.py:324
  9.0 2.1 %collective-permute-done.refs_0_.d_ref.refs_1_ = f32[320,128]{1,0:T(8,128)S(1)} collective-permute-done((f32[320,128]{1,0:T(8,128)S(1)}, f32[320,128]{1,0:T(8,128)S(1)}, u32[]{:S(2)}, u32[]{:S(2)}) %collective-permute-start) | collective-permute-done | bytes 163872 | tf_op jit(solution)/shard_map/ppermute | solution.py:322
  11.1 0.0 copy-done
  11.1 3.6 %source_panels.1 = f32[112,128]{1,0:T(8,128)S(1)} custom-call(f32[16,256,128]{2,1,0:T(8,128)} %bitcast.10, f32[320,128]{1,0:T(8,128)S(1)} %collective-permute-done.refs_0_.d_ref.refs_1_, s32[64,128]{1,0:T(8,128)S(1)} %bitcast.4), custom_call_target="tpu_custom_call" | custom-call | flops 229376 | bytes 229376 | tf_op jit(solution)/shard_map/source_panels/pallas_call | solution.py:192
  14.7 3.5 %collective-permute-start.1 = (f32[112,128]{1,0:T(8,128)S(1)}, f32[112,128]{1,0:T(8,128)S(1)}, u32[]{:S(2)}, u32[]{:S(2)}) collective-permute-start(f32[112,128]{1,0:T(8,128)S(1)} %source_panels.1), channel_id=1, source_target_pairs={{0,2},{1,3},{4,6},{5,7},{8,10},{9,11},{12,14},{13,15},{16,18},{17,... | collective-permute-start | bytes 172040 | tf_op jit(solution)/shard_map/ppermute | solution.py:24
  18.2 1.8 %collective-permute-done.1.in_ref.refs_5_ = f32[112,128]{1,0:T(8,128)S(1)} collective-permute-done((f32[112,128]{1,0:T(8,128)S(1)}, f32[112,128]{1,0:T(8,128)S(1)}, u32[]{:S(2)}, u32[]{:S(2)}) %collective-permute-start.1) | collective-permute-done | bytes 57376 | tf_op jit(solution)/shard_map/ppermute | solution.py:24
  20.0 2.2 %source_chunk.1 = f32[768,128]{1,0:T(8,128)S(1)} custom-call(f32[16,256,128]{2,1,0:T(8,128)} %bitcast.11, f32[320,128]{1,0:T(8,128)S(1)} %collective-permute-done.refs_0_.d_ref.refs_1_, f32[112,128]{1,0:T(8,128)S(1)} %collective-permute-done.1.in_ref.refs_5_), custom_call_target="tpu_custom_call" | custom-call | flops 98304 | bytes 98304 | tf_op jit(solution)/shard_map/source_chunk/pallas_call | solution.py:214
  22.2 3.8 %collective-permute-start.2 = (f32[768,128]{1,0:T(8,128)S(1)}, f32[768,128]{1,0:T(8,128)S(1)}, u32[]{:S(2)}, u32[]{:S(2)}) collective-permute-start(f32[768,128]{1,0:T(8,128)S(1)} %source_chunk.1), channel_id=1, source_target_pairs={{0,12},{4,8},{8,4},{12,0},{1,13},{5,9},{9,5},{13,1},{2,14},{6,10},... | collective-permute-start | bytes 1179656 | tf_op jit(solution)/shard_map/ppermute | solution.py:332
  25.9 18.8 %collective-permute-done.3.refs_1_.refs_2_ = f32[1024,128]{1,0:T(8,128)S(1)} collective-permute-done((f32[1024,128]{1,0:T(8,128)S(1)}, f32[1024,128]{1,0:T(8,128)S(1)}, u32[]{:S(2)}, u32[]{:S(2)}) %collective-permute-start.3) | collective-permute-done | bytes 524320 | tf_op jit(solution)/shard_map/ppermute | solution.py:324
  44.7 0.0 collective-permute-done.4.refs_2_.refs_3_
  44.7 1.2 %arrived_panels.1 = f32[144,128]{1,0:T(8,128)S(1)} custom-call(f32[320,128]{1,0:T(8,128)S(1)} %collective-permute-done.refs_0_.d_ref.refs_1_, f32[1024,128]{1,0:T(8,128)S(1)} %collective-permute-done.3.refs_1_.refs_2_, f32[1024,128]{1,0:T(8,128)S(1)} %collective-permute-done.4.refs_2_.refs_3_, s32[64,128]{1,0:T(8,128)S(1)} %bitcast.5), custom_call_target="tpu_custom_call" | custom-call | flops 294912 | bytes 294912 | tf_op jit(solution)/shard_map/arrived_panels/pallas_call | solution.py:247
  45.9 3.4 %collective-permute-start.5 = (f32[144,128]{1,0:T(8,128)S(1)}, f32[144,128]{1,0:T(8,128)S(1)}, u32[]{:S(2)}, u32[]{:S(2)}) collective-permute-start(f32[144,128]{1,0:T(8,128)S(1)} %arrived_panels.1), channel_id=1, source_target_pairs={{0,2},{1,3},{4,6},{5,7},{8,10},{9,11},{12,14},{13,15},{16,18},{17,... | collective-permute-start | bytes 221192 | tf_op jit(solution)/shard_map/ppermute | solution.py:24
  49.3 1.1 %pack.3.refs_0_ = f32[1024,128]{1,0:T(8,128)S(1)} custom-call(f32[16,256,128]{2,1,0:T(8,128)} %bitcast.12), custom_call_target="tpu_custom_call" | custom-call | flops 131072 | bytes 131072 | tf_op jit(solution)/shard_map/pack/pallas_call | solution.py:135
  50.5 0.8 %collective-permute-done.5.refs_6_ = f32[144,128]{1,0:T(8,128)S(1)} collective-permute-done((f32[144,128]{1,0:T(8,128)S(1)}, f32[144,128]{1,0:T(8,128)S(1)}, u32[]{:S(2)}, u32[]{:S(2)}) %collective-permute-start.5) | collective-permute-done | bytes 73760 | tf_op jit(solution)/shard_map/ppermute | solution.py:24
  51.3 2.4 %arrived_result.1._ = f32[4096,128]{1,0:T(8,128)} custom-call(f32[1024,128]{1,0:T(8,128)S(1)} %pack.3.refs_0_, f32[320,128]{1,0:T(8,128)S(1)} %collective-permute-done.refs_0_.d_ref.refs_1_, f32[1024,128]{1,0:T(8,128)S(1)} %collective-permute-done.3.refs_1_.refs_2_, f32[1024,128]{1,0:T(8,128)S(1)} %collective-permute-done.4.refs_2_.refs_3_, ...), custom_call_target="tpu_custom_call" | custom-call | flops 425984 | bytes 425984 | tf_op jit(solution)/shard_map/arrived_result/pallas_call | solution.py:274
  53.7 0.0 collective-permute-done.2.x_ref
  53.7 0.8 %place_chunk.1 = f32[4096,128]{1,0:T(8,128)} custom-call(f32[768,128]{1,0:T(8,128)S(1)} %collective-permute-done.2.x_ref, f32[4096,128]{1,0:T(8,128)} %arrived_result.1._), custom_call_target="tpu_custom_call", output_to_operand_aliasing={{}: (1, {})} | custom-call | flops 98304 | bytes 98304 | tf_op jit(solution)/shard_map/place_chunk/pallas_call | solution.py:293
Async XLA Ops:
  0.9 10.3 %copy-start = (s32[4,1,2048]{2,1,0:T(1,128)S(1)}, s32[4,1,2048]{2,1,0:T(1,128)}, u32[]{:S(2)}) copy-start(s32[4,1,2048]{2,1,0:T(1,128)} %param.3) | copy-start | bytes 98308
  0.9 10.2 %collective-permute-start = (f32[320,128]{1,0:T(8,128)S(1)}, f32[320,128]{1,0:T(8,128)S(1)}, u32[]{:S(2)}, u32[]{:S(2)}) collective-permute-start(f32[320,128]{1,0:T(8,128)S(1)} %pack_with_codes.1), channel_id=1, source_target_pairs={{0,12},{4,8},{8,4},{12,0},{1,13},{5,9},{9,5},{13,1},{2,14},{6,10},... | collective-permute-start | bytes 491528 | tf_op jit(solution)/shard_map/ppermute | solution.py:322
  7.1 37.6 %collective-permute-start.3 = (f32[1024,128]{1,0:T(8,128)S(1)}, f32[1024,128]{1,0:T(8,128)S(1)}, u32[]{:S(2)}, u32[]{:S(2)}) collective-permute-start(f32[1024,128]{1,0:T(8,128)S(1)} %pack.4), channel_id=1, source_target_pairs={{0,8},{4,12},{8,0},{12,4},{1,9},{5,13},{9,1},{13,5},{2,10},{6,14},... | collective-permute-start | bytes 1572872 | tf_op jit(solution)/shard_map/ppermute | solution.py:324
  8.4 36.3 %collective-permute-start.4 = (f32[1024,128]{1,0:T(8,128)S(1)}, f32[1024,128]{1,0:T(8,128)S(1)}, u32[]{:S(2)}, u32[]{:S(2)}) collective-permute-start(f32[1024,128]{1,0:T(8,128)S(1)} %pack.5), channel_id=1, source_target_pairs={{0,4},{4,0},{8,12},{12,8},{1,5},{5,1},{9,13},{13,9},{2,6},{6,2},{1... | collective-permute-start | bytes 1572872 | tf_op jit(solution)/shard_map/ppermute | solution.py:324
  14.7 5.3 %collective-permute-start.1 = (f32[112,128]{1,0:T(8,128)S(1)}, f32[112,128]{1,0:T(8,128)S(1)}, u32[]{:S(2)}, u32[]{:S(2)}) collective-permute-start(f32[112,128]{1,0:T(8,128)S(1)} %source_panels.1), channel_id=1, source_target_pairs={{0,2},{1,3},{4,6},{5,7},{8,10},{9,11},{12,14},{13,15},{16,18},{17,... | collective-permute-start | bytes 172040 | tf_op jit(solution)/shard_map/ppermute | solution.py:24
  22.2 31.6 %collective-permute-start.2 = (f32[768,128]{1,0:T(8,128)S(1)}, f32[768,128]{1,0:T(8,128)S(1)}, u32[]{:S(2)}, u32[]{:S(2)}) collective-permute-start(f32[768,128]{1,0:T(8,128)S(1)} %source_chunk.1), channel_id=1, source_target_pairs={{0,12},{4,8},{8,4},{12,0},{1,13},{5,9},{9,5},{13,1},{2,14},{6,10},... | collective-permute-start | bytes 1179656 | tf_op jit(solution)/shard_map/ppermute | solution.py:332
  45.9 5.4 %collective-permute-start.5 = (f32[144,128]{1,0:T(8,128)S(1)}, f32[144,128]{1,0:T(8,128)S(1)}, u32[]{:S(2)}, u32[]{:S(2)}) collective-permute-start(f32[144,128]{1,0:T(8,128)S(1)} %arrived_panels.1), channel_id=1, source_target_pairs={{0,2},{1,3},{4,6},{5,7},{8,10},{9,11},{12,14},{13,15},{16,18},{17,... | collective-permute-start | bytes 221192 | tf_op jit(solution)/shard_map/ppermute | solution.py:24

commit v6 on v5

--- a/solution.py
+++ b/solution.py
@@ -21,7 +21,7 @@
 
 def from_behind(value, axis):
     count = lax.axis_size(axis)
-    return lax.ppermute(value, axis, [(i, i + 1) for i in range(count - 1)])
+    return lax.ppermute(value, axis, [(i, (i + 1) % count) for i in range(count)])
 
 
 class Piece:
@@ -40,15 +40,8 @@
 
     def gather(self, x_ref, buf_ref, sem):
         size = self.sizes.per_member
-        block = partner(self.k)
-        return [
-            pltpu.make_async_copy(
-                x_ref.at[self.first + m, pl.ds(block * size, size)],
-                buf_ref.at[pl.ds(m * size, size)],
-                sem.at[m],
-            )
-            for m in range(self.members)
-        ]
+        tiles = x_ref.at[pl.ds(self.first, self.members), pl.ds(partner(self.k) * size, size)]
+        return [pltpu.make_async_copy(tiles, buf_ref.at[pl.ds(0, self.rows)].reshape(self.members, size, ROWS), sem)]
 
     def place(self, o_ref):
         sizes = self.sizes
@@ -100,7 +93,9 @@
 def registers(in_ref, start, piece):
     if in_ref is None:
         return [None] * piece.groups
-    return [in_ref[pl.ds(start + g * SUB, SUB), :] for g in range(piece.groups)]
+    upstream = lax.axis_index("chain") > 0
+    values = [in_ref[pl.ds(start + g * SUB, SUB), :] for g in range(piece.groups)]
+    return [jnp.where(upstream, value, jnp.zeros_like(value)) for value in values]
 
 
 def store_registers(o_ref, start, carried):
@@ -137,7 +132,7 @@
         out_shape=piece.shape(),
         in_specs=[HBM],
         out_specs=VMEM,
-        scratch_shapes=[pltpu.SemaphoreType.DMA((piece.members,))],
+        scratch_shapes=[pltpu.SemaphoreType.DMA],
         compiler_params=params(piece.rows),
         cost_estimate=cost(piece.rows),
         name="pack",
@@ -163,7 +158,7 @@
         out_specs=VMEM,
         scratch_shapes=[
             pltpu.VMEM(codes.shape, codes.dtype),
-            pltpu.SemaphoreType.DMA((piece.members,)),
+            pltpu.SemaphoreType.DMA,
             pltpu.SemaphoreType.DMA,
         ],
         compiler_params=params(piece.rows),
@@ -195,7 +190,7 @@
         in_specs=[HBM] + [VMEM] * (listed + (inflow is not None)),
         out_specs=VMEM,
         scratch_shapes=[pltpu.VMEM((piece.rows, ROWS), jnp.float32) for piece in pieces]
-        + [pltpu.SemaphoreType.DMA((listed, max(piece.members for piece in pieces)))],
+        + [pltpu.SemaphoreType.DMA((listed,))],
         compiler_params=params(2 * rows),
         cost_estimate=cost(rows),
         name="source_panels",
@@ -218,7 +213,7 @@
         out_specs=VMEM,
         scratch_shapes=[
             pltpu.VMEM((piece.rows, ROWS), jnp.float32),
-            pltpu.SemaphoreType.DMA((piece.members,)),
+            pltpu.SemaphoreType.DMA,
         ],
         compiler_params=params(3 * piece.rows),
         cost_estimate=cost(piece.rows),
@@ -255,33 +250,55 @@
     )(*chunks, codes, *([inflow] if inflow is not None else []))
 
 
-def arrived_result(chunks, pieces, codes, inflows, places, sizes):
-    listed, given = len(pieces), len(inflows)
+def own_result(x, piece, codes, inflow, start):
+    def body(x_ref, d_ref, in_ref, o_ref, buf, out, sem, out_sem):
+        copies = piece.gather(x_ref, buf, sem)
+        start_all(copies)
+        wait_all(copies)
+        sweep(buf, d_ref, registers(in_ref, start, piece), out, piece.sizes)
+        copy = pltpu.make_async_copy(out, piece.place(o_ref), out_sem)
+        copy.start()
+        copy.wait()
+
+    return pl.pallas_call(
+        body,
+        out_shape=piece.sizes.result(),
+        in_specs=[HBM, VMEM, VMEM],
+        out_specs=HBM,
+        scratch_shapes=[pltpu.VMEM((piece.rows, ROWS), jnp.float32)] * 2
+        + [pltpu.SemaphoreType.DMA] * 2,
+        compiler_params=params(2 * piece.rows),
+        cost_estimate=cost(piece.rows),
+        name="own_result",
+    )(x, codes, inflow)
+
+
+def arrived_result(chunks, pieces, codes, inflow, result):
+    listed, starts = len(pieces), panel_starts(pieces)
     rows = sum(piece.rows for piece in pieces)
 
     def body(*refs):
-        x_refs, d_ref = refs[:listed], refs[listed]
-        in_refs, o_ref = refs[listed + 1 : listed + 1 + given], refs[listed + 1 + given]
-        outs, sem = refs[listed + 2 + given : -1], refs[-1]
+        x_refs, d_ref, in_ref, o_ref = refs[:listed], refs[listed], refs[listed + 1], refs[listed + 3]
+        outs, sem = refs[listed + 4 : -1], refs[-1]
         copies = []
         for i, piece in enumerate(pieces):
-            which, start = places[i]
-            sweep(x_refs[i], d_ref, registers(in_refs[which], start, piece), outs[i], sizes)
+            sweep(x_refs[i], d_ref, registers(in_ref, starts[i], piece), outs[i], piece.sizes)
             copies.append(pltpu.make_async_copy(outs[i], piece.place(o_ref), sem.at[i]))
             copies[i].start()
         wait_all(copies)
 
     return pl.pallas_call(
         body,
-        out_shape=sizes.result(),
-        in_specs=[VMEM] * (listed + 1 + given),
+        out_shape=pieces[0].sizes.result(),
+        in_specs=[VMEM] * (listed + 2) + [HBM],
         out_specs=HBM,
         scratch_shapes=[pltpu.VMEM((piece.rows, ROWS), jnp.float32) for piece in pieces]
         + [pltpu.SemaphoreType.DMA((listed,))],
+        input_output_aliases={listed + 2: 0},
         compiler_params=params(2 * rows),
         cost_estimate=cost(rows),
         name="arrived_result",
-    )(*chunks, codes, *inflows)
+    )(*chunks, codes, inflow, result)
 
 
 def place_chunk(chunk, piece, result):
@@ -331,15 +348,14 @@
         inflow = jnp.zeros((panel_starts(source)[-1], ROWS), jnp.float32)
     finished = lax.ppermute(source_chunk(x, late, far_codes, inflow), "basin", pairs[far])
 
+    result = own_result(x, own, codes, inflow, late.count)
+    result, arrived = lax.optimization_barrier((result, arrived))
     late_inflow = None
     for _ in range(chain - 1):
         late_inflow = from_behind(arrived_panels(arrived, early, codes, late_inflow), "chain")
     if late_inflow is None:
         late_inflow = jnp.zeros((panel_starts(early)[-1], ROWS), jnp.float32)
-    places = [(0, late.count)] + [(1, start) for start in panel_starts(early)[:-1]]
-    result = arrived_result(
-        [pack(x, own)] + arrived, [own] + early, codes, [inflow, late_inflow], places, sizes
-    )
+    result = arrived_result(arrived, early, codes, late_inflow, result)
     result = place_chunk(finished, late, result)
     return result.reshape(basins * members, sizes.tiles, 1, cell_count)
 

time: 55.2 us -> 53.7 us (0.973)
  starting transfers between devices: 16.5 us -> 13 us
  Pallas kernels: 14.4 us -> 15.6 us
  waiting for transfers between devices: 23.5 us -> 24.7 us
    ppermute x2, starting transfers between devices: 6.9 us -> 3.31 us  [from_behind(): lax.ppermute(value, axis, [(i, (i + 1) % count) for i in range(count)])]
    ppermute x2, waiting for transfers between devices: 2.61 us -> 5.35 us  [from_behind(): lax.ppermute(value, axis, [(i, (i + 1) % count) for i in range(count)])]
    pallas_call x1 -> x2, Pallas kernels: 2.45 us -> 5.14 us  [the longest x1 2.97 us: own_result(): pl.pallas_call(body, out_shape=piece.sizes.result(), in_specs=[HBM, VMEM,...]
    ppermute x2, waiting for transfers between devices: 18.8 us -> 17 us  [local(): lax.ppermute(pack(x, piece), 'basin', pairs[piece.k])]
    pallas_call x3 -> x2, Pallas kernels: 3.43 us -> 2.11 us  [pack(): pl.pallas_call(body, out_shape=piece.shape(), in_specs=[HBM], out_specs=V...]
  transfers between devices with their start and end apart: 6 -> 6, of which waited for: 4 -> 4; matrix products, arithmetic and copies ran while one was open for 0% -> 0% of each run, Pallas kernels for 23% -> 26%
where the time goes in v6:
time: 53.7 us; the launch traced here: 53.4 us
  waiting for transfers between devices  24.7 us (46%)
  Pallas kernels  15.6 us (29%)
  starting transfers between devices  13 us (24%)
    ppermute x2, waiting for transfers between devices, local(): lax.ppermute(pack(x, piece), 'basin', pairs[piece.k])  17 us
    ppermute x2, waiting for transfers between devices, from_behind(): lax.ppermute(value, axis, [(i, (i + 1) % count) for i in range(count)])  5.35 us
    ppermute x1, starting transfers between devices, local(): arrived = [lax.ppermute(first, 'basin', pairs[far])]  5.11 us
    ppermute x1, starting transfers between devices, local(): lax.ppermute(source_chunk(x, late, far_codes, inflow), 'basin', pairs[far])  3.88 us
    pallas_call x1, Pallas kernels, source_panels(): pl.pallas_call(body, out_shape=jax.ShapeDtypeStruct((starts[-1], ROWS), j...  3.33 us
    ppermute x2, starting transfers between devices, from_behind(): lax.ppermute(value, axis, [(i, (i + 1) % count) for i in range(count)])  3.31 us
    pallas_call x1, Pallas kernels, own_result(): pl.pallas_call(body, out_shape=piece.sizes.result(), in_specs=[HBM, VMEM,...  2.97 us
    ppermute x1, waiting for transfers between devices, local(): arrived = [lax.ppermute(first, 'basin', pairs[far])]  2.3 us
  transfers between devices with their start and end apart: 6, of which 4 were waited for; matrix products, arithmetic and copies ran while one was open for 0% of the time, Pallas kernels for 26%

profile of v6, /device:TPU:0, one launch (start us, length us, event | category | flops | bytes accessed | tf_op | source)
XLA Modules:
  0.0 53.4 jit_solution(7594717653501502061)
XLA Ops:
  0.0 0.9 %pack_with_codes.1 = f32[320,128]{1,0:T(8,128)S(1)} custom-call(f32[16,256,128]{2,1,0:T(8,128)} %bitcast.8, s32[64,128]{1,0:T(8,128)} %bitcast.3), custom_call_target="tpu_custom_call" | custom-call | flops 32768 | bytes 32768 | tf_op jit(solution)/shard_map/pack_with_codes/pallas_call | solution.py:154
  0.9 0.0 copy-start
  1.0 5.1 %collective-permute-start = (f32[320,128]{1,0:T(8,128)S(1)}, f32[320,128]{1,0:T(8,128)S(1)}, u32[]{:S(2)}, u32[]{:S(2)}) collective-permute-start(f32[320,128]{1,0:T(8,128)S(1)} %pack_with_codes.1), channel_id=1, source_target_pairs={{0,12},{4,8},{8,4},{12,0},{1,13},{5,9},{9,5},{13,1},{2,14},{6,10},... | collective-permute-start | bytes 491528 | tf_op jit(solution)/shard_map/ppermute | solution.py:339
  6.1 1.0 %pack.2 = f32[1024,128]{1,0:T(8,128)S(1)} custom-call(f32[16,256,128]{2,1,0:T(8,128)} %bitcast.9), custom_call_target="tpu_custom_call" | custom-call | flops 131072 | bytes 131072 | tf_op jit(solution)/shard_map/pack/pallas_call | solution.py:130
  7.1 0.1 collective-permute-start.3
  7.2 1.1 %pack.3 = f32[1024,128]{1,0:T(8,128)S(1)} custom-call(f32[16,256,128]{2,1,0:T(8,128)} %bitcast.10), custom_call_target="tpu_custom_call" | custom-call | flops 131072 | bytes 131072 | tf_op jit(solution)/shard_map/pack/pallas_call | solution.py:130
  8.3 0.6 %collective-permute-start.4 = (f32[1024,128]{1,0:T(8,128)S(1)}, f32[1024,128]{1,0:T(8,128)S(1)}, u32[]{:S(2)}, u32[]{:S(2)}) collective-permute-start(f32[1024,128]{1,0:T(8,128)S(1)} %pack.3), channel_id=1, source_target_pairs={{0,4},{4,0},{8,12},{12,8},{1,5},{5,1},{9,13},{13,9},{2,6},{6,2},{1... | collective-permute-start | bytes 1572872 | tf_op jit(solution)/shard_map/ppermute | solution.py:341
  8.9 2.3 %collective-permute-done.refs_0_.d_ref = f32[320,128]{1,0:T(8,128)S(1)} collective-permute-done((f32[320,128]{1,0:T(8,128)S(1)}, f32[320,128]{1,0:T(8,128)S(1)}, u32[]{:S(2)}, u32[]{:S(2)}) %collective-permute-start) | collective-permute-done | bytes 163872 | tf_op jit(solution)/shard_map/ppermute | solution.py:339
  11.2 0.0 copy-done
  11.2 3.3 %source_panels.1 = f32[112,128]{1,0:T(8,128)S(1)} custom-call(f32[16,256,128]{2,1,0:T(8,128)} %bitcast.11, f32[320,128]{1,0:T(8,128)S(1)} %collective-permute-done.refs_0_.d_ref, s32[64,128]{1,0:T(8,128)S(1)} %bitcast.4), custom_call_target="tpu_custom_call" | custom-call | flops 229376 | bytes 229376 | tf_op jit(solution)/shard_map/source_panels/pallas_call | solution.py:187
  14.5 1.8 %collective-permute-start.1 = (f32[112,128]{1,0:T(8,128)S(1)}, f32[112,128]{1,0:T(8,128)S(1)}, u32[]{:S(2)}, u32[]{:S(2)}) collective-permute-start(f32[112,128]{1,0:T(8,128)S(1)} %source_panels.1), channel_id=1, source_target_pairs={{0,2},{2,0},{1,3},{3,1},{4,6},{6,4},{5,7},{7,5},{8,10},{10,8},{9,1... | collective-permute-start | bytes 172040 | tf_op jit(solution)/shard_map/ppermute | solution.py:24
  16.3 2.5 %collective-permute-done.1.in_ref = f32[112,128]{1,0:T(8,128)S(1)} collective-permute-done((f32[112,128]{1,0:T(8,128)S(1)}, f32[112,128]{1,0:T(8,128)S(1)}, u32[]{:S(2)}, u32[]{:S(2)}) %collective-permute-start.1) | collective-permute-done | bytes 57376 | tf_op jit(solution)/shard_map/ppermute | solution.py:24
  18.8 2.1 %source_chunk.1 = f32[768,128]{1,0:T(8,128)S(1)} custom-call(f32[16,256,128]{2,1,0:T(8,128)} %bitcast.12, f32[320,128]{1,0:T(8,128)S(1)} %collective-permute-done.refs_0_.d_ref, f32[112,128]{1,0:T(8,128)S(1)} %collective-permute-done.1.in_ref), custom_call_target="tpu_custom_call" | custom-call | flops 98304 | bytes 98304 | tf_op jit(solution)/shard_map/source_chunk/pallas_call | solution.py:209
  20.9 3.9 %collective-permute-start.2 = (f32[768,128]{1,0:T(8,128)S(1)}, f32[768,128]{1,0:T(8,128)S(1)}, u32[]{:S(2)}, u32[]{:S(2)}) collective-permute-start(f32[768,128]{1,0:T(8,128)S(1)} %source_chunk.1), channel_id=1, source_target_pairs={{0,12},{4,8},{8,4},{12,0},{1,13},{5,9},{9,5},{13,1},{2,14},{6,10},... | collective-permute-start | bytes 1179656 | tf_op jit(solution)/shard_map/ppermute | solution.py:349
  24.8 3.0 %own_result.1.refs_5_ = f32[4096,128]{1,0:T(8,128)} custom-call(f32[16,256,128]{2,1,0:T(8,128)} %bitcast.13, s32[64,128]{1,0:T(8,128)S(1)} %bitcast.5, f32[112,128]{1,0:T(8,128)S(1)} %collective-permute-done.1.in_ref), custom_call_target="tpu_custom_call" | custom-call | flops 131072 | bytes 131072 | tf_op jit(solution)/shard_map/own_result/pallas_call | solution.py:263
  27.8 17.0 %collective-permute-done.3.refs_1_ = f32[1024,128]{1,0:T(8,128)S(1)} collective-permute-done((f32[1024,128]{1,0:T(8,128)S(1)}, f32[1024,128]{1,0:T(8,128)S(1)}, u32[]{:S(2)}, u32[]{:S(2)}) %collective-permute-start.3) | collective-permute-done | bytes 524320 | tf_op jit(solution)/shard_map/ppermute | solution.py:341
  44.8 0.0 collective-permute-done.4.refs_2_
  44.8 1.2 %arrived_panels.1 = f32[144,128]{1,0:T(8,128)S(1)} custom-call(f32[320,128]{1,0:T(8,128)S(1)} %collective-permute-done.refs_0_.d_ref, f32[1024,128]{1,0:T(8,128)S(1)} %collective-permute-done.3.refs_1_, f32[1024,128]{1,0:T(8,128)S(1)} %collective-permute-done.4.refs_2_, s32[64,128]{1,0:T(8,128)S(1)} %bitcast.6), custom_call_target="tpu_custom_call" | custom-call | flops 294912 | bytes 294912 | tf_op jit(solution)/shard_map/arrived_panels/pallas_call | solution.py:242
  46.0 1.6 %collective-permute-start.5 = (f32[144,128]{1,0:T(8,128)S(1)}, f32[144,128]{1,0:T(8,128)S(1)}, u32[]{:S(2)}, u32[]{:S(2)}) collective-permute-start(f32[144,128]{1,0:T(8,128)S(1)} %arrived_panels.1), channel_id=1, source_target_pairs={{0,2},{2,0},{1,3},{3,1},{4,6},{6,4},{5,7},{7,5},{8,10},{10,8},{9,1... | collective-permute-start | bytes 221192 | tf_op jit(solution)/shard_map/ppermute | solution.py:24
  47.5 2.9 %collective-permute-done.5.refs_4_ = f32[144,128]{1,0:T(8,128)S(1)} collective-permute-done((f32[144,128]{1,0:T(8,128)S(1)}, f32[144,128]{1,0:T(8,128)S(1)}, u32[]{:S(2)}, u32[]{:S(2)}) %collective-permute-start.5) | collective-permute-done | bytes 73760 | tf_op jit(solution)/shard_map/ppermute | solution.py:24
  50.4 2.2 %arrived_result.1._ = f32[4096,128]{1,0:T(8,128)} custom-call(f32[320,128]{1,0:T(8,128)S(1)} %collective-permute-done.refs_0_.d_ref, f32[1024,128]{1,0:T(8,128)S(1)} %collective-permute-done.3.refs_1_, f32[1024,128]{1,0:T(8,128)S(1)} %collective-permute-done.4.refs_2_, s32[64,128]{1,0:T(8,128)S(1)} %bitcast.7, ...), custom_call_target="tpu_custom_call", output_to_operand_aliasing={{}: (5, {})} | custom-call | flops 294912 | bytes 294912 | tf_op jit(solution)/shard_map/arrived_result/pallas_call | solution.py:290
  52.6 0.0 collective-permute-done.2.x_ref
  52.6 0.8 %place_chunk.1 = f32[4096,128]{1,0:T(8,128)} custom-call(f32[768,128]{1,0:T(8,128)S(1)} %collective-permute-done.2.x_ref, f32[4096,128]{1,0:T(8,128)} %arrived_result.1._), custom_call_target="tpu_custom_call", output_to_operand_aliasing={{}: (1, {})} | custom-call | flops 98304 | bytes 98304 | tf_op jit(solution)/shard_map/place_chunk/pallas_call | solution.py:310
Async XLA Ops:
  0.9 10.3 %copy-start = (s32[4,1,2048]{2,1,0:T(1,128)S(1)}, s32[4,1,2048]{2,1,0:T(1,128)}, u32[]{:S(2)}) copy-start(s32[4,1,2048]{2,1,0:T(1,128)} %param.3) | copy-start | bytes 98308
  1.0 10.2 %collective-permute-start = (f32[320,128]{1,0:T(8,128)S(1)}, f32[320,128]{1,0:T(8,128)S(1)}, u32[]{:S(2)}, u32[]{:S(2)}) collective-permute-start(f32[320,128]{1,0:T(8,128)S(1)} %pack_with_codes.1), channel_id=1, source_target_pairs={{0,12},{4,8},{8,4},{12,0},{1,13},{5,9},{9,5},{13,1},{2,14},{6,10},... | collective-permute-start | bytes 491528 | tf_op jit(solution)/shard_map/ppermute | solution.py:339
  7.1 37.7 %collective-permute-start.3 = (f32[1024,128]{1,0:T(8,128)S(1)}, f32[1024,128]{1,0:T(8,128)S(1)}, u32[]{:S(2)}, u32[]{:S(2)}) collective-permute-start(f32[1024,128]{1,0:T(8,128)S(1)} %pack.2), channel_id=1, source_target_pairs={{0,8},{4,12},{8,0},{12,4},{1,9},{5,13},{9,1},{13,5},{2,10},{6,14},... | collective-permute-start | bytes 1572872 | tf_op jit(solution)/shard_map/ppermute | solution.py:341
  8.3 36.5 %collective-permute-start.4 = (f32[1024,128]{1,0:T(8,128)S(1)}, f32[1024,128]{1,0:T(8,128)S(1)}, u32[]{:S(2)}, u32[]{:S(2)}) collective-permute-start(f32[1024,128]{1,0:T(8,128)S(1)} %pack.3), channel_id=1, source_target_pairs={{0,4},{4,0},{8,12},{12,8},{1,5},{5,1},{9,13},{13,9},{2,6},{6,2},{1... | collective-permute-start | bytes 1572872 | tf_op jit(solution)/shard_map/ppermute | solution.py:341
  14.5 4.2 %collective-permute-start.1 = (f32[112,128]{1,0:T(8,128)S(1)}, f32[112,128]{1,0:T(8,128)S(1)}, u32[]{:S(2)}, u32[]{:S(2)}) collective-permute-start(f32[112,128]{1,0:T(8,128)S(1)} %source_panels.1), channel_id=1, source_target_pairs={{0,2},{2,0},{1,3},{3,1},{4,6},{6,4},{5,7},{7,5},{8,10},{10,8},{9,1... | collective-permute-start | bytes 172040 | tf_op jit(solution)/shard_map/ppermute | solution.py:24
  20.9 31.7 %collective-permute-start.2 = (f32[768,128]{1,0:T(8,128)S(1)}, f32[768,128]{1,0:T(8,128)S(1)}, u32[]{:S(2)}, u32[]{:S(2)}) collective-permute-start(f32[768,128]{1,0:T(8,128)S(1)} %source_chunk.1), channel_id=1, source_target_pairs={{0,12},{4,8},{8,4},{12,0},{1,13},{5,9},{9,5},{13,1},{2,14},{6,10},... | collective-permute-start | bytes 1179656 | tf_op jit(solution)/shard_map/ppermute | solution.py:349
  46.0 4.4 %collective-permute-start.5 = (f32[144,128]{1,0:T(8,128)S(1)}, f32[144,128]{1,0:T(8,128)S(1)}, u32[]{:S(2)}, u32[]{:S(2)}) collective-permute-start(f32[144,128]{1,0:T(8,128)S(1)} %arrived_panels.1), channel_id=1, source_target_pairs={{0,2},{2,0},{1,3},{3,1},{4,6},{6,4},{5,7},{7,5},{8,10},{10,8},{9,1... | collective-permute-start | bytes 221192 | tf_op jit(solution)/shard_map/ppermute | solution.py:24

commit v7 on v6

--- a/solution.py
+++ b/solution.py
@@ -330,15 +330,17 @@
     pairs = {k: exchange_pairs(basins, k) for k in range(basins)}
 
     far = basins - 1
-    cut = max(SUB // sizes.tiles, members // 4)
+    cut = SUB // sizes.tiles
     late = Piece(far, cut, members, sizes)
-    early = [Piece(far, 0, cut, sizes)]
-    early += [Piece(k, 0, members, sizes) for k in range(far - 1, 0, -1)]
-
-    first = pack_with_codes(x, early[0], pltpu.with_memory_space_constraint(codes, pltpu.HBM))
-    arrived = [lax.ppermute(first, "basin", pairs[far])]
-    far_codes = arrived[0]
-    arrived += [lax.ppermute(pack(x, piece), "basin", pairs[piece.k]) for piece in early[1:]]
+    head = Piece(far, 0, cut, sizes)
+    near = [Piece(k, 0, members, sizes) for k in range(1, basins // 2)]
+    across = [Piece(k, 0, members, sizes) for k in range(basins // 2, far)]
+
+    first = pack_with_codes(x, head, pltpu.with_memory_space_constraint(codes, pltpu.HBM))
+    far_codes = lax.ppermute(first, "basin", pairs[far])
+    arrived = {head: far_codes}
+    for piece in across + near:
+        arrived[piece] = lax.ppermute(pack(x, piece), "basin", pairs[piece.k])
 
     own = Piece(0, 0, members, sizes)
     source, source_codes, inflow = [late, own], [far_codes, codes], None
@@ -349,13 +351,15 @@
     finished = lax.ppermute(source_chunk(x, late, far_codes, inflow), "basin", pairs[far])
 
     result = own_result(x, own, codes, inflow, late.count)
-    result, arrived = lax.optimization_barrier((result, arrived))
-    late_inflow = None
-    for _ in range(chain - 1):
-        late_inflow = from_behind(arrived_panels(arrived, early, codes, late_inflow), "chain")
-    if late_inflow is None:
-        late_inflow = jnp.zeros((panel_starts(early)[-1], ROWS), jnp.float32)
-    result = arrived_result(arrived, early, codes, late_inflow, result)
+    for group in ([head] + near, across):
+        chunks = [arrived[piece] for piece in group]
+        result, chunks = lax.optimization_barrier((result, chunks))
+        inflow = None
+        for _ in range(chain - 1):
+            inflow = from_behind(arrived_panels(chunks, group, codes, inflow), "chain")
+        if inflow is None:
+            inflow = jnp.zeros((panel_starts(group)[-1], ROWS), jnp.float32)
+        result = arrived_result(chunks, group, codes, inflow, result)
     result = place_chunk(finished, late, result)
     return result.reshape(basins * members, sizes.tiles, 1, cell_count)
 

time: 53.7 us -> 53.3 us (level)
  waiting for transfers between devices: 24.7 us -> 19.9 us
  Pallas kernels: 15.6 us -> 18.5 us
  starting transfers between devices: 13 us -> 14.5 us
    ppermute x3, waiting for transfers between devices: 19.3 us -> 12.3 us  [the longest x2 11.6 us: local(): arrived[piece] = lax.ppermute(pack(x, piece), 'basin', pairs[piece.k])]
    ppermute x2 -> x3, waiting for transfers between devices: 5.35 us -> 7.57 us  [from_behind(): lax.ppermute(value, axis, [(i, (i + 1) % count) for i in range(count)])]
    pallas_call x1 -> x2, Pallas kernels: 2.17 us -> 3.88 us  [arrived_result(): pl.pallas_call(body, out_shape=pieces[0].sizes.result(), in_specs=[VMEM]...]
    ppermute x2 -> x3, starting transfers between devices: 3.31 us -> 4.72 us  [from_behind(): lax.ppermute(value, axis, [(i, (i + 1) % count) for i in range(count)])]
    pallas_call x1 -> x2, Pallas kernels: 1.18 us -> 2.32 us  [arrived_panels(): pl.pallas_call(body, out_shape=jax.ShapeDtypeStruct((starts[-1], ROWS), j...]
  transfers between devices with their start and end apart: 6 -> 7, of which waited for: 4 -> 6; matrix products, arithmetic and copies ran while one was open for 0% -> 0% of each run, Pallas kernels for 26% -> 32%
where the time goes in v7:
time: 53.3 us; the launch traced here: 53 us
  waiting for transfers between devices  19.9 us (37%)
  Pallas kernels  18.5 us (35%)
  starting transfers between devices  14.5 us (27%)
    ppermute x2, waiting for transfers between devices, local(): arrived[piece] = lax.ppermute(pack(x, piece), 'basin', pairs[piece.k])  11.6 us
    ppermute x3, waiting for transfers between devices, from_behind(): lax.ppermute(value, axis, [(i, (i + 1) % count) for i in range(count)])  7.57 us
    ppermute x1, starting transfers between devices, local(): far_codes = lax.ppermute(first, 'basin', pairs[far])  5.11 us
    ppermute x3, starting transfers between devices, from_behind(): lax.ppermute(value, axis, [(i, (i + 1) % count) for i in range(count)])  4.72 us
    ppermute x1, starting transfers between devices, local(): lax.ppermute(source_chunk(x, late, far_codes, inflow), 'basin', pairs[far])  3.99 us
    pallas_call x2, Pallas kernels, arrived_result(): pl.pallas_call(body, out_shape=pieces[0].sizes.result(), in_specs=[VMEM]...  3.88 us
    pallas_call x1, Pallas kernels, source_panels(): pl.pallas_call(body, out_shape=jax.ShapeDtypeStruct((starts[-1], ROWS), j...  3.36 us
    pallas_call x1, Pallas kernels, own_result(): pl.pallas_call(body, out_shape=piece.sizes.result(), in_specs=[HBM, VMEM,...  2.97 us
  transfers between devices with their start and end apart: 7, of which 6 were waited for; matrix products, arithmetic and copies ran while one was open for 0% of the time, Pallas kernels for 32%

profile of v7, /device:TPU:0, one launch (start us, length us, event | category | flops | bytes accessed | tf_op | source)
XLA Modules:
  0.0 53.0 jit_solution(14220653126095774719)
XLA Ops:
  0.0 0.9 %pack_with_codes.1 = f32[192,128]{1,0:T(8,128)S(1)} custom-call(f32[16,256,128]{2,1,0:T(8,128)} %bitcast.10, s32[64,128]{1,0:T(8,128)} %bitcast.3), custom_call_target="tpu_custom_call" | custom-call | flops 16384 | bytes 16384 | tf_op jit(solution)/shard_map/pack_with_codes/pallas_call | solution.py:154
  0.9 0.0 copy-start
  0.9 5.1 %collective-permute-start = (f32[192,128]{1,0:T(8,128)S(1)}, f32[192,128]{1,0:T(8,128)S(1)}, u32[]{:S(2)}, u32[]{:S(2)}) collective-permute-start(f32[192,128]{1,0:T(8,128)S(1)} %pack_with_codes.1), channel_id=1, source_target_pairs={{0,12},{4,8},{8,4},{12,0},{1,13},{5,9},{9,5},{13,1},{2,14},{6,10},... | collective-permute-start | bytes 294920 | tf_op jit(solution)/shard_map/ppermute | solution.py:340
  6.0 1.0 %pack.2 = f32[1024,128]{1,0:T(8,128)S(1)} custom-call(f32[16,256,128]{2,1,0:T(8,128)} %bitcast.11), custom_call_target="tpu_custom_call" | custom-call | flops 131072 | bytes 131072 | tf_op jit(solution)/shard_map/pack/pallas_call | solution.py:130
  7.1 0.1 collective-permute-start.3
  7.1 1.1 %pack.3 = f32[1024,128]{1,0:T(8,128)S(1)} custom-call(f32[16,256,128]{2,1,0:T(8,128)} %bitcast.12), custom_call_target="tpu_custom_call" | custom-call | flops 131072 | bytes 131072 | tf_op jit(solution)/shard_map/pack/pallas_call | solution.py:130
  8.2 0.6 %collective-permute-start.5 = (f32[1024,128]{1,0:T(8,128)S(1)}, f32[1024,128]{1,0:T(8,128)S(1)}, u32[]{:S(2)}, u32[]{:S(2)}) collective-permute-start(f32[1024,128]{1,0:T(8,128)S(1)} %pack.3), channel_id=1, source_target_pairs={{0,8},{4,12},{8,0},{12,4},{1,9},{5,13},{9,1},{13,5},{2,10},{6,14},... | collective-permute-start | bytes 1572872 | tf_op jit(solution)/shard_map/ppermute | solution.py:343
  8.8 0.8 %collective-permute-done.refs_0_.d_ref = f32[192,128]{1,0:T(8,128)S(1)} collective-permute-done((f32[192,128]{1,0:T(8,128)S(1)}, f32[192,128]{1,0:T(8,128)S(1)}, u32[]{:S(2)}, u32[]{:S(2)}) %collective-permute-start) | collective-permute-done | bytes 98336 | tf_op jit(solution)/shard_map/ppermute | solution.py:340
  9.6 0.0 copy-done
  9.6 3.4 %source_panels.1 = f32[120,128]{1,0:T(8,128)S(1)} custom-call(f32[16,256,128]{2,1,0:T(8,128)} %bitcast.13, f32[192,128]{1,0:T(8,128)S(1)} %collective-permute-done.refs_0_.d_ref, s32[64,128]{1,0:T(8,128)S(1)} %bitcast.4), custom_call_target="tpu_custom_call" | custom-call | flops 245760 | bytes 245760 | tf_op jit(solution)/shard_map/source_panels/pallas_call | solution.py:187
  13.0 1.6 %collective-permute-start.1 = (f32[120,128]{1,0:T(8,128)S(1)}, f32[120,128]{1,0:T(8,128)S(1)}, u32[]{:S(2)}, u32[]{:S(2)}) collective-permute-start(f32[120,128]{1,0:T(8,128)S(1)} %source_panels.1), channel_id=1, source_target_pairs={{0,2},{2,0},{1,3},{3,1},{4,6},{6,4},{5,7},{7,5},{8,10},{10,8},{9,1... | collective-permute-start | bytes 184328 | tf_op jit(solution)/shard_map/ppermute | solution.py:24
  14.6 2.7 %collective-permute-done.1.in_ref = f32[120,128]{1,0:T(8,128)S(1)} collective-permute-done((f32[120,128]{1,0:T(8,128)S(1)}, f32[120,128]{1,0:T(8,128)S(1)}, u32[]{:S(2)}, u32[]{:S(2)}) %collective-permute-start.1) | collective-permute-done | bytes 61472 | tf_op jit(solution)/shard_map/ppermute | solution.py:24
  17.3 2.1 %source_chunk.1 = f32[896,128]{1,0:T(8,128)S(1)} custom-call(f32[16,256,128]{2,1,0:T(8,128)} %bitcast.14, f32[192,128]{1,0:T(8,128)S(1)} %collective-permute-done.refs_0_.d_ref, f32[120,128]{1,0:T(8,128)S(1)} %collective-permute-done.1.in_ref), custom_call_target="tpu_custom_call" | custom-call | flops 114688 | bytes 114688 | tf_op jit(solution)/shard_map/source_chunk/pallas_call | solution.py:209
  19.4 4.0 %collective-permute-start.2 = (f32[896,128]{1,0:T(8,128)S(1)}, f32[896,128]{1,0:T(8,128)S(1)}, u32[]{:S(2)}, u32[]{:S(2)}) collective-permute-start(f32[896,128]{1,0:T(8,128)S(1)} %source_chunk.1), channel_id=1, source_target_pairs={{0,12},{4,8},{8,4},{12,0},{1,13},{5,9},{9,5},{13,1},{2,14},{6,10},... | collective-permute-start | bytes 1376264 | tf_op jit(solution)/shard_map/ppermute | solution.py:351
  23.4 3.0 %own_result.1.refs_4_ = f32[4096,128]{1,0:T(8,128)} custom-call(f32[16,256,128]{2,1,0:T(8,128)} %bitcast.15, s32[64,128]{1,0:T(8,128)S(1)} %bitcast.5, f32[120,128]{1,0:T(8,128)S(1)} %collective-permute-done.1.in_ref), custom_call_target="tpu_custom_call" | custom-call | flops 131072 | bytes 131072 | tf_op jit(solution)/shard_map/own_result/pallas_call | solution.py:263
  26.4 3.1 %collective-permute-done.3.refs_1_ = f32[1024,128]{1,0:T(8,128)S(1)} collective-permute-done((f32[1024,128]{1,0:T(8,128)S(1)}, f32[1024,128]{1,0:T(8,128)S(1)}, u32[]{:S(2)}, u32[]{:S(2)}) %collective-permute-start.3) | collective-permute-done | bytes 524320 | tf_op jit(solution)/shard_map/ppermute | solution.py:343
  29.5 1.2 %arrived_panels.2 = f32[72,128]{1,0:T(8,128)S(1)} custom-call(f32[192,128]{1,0:T(8,128)S(1)} %collective-permute-done.refs_0_.d_ref, f32[1024,128]{1,0:T(8,128)S(1)} %collective-permute-done.3.refs_1_, s32[64,128]{1,0:T(8,128)S(1)} %bitcast.6), custom_call_target="tpu_custom_call" | custom-call | flops 147456 | bytes 147456 | tf_op jit(solution)/shard_map/arrived_panels/pallas_call | solution.py:242
  30.7 1.6 %collective-permute-start.4 = (f32[72,128]{1,0:T(8,128)S(1)}, f32[72,128]{1,0:T(8,128)S(1)}, u32[]{:S(2)}, u32[]{:S(2)}) collective-permute-start(f32[72,128]{1,0:T(8,128)S(1)} %arrived_panels.2), channel_id=1, source_target_pairs={{0,2},{2,0},{1,3},{3,1},{4,6},{6,4},{5,7},{7,5},{8,10},{10,8},{9,1... | collective-permute-start | bytes 110600 | tf_op jit(solution)/shard_map/ppermute | solution.py:24
  32.2 2.5 %collective-permute-done.4.refs_3_ = f32[72,128]{1,0:T(8,128)S(1)} collective-permute-done((f32[72,128]{1,0:T(8,128)S(1)}, f32[72,128]{1,0:T(8,128)S(1)}, u32[]{:S(2)}, u32[]{:S(2)}) %collective-permute-start.4) | collective-permute-done | bytes 36896 | tf_op jit(solution)/shard_map/ppermute | solution.py:24
  34.7 1.9 %arrived_result.2.refs_3_ = f32[4096,128]{1,0:T(8,128)} custom-call(f32[192,128]{1,0:T(8,128)S(1)} %collective-permute-done.refs_0_.d_ref, f32[1024,128]{1,0:T(8,128)S(1)} %collective-permute-done.3.refs_1_, s32[64,128]{1,0:T(8,128)S(1)} %bitcast.7, f32[72,128]{1,0:T(8,128)S(1)} %collective-permute-done.4.refs_3_, ...), custom_call_target="tpu_custom_call", output_to_operand_aliasing={{}: (4, {})} | custom-call | flops 147456 | bytes 147456 | tf_op jit(solution)/shard_map/arrived_result/pallas_call | solution.py:290
  36.6 8.5 %collective-permute-done.5.refs_0_ = f32[1024,128]{1,0:T(8,128)S(1)} collective-permute-done((f32[1024,128]{1,0:T(8,128)S(1)}, f32[1024,128]{1,0:T(8,128)S(1)}, u32[]{:S(2)}, u32[]{:S(2)}) %collective-permute-start.5) | collective-permute-done | bytes 524320 | tf_op jit(solution)/shard_map/ppermute | solution.py:343
  45.1 1.2 %arrived_panels.3 = f32[64,128]{1,0:T(8,128)S(1)} custom-call(f32[1024,128]{1,0:T(8,128)S(1)} %collective-permute-done.5.refs_0_, s32[64,128]{1,0:T(8,128)S(1)} %bitcast.8), custom_call_target="tpu_custom_call" | custom-call | flops 131072 | bytes 131072 | tf_op jit(solution)/shard_map/arrived_panels/pallas_call | solution.py:242
  46.3 1.6 %collective-permute-start.6 = (f32[64,128]{1,0:T(8,128)S(1)}, f32[64,128]{1,0:T(8,128)S(1)}, u32[]{:S(2)}, u32[]{:S(2)}) collective-permute-start(f32[64,128]{1,0:T(8,128)S(1)} %arrived_panels.3), channel_id=1, source_target_pairs={{0,2},{2,0},{1,3},{3,1},{4,6},{6,4},{5,7},{7,5},{8,10},{10,8},{9,1... | collective-permute-start | bytes 98312 | tf_op jit(solution)/shard_map/ppermute | solution.py:24
  47.8 2.4 %collective-permute-done.6.refs_2_ = f32[64,128]{1,0:T(8,128)S(1)} collective-permute-done((f32[64,128]{1,0:T(8,128)S(1)}, f32[64,128]{1,0:T(8,128)S(1)}, u32[]{:S(2)}, u32[]{:S(2)}) %collective-permute-start.6) | collective-permute-done | bytes 32800 | tf_op jit(solution)/shard_map/ppermute | solution.py:24
  50.2 1.9 %arrived_result.3._ = f32[4096,128]{1,0:T(8,128)} custom-call(f32[1024,128]{1,0:T(8,128)S(1)} %collective-permute-done.5.refs_0_, s32[64,128]{1,0:T(8,128)S(1)} %bitcast.9, f32[64,128]{1,0:T(8,128)S(1)} %collective-permute-done.6.refs_2_, f32[4096,128]{1,0:T(8,128)} %arrived_result.2.refs_3_), custom_call_target="tpu_custom_call", output_to_operand_aliasing={{}: (3, {})} | custom-call | flops 131072 | bytes 131072 | tf_op jit(solution)/shard_map/arrived_result/pallas_call | solution.py:290
  52.2 0.0 collective-permute-done.2.x_ref
  52.2 0.8 %place_chunk.1 = f32[4096,128]{1,0:T(8,128)} custom-call(f32[896,128]{1,0:T(8,128)S(1)} %collective-permute-done.2.x_ref, f32[4096,128]{1,0:T(8,128)} %arrived_result.3._), custom_call_target="tpu_custom_call", output_to_operand_aliasing={{}: (1, {})} | custom-call | flops 114688 | bytes 114688 | tf_op jit(solution)/shard_map/place_chunk/pallas_call | solution.py:310
Async XLA Ops:
  0.9 8.7 %copy-start = (s32[4,1,2048]{2,1,0:T(1,128)S(1)}, s32[4,1,2048]{2,1,0:T(1,128)}, u32[]{:S(2)}) copy-start(s32[4,1,2048]{2,1,0:T(1,128)} %param.3) | copy-start | bytes 98308
  0.9 8.7 %collective-permute-start = (f32[192,128]{1,0:T(8,128)S(1)}, f32[192,128]{1,0:T(8,128)S(1)}, u32[]{:S(2)}, u32[]{:S(2)}) collective-permute-start(f32[192,128]{1,0:T(8,128)S(1)} %pack_with_codes.1), channel_id=1, source_target_pairs={{0,12},{4,8},{8,4},{12,0},{1,13},{5,9},{9,5},{13,1},{2,14},{6,10},... | collective-permute-start | bytes 294920 | tf_op jit(solution)/shard_map/ppermute | solution.py:340
  7.1 22.4 %collective-permute-start.3 = (f32[1024,128]{1,0:T(8,128)S(1)}, f32[1024,128]{1,0:T(8,128)S(1)}, u32[]{:S(2)}, u32[]{:S(2)}) collective-permute-start(f32[1024,128]{1,0:T(8,128)S(1)} %pack.2), channel_id=1, source_target_pairs={{0,4},{4,0},{8,12},{12,8},{1,5},{5,1},{9,13},{13,9},{2,6},{6,2},{1... | collective-permute-start | bytes 1572872 | tf_op jit(solution)/shard_map/ppermute | solution.py:343
  8.2 36.9 %collective-permute-start.5 = (f32[1024,128]{1,0:T(8,128)S(1)}, f32[1024,128]{1,0:T(8,128)S(1)}, u32[]{:S(2)}, u32[]{:S(2)}) collective-permute-start(f32[1024,128]{1,0:T(8,128)S(1)} %pack.3), channel_id=1, source_target_pairs={{0,8},{4,12},{8,0},{12,4},{1,9},{5,13},{9,1},{13,5},{2,10},{6,14},... | collective-permute-start | bytes 1572872 | tf_op jit(solution)/shard_map/ppermute | solution.py:343
  13.0 4.3 %collective-permute-start.1 = (f32[120,128]{1,0:T(8,128)S(1)}, f32[120,128]{1,0:T(8,128)S(1)}, u32[]{:S(2)}, u32[]{:S(2)}) collective-permute-start(f32[120,128]{1,0:T(8,128)S(1)} %source_panels.1), channel_id=1, source_target_pairs={{0,2},{2,0},{1,3},{3,1},{4,6},{6,4},{5,7},{7,5},{8,10},{10,8},{9,1... | collective-permute-start | bytes 184328 | tf_op jit(solution)/shard_map/ppermute | solution.py:24
  19.4 32.8 %collective-permute-start.2 = (f32[896,128]{1,0:T(8,128)S(1)}, f32[896,128]{1,0:T(8,128)S(1)}, u32[]{:S(2)}, u32[]{:S(2)}) collective-permute-start(f32[896,128]{1,0:T(8,128)S(1)} %source_chunk.1), channel_id=1, source_target_pairs={{0,12},{4,8},{8,4},{12,0},{1,13},{5,9},{9,5},{13,1},{2,14},{6,10},... | collective-permute-start | bytes 1376264 | tf_op jit(solution)/shard_map/ppermute | solution.py:351
  30.7 4.0 %collective-permute-start.4 = (f32[72,128]{1,0:T(8,128)S(1)}, f32[72,128]{1,0:T(8,128)S(1)}, u32[]{:S(2)}, u32[]{:S(2)}) collective-permute-start(f32[72,128]{1,0:T(8,128)S(1)} %arrived_panels.2), channel_id=1, source_target_pairs={{0,2},{2,0},{1,3},{3,1},{4,6},{6,4},{5,7},{7,5},{8,10},{10,8},{9,1... | collective-permute-start | bytes 110600 | tf_op jit(solution)/shard_map/ppermute | solution.py:24
  46.3 4.0 %collective-permute-start.6 = (f32[64,128]{1,0:T(8,128)S(1)}, f32[64,128]{1,0:T(8,128)S(1)}, u32[]{:S(2)}, u32[]{:S(2)}) collective-permute-start(f32[64,128]{1,0:T(8,128)S(1)} %arrived_panels.3), channel_id=1, source_target_pairs={{0,2},{2,0},{1,3},{3,1},{4,6},{6,4},{5,7},{7,5},{8,10},{10,8},{9,1... | collective-permute-start | bytes 98312 | tf_op jit(solution)/shard_map/ppermute | solution.py:24

commit v8 on v7

--- a/solution.py
+++ b/solution.py
@@ -121,20 +121,25 @@
     return pl.CostEstimate(flops=rows * ROWS, bytes_accessed=rows * ROWS, transcendentals=0)
 
 
-def pack(x, piece):
-    def body(x_ref, o_ref, sem):
-        copies = piece.gather(x_ref, o_ref, sem)
-        start_all(copies)
-        wait_all(copies)
-
-    return pl.pallas_call(
-        body,
-        out_shape=piece.shape(),
+def pack(x, pieces):
+    rows = sum(piece.rows for piece in pieces)
+
+    def body(x_ref, *refs):
+        o_refs, sem = refs[:-1], refs[-1]
+        copies = [piece.gather(x_ref, o_refs[i], sem.at[i]) for i, piece in enumerate(pieces)]
+        for c in copies:
+            start_all(c)
+        for c in copies:
+            wait_all(c)
+
+    return pl.pallas_call(
+        body,
+        out_shape=[piece.shape() for piece in pieces],
         in_specs=[HBM],
-        out_specs=VMEM,
-        scratch_shapes=[pltpu.SemaphoreType.DMA],
-        compiler_params=params(piece.rows),
-        cost_estimate=cost(piece.rows),
+        out_specs=[VMEM] * len(pieces),
+        scratch_shapes=[pltpu.SemaphoreType.DMA((len(pieces),))],
+        compiler_params=params(rows),
+        cost_estimate=cost(rows),
         name="pack",
     )(x)
 
@@ -330,17 +335,23 @@
     pairs = {k: exchange_pairs(basins, k) for k in range(basins)}
 
     far = basins - 1
-    cut = SUB // sizes.tiles
+    cut = max(SUB // sizes.tiles, members // 4)
     late = Piece(far, cut, members, sizes)
     head = Piece(far, 0, cut, sizes)
-    near = [Piece(k, 0, members, sizes) for k in range(1, basins // 2)]
+    part = max(SUB // sizes.tiles, members // 4)
+    near = [
+        Piece(k, start, start + part, sizes)
+        for k in range(1, basins // 2)
+        for start in range(0, members, part)
+    ]
     across = [Piece(k, 0, members, sizes) for k in range(basins // 2, far)]
 
     first = pack_with_codes(x, head, pltpu.with_memory_space_constraint(codes, pltpu.HBM))
     far_codes = lax.ppermute(first, "basin", pairs[far])
     arrived = {head: far_codes}
-    for piece in across + near:
-        arrived[piece] = lax.ppermute(pack(x, piece), "basin", pairs[piece.k])
+    for group in (across, near):
+        for piece, chunk in zip(group, pack(x, group)):
+            arrived[piece] = lax.ppermute(chunk, "basin", pairs[piece.k])
 
     own = Piece(0, 0, members, sizes)
     source, source_codes, inflow = [late, own], [far_codes, codes], None
@@ -348,6 +359,9 @@
         inflow = from_behind(source_panels(x, source, source_codes, inflow), "chain")
     if inflow is None:
         inflow = jnp.zeros((panel_starts(source)[-1], ROWS), jnp.float32)
+    waited = [arrived[piece] for piece in near]
+    inflow, waited = lax.optimization_barrier((inflow, waited))
+    arrived.update(zip(near, waited))
     finished = lax.ppermute(source_chunk(x, late, far_codes, inflow), "basin", pairs[far])
 
     result = own_result(x, own, codes, inflow, late.count)

time: 53.3 us -> 57.5 us (1.079)
  starting transfers between devices: 14.5 us -> 26.6 us
  waiting for transfers between devices: 19.9 us -> 11.8 us
    ppermute x2 -> x5, starting transfers between devices: 0.7 us -> 16.7 us  [local(): arrived[piece] = lax.ppermute(chunk, 'basin', pairs[piece.k])]
    ppermute x2 -> x5, waiting for transfers between devices: 11.6 us -> 6.75 us  [local(): arrived[piece] = lax.ppermute(chunk, 'basin', pairs[piece.k])]
    ppermute x1, starting transfers between devices: 3.99 us -> 0.07 us  [local(): lax.ppermute(source_chunk(x, late, far_codes, inflow), 'basin', pairs[far])]
    ppermute x3, waiting for transfers between devices: 7.57 us -> 4.94 us  [from_behind(): lax.ppermute(value, axis, [(i, (i + 1) % count) for i in range(count)])]
    ppermute x1, waiting for transfers between devices: 0.76 us -> 0.13 us  [local(): far_codes = lax.ppermute(first, 'basin', pairs[far])]
  transfers between devices with their start and end apart: 7 -> 10, of which waited for: 6 -> 5; matrix products, arithmetic and copies ran while one was open for 0% -> 0% of each run, Pallas kernels for 32% -> 30%
where the time goes in v8:
time: 57.5 us; the launch traced here: 57.2 us
  starting transfers between devices  26.6 us (46%)
  Pallas kernels  18.6 us (32%)
  waiting for transfers between devices  11.8 us (21%)
    ppermute x5, starting transfers between devices, local(): arrived[piece] = lax.ppermute(chunk, 'basin', pairs[piece.k])  16.7 us
    ppermute x5, waiting for transfers between devices, local(): arrived[piece] = lax.ppermute(chunk, 'basin', pairs[piece.k])  6.75 us
    ppermute x1, starting transfers between devices, local(): far_codes = lax.ppermute(first, 'basin', pairs[far])  5.11 us
    ppermute x3, waiting for transfers between devices, from_behind(): lax.ppermute(value, axis, [(i, (i + 1) % count) for i in range(count)])  4.94 us
    ppermute x3, starting transfers between devices, from_behind(): lax.ppermute(value, axis, [(i, (i + 1) % count) for i in range(count)])  4.69 us
    pallas_call x2, Pallas kernels, arrived_result(): pl.pallas_call(body, out_shape=pieces[0].sizes.result(), in_specs=[VMEM]...  3.93 us
    pallas_call x1, Pallas kernels, source_panels(): pl.pallas_call(body, out_shape=jax.ShapeDtypeStruct((starts[-1], ROWS), j...  3.33 us
    pallas_call x1, Pallas kernels, own_result(): pl.pallas_call(body, out_shape=piece.sizes.result(), in_specs=[HBM, VMEM,...  2.98 us
  transfers between devices with their start and end apart: 10, of which 5 were waited for; matrix products, arithmetic and copies ran while one was open for 0% of the time, Pallas kernels for 30%

profile of v8, /device:TPU:0, one launch (start us, length us, event | category | flops | bytes accessed | tf_op | source)
XLA Modules:
  0.0 57.2 jit_solution(463706903257679169)
XLA Ops:
  0.0 0.9 %pack_with_codes.1 = f32[320,128]{1,0:T(8,128)S(1)} custom-call(f32[16,256,128]{2,1,0:T(8,128)} %bitcast.10, s32[64,128]{1,0:T(8,128)} %bitcast.3), custom_call_target="tpu_custom_call" | custom-call | flops 32768 | bytes 32768 | tf_op jit(solution)/shard_map/pack_with_codes/pallas_call | solution.py:159
  0.9 0.0 copy-start
  1.0 5.1 %collective-permute-start = (f32[320,128]{1,0:T(8,128)S(1)}, f32[320,128]{1,0:T(8,128)S(1)}, u32[]{:S(2)}, u32[]{:S(2)}) collective-permute-start(f32[320,128]{1,0:T(8,128)S(1)} %pack_with_codes.1), channel_id=1, source_target_pairs={{0,12},{4,8},{8,4},{12,0},{1,13},{5,9},{9,5},{13,1},{2,14},{6,10},... | collective-permute-start | bytes 491528 | tf_op jit(solution)/shard_map/ppermute | solution.py:350
  6.1 1.1 %pack.2 = (f32[256,128]{1,0:T(8,128)S(1)}, f32[256,128]{1,0:T(8,128)S(1)}, f32[256,128]{1,0:T(8,128)S(1)}, f32[256,128]{1,0:T(8,128)S(1)}) custom-call(f32[16,256,128]{2,1,0:T(8,128)} %bitcast.11), custom_call_target="tpu_custom_call" | custom-call | flops 131072 | bytes 131072 | tf_op jit(solution)/shard_map/pack/pallas_call | solution.py:135
  7.2 0.1 collective-permute-start.2
  7.3 1.1 %pack.3 = f32[1024,128]{1,0:T(8,128)S(1)} custom-call(f32[16,256,128]{2,1,0:T(8,128)} %bitcast.12), custom_call_target="tpu_custom_call" | custom-call | flops 131072 | bytes 131072 | tf_op jit(solution)/shard_map/pack/pallas_call | solution.py:135
  8.4 0.6 %collective-permute-start.8 = (f32[1024,128]{1,0:T(8,128)S(1)}, f32[1024,128]{1,0:T(8,128)S(1)}, u32[]{:S(2)}, u32[]{:S(2)}) collective-permute-start(f32[1024,128]{1,0:T(8,128)S(1)} %pack.3), channel_id=1, source_target_pairs={{0,8},{4,12},{8,0},{12,4},{1,9},{5,13},{9,1},{13,5},{2,10},{6,14},... | collective-permute-start | bytes 1572872 | tf_op jit(solution)/shard_map/ppermute | solution.py:354
  9.0 1.5 %collective-permute-start.3 = (f32[256,128]{1,0:T(8,128)S(1)}, f32[256,128]{1,0:T(8,128)S(1)}, u32[]{:S(2)}, u32[]{:S(2)}) collective-permute-start(f32[256,128]{1,0:T(8,128)S(1)} %get-tuple-element.23), channel_id=1, source_target_pairs={{0,4},{4,0},{8,12},{12,8},{1,5},{5,1},{9,13},{13,9},{2,6},{6,2},{1... | collective-permute-start | bytes 393224 | tf_op jit(solution)/shard_map/ppermute | solution.py:354
  10.5 0.5 collective-permute-start.4
  11.0 0.1 collective-permute-done.refs_0_.d_ref
  11.1 14.0 %collective-permute-start.5 = (f32[256,128]{1,0:T(8,128)S(1)}, f32[256,128]{1,0:T(8,128)S(1)}, u32[]{:S(2)}, u32[]{:S(2)}) collective-permute-start(f32[256,128]{1,0:T(8,128)S(1)} %get-tuple-element.25), channel_id=1, source_target_pairs={{0,4},{4,0},{8,12},{12,8},{1,5},{5,1},{9,13},{13,9},{2,6},{6,2},{1... | collective-permute-start | bytes 393224 | tf_op jit(solution)/shard_map/ppermute | solution.py:354
  25.2 0.0 copy-done
  25.2 3.3 %source_panels.1 = f32[112,128]{1,0:T(8,128)S(1)} custom-call(f32[16,256,128]{2,1,0:T(8,128)} %bitcast.13, f32[320,128]{1,0:T(8,128)S(1)} %collective-permute-done.refs_0_.d_ref, s32[64,128]{1,0:T(8,128)S(1)} %bitcast.4), custom_call_target="tpu_custom_call" | custom-call | flops 229376 | bytes 229376 | tf_op jit(solution)/shard_map/source_panels/pallas_call | solution.py:192
  28.5 0.0 collective-permute-done.2.refs_1_
  28.5 1.6 %collective-permute-start.1 = (f32[112,128]{1,0:T(8,128)S(1)}, f32[112,128]{1,0:T(8,128)S(1)}, u32[]{:S(2)}, u32[]{:S(2)}) collective-permute-start(f32[112,128]{1,0:T(8,128)S(1)} %source_panels.1), channel_id=1, source_target_pairs={{0,2},{2,0},{1,3},{3,1},{4,6},{6,4},{5,7},{7,5},{8,10},{10,8},{9,1... | collective-permute-start | bytes 172040 | tf_op jit(solution)/shard_map/ppermute | solution.py:24
  30.1 0.0 collective-permute-done.3.refs_2_
  30.1 0.3 collective-permute-done.4.refs_3_
  30.4 6.4 %collective-permute-done.5.refs_4_ = f32[256,128]{1,0:T(8,128)S(1)} collective-permute-done((f32[256,128]{1,0:T(8,128)S(1)}, f32[256,128]{1,0:T(8,128)S(1)}, u32[]{:S(2)}, u32[]{:S(2)}) %collective-permute-start.5) | collective-permute-done | bytes 131104 | tf_op jit(solution)/shard_map/ppermute | solution.py:354
  36.8 0.0 collective-permute-done.1.in_ref
  36.8 2.1 %source_chunk.1 = f32[768,128]{1,0:T(8,128)S(1)} custom-call(f32[16,256,128]{2,1,0:T(8,128)} %bitcast.14, f32[320,128]{1,0:T(8,128)S(1)} %collective-permute-done.refs_0_.d_ref, f32[112,128]{1,0:T(8,128)S(1)} %collective-permute-done.1.in_ref), custom_call_target="tpu_custom_call" | custom-call | flops 98304 | bytes 98304 | tf_op jit(solution)/shard_map/source_chunk/pallas_call | solution.py:214
  38.9 0.1 collective-permute-start.6
  39.0 3.0 %own_result.1.refs_7_ = f32[4096,128]{1,0:T(8,128)} custom-call(f32[16,256,128]{2,1,0:T(8,128)} %bitcast.15, s32[64,128]{1,0:T(8,128)S(1)} %bitcast.5, f32[112,128]{1,0:T(8,128)S(1)} %collective-permute-done.1.in_ref), custom_call_target="tpu_custom_call" | custom-call | flops 131072 | bytes 131072 | tf_op jit(solution)/shard_map/own_result/pallas_call | solution.py:268
  42.0 1.2 %arrived_panels.2 = f32[80,128]{1,0:T(8,128)S(1)} custom-call(f32[320,128]{1,0:T(8,128)S(1)} %collective-permute-done.refs_0_.d_ref, f32[256,128]{1,0:T(8,128)S(1)} %collective-permute-done.2.refs_1_, f32[256,128]{1,0:T(8,128)S(1)} %collective-permute-done.3.refs_2_, f32[256,128]{1,0:T(8,128)S(1)} %collective-permute-done.4.refs_3_, ...), custom_call_target="tpu_custom_call" | custom-call | flops 163840 | bytes 163840 | tf_op jit(solution)/shard_map/arrived_panels/pallas_call | solution.py:247
  43.2 1.6 %collective-permute-start.7 = (f32[80,128]{1,0:T(8,128)S(1)}, f32[80,128]{1,0:T(8,128)S(1)}, u32[]{:S(2)}, u32[]{:S(2)}) collective-permute-start(f32[80,128]{1,0:T(8,128)S(1)} %arrived_panels.2), channel_id=1, source_target_pairs={{0,2},{2,0},{1,3},{3,1},{4,6},{6,4},{5,7},{7,5},{8,10},{10,8},{9,1... | collective-permute-start | bytes 122888 | tf_op jit(solution)/shard_map/ppermute | solution.py:24
  44.8 2.5 %collective-permute-done.7.refs_6_ = f32[80,128]{1,0:T(8,128)S(1)} collective-permute-done((f32[80,128]{1,0:T(8,128)S(1)}, f32[80,128]{1,0:T(8,128)S(1)}, u32[]{:S(2)}, u32[]{:S(2)}) %collective-permute-start.7) | collective-permute-done | bytes 40992 | tf_op jit(solution)/shard_map/ppermute | solution.py:24
  47.3 2.0 %arrived_result.2.refs_3_ = f32[4096,128]{1,0:T(8,128)} custom-call(f32[320,128]{1,0:T(8,128)S(1)} %collective-permute-done.refs_0_.d_ref, f32[256,128]{1,0:T(8,128)S(1)} %collective-permute-done.2.refs_1_, f32[256,128]{1,0:T(8,128)S(1)} %collective-permute-done.3.refs_2_, ...), custom_call_target="tpu_custom_call", output_to_operand_aliasing={{}: (7, {})} | custom-call | flops 163840 | bytes 163840 | tf_op jit(solution)/shard_map/arrived_result/pallas_call | solution.py:295
  49.3 0.0 collective-permute-done.8.refs_0_
  49.3 1.2 %arrived_panels.3 = f32[64,128]{1,0:T(8,128)S(1)} custom-call(f32[1024,128]{1,0:T(8,128)S(1)} %collective-permute-done.8.refs_0_, s32[64,128]{1,0:T(8,128)S(1)} %bitcast.8), custom_call_target="tpu_custom_call" | custom-call | flops 131072 | bytes 131072 | tf_op jit(solution)/shard_map/arrived_panels/pallas_call | solution.py:247
  50.5 1.6 %collective-permute-start.9 = (f32[64,128]{1,0:T(8,128)S(1)}, f32[64,128]{1,0:T(8,128)S(1)}, u32[]{:S(2)}, u32[]{:S(2)}) collective-permute-start(f32[64,128]{1,0:T(8,128)S(1)} %arrived_panels.3), channel_id=1, source_target_pairs={{0,2},{2,0},{1,3},{3,1},{4,6},{6,4},{5,7},{7,5},{8,10},{10,8},{9,1... | collective-permute-start | bytes 98312 | tf_op jit(solution)/shard_map/ppermute | solution.py:24
  52.0 2.4 %collective-permute-done.9.refs_2_ = f32[64,128]{1,0:T(8,128)S(1)} collective-permute-done((f32[64,128]{1,0:T(8,128)S(1)}, f32[64,128]{1,0:T(8,128)S(1)}, u32[]{:S(2)}, u32[]{:S(2)}) %collective-permute-start.9) | collective-permute-done | bytes 32800 | tf_op jit(solution)/shard_map/ppermute | solution.py:24
  54.4 1.9 %arrived_result.3._ = f32[4096,128]{1,0:T(8,128)} custom-call(f32[1024,128]{1,0:T(8,128)S(1)} %collective-permute-done.8.refs_0_, s32[64,128]{1,0:T(8,128)S(1)} %bitcast.9, f32[64,128]{1,0:T(8,128)S(1)} %collective-permute-done.9.refs_2_, f32[4096,128]{1,0:T(8,128)} %arrived_result.2.refs_3_), custom_call_target="tpu_custom_call", output_to_operand_aliasing={{}: (3, {})} | custom-call | flops 131072 | bytes 131072 | tf_op jit(solution)/shard_map/arrived_result/pallas_call | solution.py:295
  56.4 0.0 collective-permute-done.6.x_ref
  56.4 0.8 %place_chunk.1 = f32[4096,128]{1,0:T(8,128)} custom-call(f32[768,128]{1,0:T(8,128)S(1)} %collective-permute-done.6.x_ref, f32[4096,128]{1,0:T(8,128)} %arrived_result.3._), custom_call_target="tpu_custom_call", output_to_operand_aliasing={{}: (1, {})} | custom-call | flops 98304 | bytes 98304 | tf_op jit(solution)/shard_map/place_chunk/pallas_call | solution.py:315
Async XLA Ops:
  0.9 24.2 %copy-start = (s32[4,1,2048]{2,1,0:T(1,128)S(1)}, s32[4,1,2048]{2,1,0:T(1,128)}, u32[]{:S(2)}) copy-start(s32[4,1,2048]{2,1,0:T(1,128)} %param.3) | copy-start | bytes 98308
  1.0 10.2 %collective-permute-start = (f32[320,128]{1,0:T(8,128)S(1)}, f32[320,128]{1,0:T(8,128)S(1)}, u32[]{:S(2)}, u32[]{:S(2)}) collective-permute-start(f32[320,128]{1,0:T(8,128)S(1)} %pack_with_codes.1), channel_id=1, source_target_pairs={{0,12},{4,8},{8,4},{12,0},{1,13},{5,9},{9,5},{13,1},{2,14},{6,10},... | collective-permute-start | bytes 491528 | tf_op jit(solution)/shard_map/ppermute | solution.py:350
  7.2 21.3 %collective-permute-start.2 = (f32[256,128]{1,0:T(8,128)S(1)}, f32[256,128]{1,0:T(8,128)S(1)}, u32[]{:S(2)}, u32[]{:S(2)}) collective-permute-start(f32[256,128]{1,0:T(8,128)S(1)} %get-tuple-element.22), channel_id=1, source_target_pairs={{0,4},{4,0},{8,12},{12,8},{1,5},{5,1},{9,13},{13,9},{2,6},{6,2},{1... | collective-permute-start | bytes 393224 | tf_op jit(solution)/shard_map/ppermute | solution.py:354
  8.4 40.9 %collective-permute-start.8 = (f32[1024,128]{1,0:T(8,128)S(1)}, f32[1024,128]{1,0:T(8,128)S(1)}, u32[]{:S(2)}, u32[]{:S(2)}) collective-permute-start(f32[1024,128]{1,0:T(8,128)S(1)} %pack.3), channel_id=1, source_target_pairs={{0,8},{4,12},{8,0},{12,4},{1,9},{5,13},{9,1},{13,5},{2,10},{6,14},... | collective-permute-start | bytes 1572872 | tf_op jit(solution)/shard_map/ppermute | solution.py:354
  9.0 21.1 %collective-permute-start.3 = (f32[256,128]{1,0:T(8,128)S(1)}, f32[256,128]{1,0:T(8,128)S(1)}, u32[]{:S(2)}, u32[]{:S(2)}) collective-permute-start(f32[256,128]{1,0:T(8,128)S(1)} %get-tuple-element.23), channel_id=1, source_target_pairs={{0,4},{4,0},{8,12},{12,8},{1,5},{5,1},{9,13},{13,9},{2,6},{6,2},{1... | collective-permute-start | bytes 393224 | tf_op jit(solution)/shard_map/ppermute | solution.py:354
  10.5 19.9 %collective-permute-start.4 = (f32[256,128]{1,0:T(8,128)S(1)}, f32[256,128]{1,0:T(8,128)S(1)}, u32[]{:S(2)}, u32[]{:S(2)}) collective-permute-start(f32[256,128]{1,0:T(8,128)S(1)} %get-tuple-element.24), channel_id=1, source_target_pairs={{0,4},{4,0},{8,12},{12,8},{1,5},{5,1},{9,13},{13,9},{2,6},{6,2},{1... | collective-permute-start | bytes 393224 | tf_op jit(solution)/shard_map/ppermute | solution.py:354
  11.1 25.7 %collective-permute-start.5 = (f32[256,128]{1,0:T(8,128)S(1)}, f32[256,128]{1,0:T(8,128)S(1)}, u32[]{:S(2)}, u32[]{:S(2)}) collective-permute-start(f32[256,128]{1,0:T(8,128)S(1)} %get-tuple-element.25), channel_id=1, source_target_pairs={{0,4},{4,0},{8,12},{12,8},{1,5},{5,1},{9,13},{13,9},{2,6},{6,2},{1... | collective-permute-start | bytes 393224 | tf_op jit(solution)/shard_map/ppermute | solution.py:354
  28.5 8.3 %collective-permute-start.1 = (f32[112,128]{1,0:T(8,128)S(1)}, f32[112,128]{1,0:T(8,128)S(1)}, u32[]{:S(2)}, u32[]{:S(2)}) collective-permute-start(f32[112,128]{1,0:T(8,128)S(1)} %source_panels.1), channel_id=1, source_target_pairs={{0,2},{2,0},{1,3},{3,1},{4,6},{6,4},{5,7},{7,5},{8,10},{10,8},{9,1... | collective-permute-start | bytes 172040 | tf_op jit(solution)/shard_map/ppermute | solution.py:24
  38.9 17.4 %collective-permute-start.6 = (f32[768,128]{1,0:T(8,128)S(1)}, f32[768,128]{1,0:T(8,128)S(1)}, u32[]{:S(2)}, u32[]{:S(2)}) collective-permute-start(f32[768,128]{1,0:T(8,128)S(1)} %source_chunk.1), channel_id=1, source_target_pairs={{0,12},{4,8},{8,4},{12,0},{1,13},{5,9},{9,5},{13,1},{2,14},{6,10},... | collective-permute-start | bytes 1179656 | tf_op jit(solution)/shard_map/ppermute | solution.py:365
  43.2 4.1 %collective-permute-start.7 = (f32[80,128]{1,0:T(8,128)S(1)}, f32[80,128]{1,0:T(8,128)S(1)}, u32[]{:S(2)}, u32[]{:S(2)}) collective-permute-start(f32[80,128]{1,0:T(8,128)S(1)} %arrived_panels.2), channel_id=1, source_target_pairs={{0,2},{2,0},{1,3},{3,1},{4,6},{6,4},{5,7},{7,5},{8,10},{10,8},{9,1... | collective-permute-start | bytes 122888 | tf_op jit(solution)/shard_map/ppermute | solution.py:24
  50.5 4.0 %collective-permute-start.9 = (f32[64,128]{1,0:T(8,128)S(1)}, f32[64,128]{1,0:T(8,128)S(1)}, u32[]{:S(2)}, u32[]{:S(2)}) collective-permute-start(f32[64,128]{1,0:T(8,128)S(1)} %arrived_panels.3), channel_id=1, source_target_pairs={{0,2},{2,0},{1,3},{3,1},{4,6},{6,4},{5,7},{7,5},{8,10},{10,8},{9,1... | collective-permute-start | bytes 98312 | tf_op jit(solution)/shard_map/ppermute | solution.py:24

commit v9 on v7

--- a/solution.py
+++ b/solution.py
@@ -330,7 +330,7 @@
     pairs = {k: exchange_pairs(basins, k) for k in range(basins)}
 
     far = basins - 1
-    cut = SUB // sizes.tiles
+    cut = max(SUB // sizes.tiles, members // 4)
     late = Piece(far, cut, members, sizes)
     head = Piece(far, 0, cut, sizes)
     near = [Piece(k, 0, members, sizes) for k in range(1, basins // 2)]
@@ -348,9 +348,9 @@
         inflow = from_behind(source_panels(x, source, source_codes, inflow), "chain")
     if inflow is None:
         inflow = jnp.zeros((panel_starts(source)[-1], ROWS), jnp.float32)
+    result = own_result(x, own, codes, inflow, late.count)
+    result, inflow = lax.optimization_barrier((result, inflow))
     finished = lax.ppermute(source_chunk(x, late, far_codes, inflow), "basin", pairs[far])
-
-    result = own_result(x, own, codes, inflow, late.count)
     for group in ([head] + near, across):
         chunks = [arrived[piece] for piece in group]
         result, chunks = lax.optimization_barrier((result, chunks))

time: 53.3 us -> 53 us (level)
    ppermute x2, waiting for transfers between devices: 11.6 us -> 9.88 us  [local(): arrived[piece] = lax.ppermute(pack(x, piece), 'basin', pairs[piece.k])]
    ppermute x1, waiting for transfers between devices: 0.76 us -> 2.24 us  [local(): far_codes = lax.ppermute(first, 'basin', pairs[far])]
where the time goes in v9:
time: 53 us; the launch traced here: 52.7 us
  waiting for transfers between devices  19.5 us (37%)
  Pallas kernels  18.5 us (35%)
  starting transfers between devices  14.6 us (28%)
    ppermute x2, waiting for transfers between devices, local(): arrived[piece] = lax.ppermute(pack(x, piece), 'basin', pairs[piece.k])  9.88 us
    ppermute x3, waiting for transfers between devices, from_behind(): lax.ppermute(value, axis, [(i, (i + 1) % count) for i in range(count)])  7.41 us
    ppermute x1, starting transfers between devices, local(): far_codes = lax.ppermute(first, 'basin', pairs[far])  5.11 us
    ppermute x3, starting transfers between devices, from_behind(): lax.ppermute(value, axis, [(i, (i + 1) % count) for i in range(count)])  4.88 us
    pallas_call x2, Pallas kernels, arrived_result(): pl.pallas_call(body, out_shape=pieces[0].sizes.result(), in_specs=[VMEM]...  3.91 us
    ppermute x1, starting transfers between devices, local(): lax.ppermute(source_chunk(x, late, far_codes, inflow), 'basin', pairs[far])  3.88 us
    pallas_call x1, Pallas kernels, source_panels(): pl.pallas_call(body, out_shape=jax.ShapeDtypeStruct((starts[-1], ROWS), j...  3.33 us
    pallas_call x1, Pallas kernels, own_result(): pl.pallas_call(body, out_shape=piece.sizes.result(), in_specs=[HBM, VMEM,...  2.97 us
  transfers between devices with their start and end apart: 7, of which 6 were waited for; matrix products, arithmetic and copies ran while one was open for 0% of the time, Pallas kernels for 32%

profile of v9, /device:TPU:0, one launch (start us, length us, event | category | flops | bytes accessed | tf_op | source)
XLA Modules:
  0.0 52.7 jit_solution(2690049847313758354)
XLA Ops:
  0.0 0.9 %pack_with_codes.1 = f32[320,128]{1,0:T(8,128)S(1)} custom-call(f32[16,256,128]{2,1,0:T(8,128)} %bitcast.10, s32[64,128]{1,0:T(8,128)} %bitcast.3), custom_call_target="tpu_custom_call" | custom-call | flops 32768 | bytes 32768 | tf_op jit(solution)/shard_map/pack_with_codes/pallas_call | solution.py:154
  0.9 0.0 copy-start
  1.0 5.1 %collective-permute-start = (f32[320,128]{1,0:T(8,128)S(1)}, f32[320,128]{1,0:T(8,128)S(1)}, u32[]{:S(2)}, u32[]{:S(2)}) collective-permute-start(f32[320,128]{1,0:T(8,128)S(1)} %pack_with_codes.1), channel_id=1, source_target_pairs={{0,12},{4,8},{8,4},{12,0},{1,13},{5,9},{9,5},{13,1},{2,14},{6,10},... | collective-permute-start | bytes 491528 | tf_op jit(solution)/shard_map/ppermute | solution.py:340
  6.1 1.0 %pack.2 = f32[1024,128]{1,0:T(8,128)S(1)} custom-call(f32[16,256,128]{2,1,0:T(8,128)} %bitcast.11), custom_call_target="tpu_custom_call" | custom-call | flops 131072 | bytes 131072 | tf_op jit(solution)/shard_map/pack/pallas_call | solution.py:130
  7.1 0.1 collective-permute-start.3
  7.2 1.1 %pack.3 = f32[1024,128]{1,0:T(8,128)S(1)} custom-call(f32[16,256,128]{2,1,0:T(8,128)} %bitcast.12), custom_call_target="tpu_custom_call" | custom-call | flops 131072 | bytes 131072 | tf_op jit(solution)/shard_map/pack/pallas_call | solution.py:130
  8.3 0.6 %collective-permute-start.5 = (f32[1024,128]{1,0:T(8,128)S(1)}, f32[1024,128]{1,0:T(8,128)S(1)}, u32[]{:S(2)}, u32[]{:S(2)}) collective-permute-start(f32[1024,128]{1,0:T(8,128)S(1)} %pack.3), channel_id=1, source_target_pairs={{0,8},{4,12},{8,0},{12,4},{1,9},{5,13},{9,1},{13,5},{2,10},{6,14},... | collective-permute-start | bytes 1572872 | tf_op jit(solution)/shard_map/ppermute | solution.py:343
  8.9 2.2 %collective-permute-done.refs_0_.d_ref = f32[320,128]{1,0:T(8,128)S(1)} collective-permute-done((f32[320,128]{1,0:T(8,128)S(1)}, f32[320,128]{1,0:T(8,128)S(1)}, u32[]{:S(2)}, u32[]{:S(2)}) %collective-permute-start) | collective-permute-done | bytes 163872 | tf_op jit(solution)/shard_map/ppermute | solution.py:340
  11.1 0.0 copy-done
  11.2 3.3 %source_panels.1 = f32[112,128]{1,0:T(8,128)S(1)} custom-call(f32[16,256,128]{2,1,0:T(8,128)} %bitcast.13, f32[320,128]{1,0:T(8,128)S(1)} %collective-permute-done.refs_0_.d_ref, s32[64,128]{1,0:T(8,128)S(1)} %bitcast.4), custom_call_target="tpu_custom_call" | custom-call | flops 229376 | bytes 229376 | tf_op jit(solution)/shard_map/source_panels/pallas_call | solution.py:187
  14.5 1.8 %collective-permute-start.1 = (f32[112,128]{1,0:T(8,128)S(1)}, f32[112,128]{1,0:T(8,128)S(1)}, u32[]{:S(2)}, u32[]{:S(2)}) collective-permute-start(f32[112,128]{1,0:T(8,128)S(1)} %source_panels.1), channel_id=1, source_target_pairs={{0,2},{2,0},{1,3},{3,1},{4,6},{6,4},{5,7},{7,5},{8,10},{10,8},{9,1... | collective-permute-start | bytes 172040 | tf_op jit(solution)/shard_map/ppermute | solution.py:24
  16.3 2.5 %collective-permute-done.1.in_ref = f32[112,128]{1,0:T(8,128)S(1)} collective-permute-done((f32[112,128]{1,0:T(8,128)S(1)}, f32[112,128]{1,0:T(8,128)S(1)}, u32[]{:S(2)}, u32[]{:S(2)}) %collective-permute-start.1) | collective-permute-done | bytes 57376 | tf_op jit(solution)/shard_map/ppermute | solution.py:24
  18.7 3.0 %own_result.1.refs_4_ = f32[4096,128]{1,0:T(8,128)} custom-call(f32[16,256,128]{2,1,0:T(8,128)} %bitcast.14, s32[64,128]{1,0:T(8,128)S(1)} %bitcast.5, f32[112,128]{1,0:T(8,128)S(1)} %collective-permute-done.1.in_ref), custom_call_target="tpu_custom_call" | custom-call | flops 131072 | bytes 131072 | tf_op jit(solution)/shard_map/own_result/pallas_call | solution.py:263
  21.7 2.1 %source_chunk.1 = f32[768,128]{1,0:T(8,128)S(1)} custom-call(f32[16,256,128]{2,1,0:T(8,128)} %bitcast.15, f32[320,128]{1,0:T(8,128)S(1)} %collective-permute-done.refs_0_.d_ref, f32[112,128]{1,0:T(8,128)S(1)} %collective-permute-done.1.in_ref), custom_call_target="tpu_custom_call" | custom-call | flops 98304 | bytes 98304 | tf_op jit(solution)/shard_map/source_chunk/pallas_call | solution.py:209
  23.9 3.9 %collective-permute-start.2 = (f32[768,128]{1,0:T(8,128)S(1)}, f32[768,128]{1,0:T(8,128)S(1)}, u32[]{:S(2)}, u32[]{:S(2)}) collective-permute-start(f32[768,128]{1,0:T(8,128)S(1)} %source_chunk.1), channel_id=1, source_target_pairs={{0,12},{4,8},{8,4},{12,0},{1,13},{5,9},{9,5},{13,1},{2,14},{6,10},... | collective-permute-start | bytes 1179656 | tf_op jit(solution)/shard_map/ppermute | solution.py:353
  27.7 2.5 %collective-permute-done.3.refs_1_ = f32[1024,128]{1,0:T(8,128)S(1)} collective-permute-done((f32[1024,128]{1,0:T(8,128)S(1)}, f32[1024,128]{1,0:T(8,128)S(1)}, u32[]{:S(2)}, u32[]{:S(2)}) %collective-permute-start.3) | collective-permute-done | bytes 524320 | tf_op jit(solution)/shard_map/ppermute | solution.py:343
  30.3 1.2 %arrived_panels.2 = f32[80,128]{1,0:T(8,128)S(1)} custom-call(f32[320,128]{1,0:T(8,128)S(1)} %collective-permute-done.refs_0_.d_ref, f32[1024,128]{1,0:T(8,128)S(1)} %collective-permute-done.3.refs_1_, s32[64,128]{1,0:T(8,128)S(1)} %bitcast.6), custom_call_target="tpu_custom_call" | custom-call | flops 163840 | bytes 163840 | tf_op jit(solution)/shard_map/arrived_panels/pallas_call | solution.py:242
  31.4 1.6 %collective-permute-start.4 = (f32[80,128]{1,0:T(8,128)S(1)}, f32[80,128]{1,0:T(8,128)S(1)}, u32[]{:S(2)}, u32[]{:S(2)}) collective-permute-start(f32[80,128]{1,0:T(8,128)S(1)} %arrived_panels.2), channel_id=1, source_target_pairs={{0,2},{2,0},{1,3},{3,1},{4,6},{6,4},{5,7},{7,5},{8,10},{10,8},{9,1... | collective-permute-start | bytes 122888 | tf_op jit(solution)/shard_map/ppermute | solution.py:24
  33.0 2.5 %collective-permute-done.4.refs_3_ = f32[80,128]{1,0:T(8,128)S(1)} collective-permute-done((f32[80,128]{1,0:T(8,128)S(1)}, f32[80,128]{1,0:T(8,128)S(1)}, u32[]{:S(2)}, u32[]{:S(2)}) %collective-permute-start.4) | collective-permute-done | bytes 40992 | tf_op jit(solution)/shard_map/ppermute | solution.py:24
  35.5 2.0 %arrived_result.2.refs_3_ = f32[4096,128]{1,0:T(8,128)} custom-call(f32[320,128]{1,0:T(8,128)S(1)} %collective-permute-done.refs_0_.d_ref, f32[1024,128]{1,0:T(8,128)S(1)} %collective-permute-done.3.refs_1_, s32[64,128]{1,0:T(8,128)S(1)} %bitcast.7, f32[80,128]{1,0:T(8,128)S(1)} %collective-permute-done.4.refs_3_, ...), custom_call_target="tpu_custom_call", output_to_operand_aliasing={{}: (4, {})} | custom-call | flops 163840 | bytes 163840 | tf_op jit(solution)/shard_map/arrived_result/pallas_call | solution.py:290
  37.5 7.3 %collective-permute-done.5.refs_0_ = f32[1024,128]{1,0:T(8,128)S(1)} collective-permute-done((f32[1024,128]{1,0:T(8,128)S(1)}, f32[1024,128]{1,0:T(8,128)S(1)}, u32[]{:S(2)}, u32[]{:S(2)}) %collective-permute-start.5) | collective-permute-done | bytes 524320 | tf_op jit(solution)/shard_map/ppermute | solution.py:343
  44.8 1.2 %arrived_panels.3 = f32[64,128]{1,0:T(8,128)S(1)} custom-call(f32[1024,128]{1,0:T(8,128)S(1)} %collective-permute-done.5.refs_0_, s32[64,128]{1,0:T(8,128)S(1)} %bitcast.8), custom_call_target="tpu_custom_call" | custom-call | flops 131072 | bytes 131072 | tf_op jit(solution)/shard_map/arrived_panels/pallas_call | solution.py:242
  46.0 1.6 %collective-permute-start.6 = (f32[64,128]{1,0:T(8,128)S(1)}, f32[64,128]{1,0:T(8,128)S(1)}, u32[]{:S(2)}, u32[]{:S(2)}) collective-permute-start(f32[64,128]{1,0:T(8,128)S(1)} %arrived_panels.3), channel_id=1, source_target_pairs={{0,2},{2,0},{1,3},{3,1},{4,6},{6,4},{5,7},{7,5},{8,10},{10,8},{9,1... | collective-permute-start | bytes 98312 | tf_op jit(solution)/shard_map/ppermute | solution.py:24
  47.6 2.4 %collective-permute-done.6.refs_2_ = f32[64,128]{1,0:T(8,128)S(1)} collective-permute-done((f32[64,128]{1,0:T(8,128)S(1)}, f32[64,128]{1,0:T(8,128)S(1)}, u32[]{:S(2)}, u32[]{:S(2)}) %collective-permute-start.6) | collective-permute-done | bytes 32800 | tf_op jit(solution)/shard_map/ppermute | solution.py:24
  50.0 1.9 %arrived_result.3._ = f32[4096,128]{1,0:T(8,128)} custom-call(f32[1024,128]{1,0:T(8,128)S(1)} %collective-permute-done.5.refs_0_, s32[64,128]{1,0:T(8,128)S(1)} %bitcast.9, f32[64,128]{1,0:T(8,128)S(1)} %collective-permute-done.6.refs_2_, f32[4096,128]{1,0:T(8,128)} %arrived_result.2.refs_3_), custom_call_target="tpu_custom_call", output_to_operand_aliasing={{}: (3, {})} | custom-call | flops 131072 | bytes 131072 | tf_op jit(solution)/shard_map/arrived_result/pallas_call | solution.py:290
  51.9 0.0 collective-permute-done.2.x_ref
  51.9 0.8 %place_chunk.1 = f32[4096,128]{1,0:T(8,128)} custom-call(f32[768,128]{1,0:T(8,128)S(1)} %collective-permute-done.2.x_ref, f32[4096,128]{1,0:T(8,128)} %arrived_result.3._), custom_call_target="tpu_custom_call", output_to_operand_aliasing={{}: (1, {})} | custom-call | flops 98304 | bytes 98304 | tf_op jit(solution)/shard_map/place_chunk/pallas_call | solution.py:310
Async XLA Ops:
  0.9 10.2 %copy-start = (s32[4,1,2048]{2,1,0:T(1,128)S(1)}, s32[4,1,2048]{2,1,0:T(1,128)}, u32[]{:S(2)}) copy-start(s32[4,1,2048]{2,1,0:T(1,128)} %param.3) | copy-start | bytes 98308
  1.0 10.2 %collective-permute-start = (f32[320,128]{1,0:T(8,128)S(1)}, f32[320,128]{1,0:T(8,128)S(1)}, u32[]{:S(2)}, u32[]{:S(2)}) collective-permute-start(f32[320,128]{1,0:T(8,128)S(1)} %pack_with_codes.1), channel_id=1, source_target_pairs={{0,12},{4,8},{8,4},{12,0},{1,13},{5,9},{9,5},{13,1},{2,14},{6,10},... | collective-permute-start | bytes 491528 | tf_op jit(solution)/shard_map/ppermute | solution.py:340
  7.1 23.2 %collective-permute-start.3 = (f32[1024,128]{1,0:T(8,128)S(1)}, f32[1024,128]{1,0:T(8,128)S(1)}, u32[]{:S(2)}, u32[]{:S(2)}) collective-permute-start(f32[1024,128]{1,0:T(8,128)S(1)} %pack.2), channel_id=1, source_target_pairs={{0,4},{4,0},{8,12},{12,8},{1,5},{5,1},{9,13},{13,9},{2,6},{6,2},{1... | collective-permute-start | bytes 1572872 | tf_op jit(solution)/shard_map/ppermute | solution.py:343
  8.3 36.6 %collective-permute-start.5 = (f32[1024,128]{1,0:T(8,128)S(1)}, f32[1024,128]{1,0:T(8,128)S(1)}, u32[]{:S(2)}, u32[]{:S(2)}) collective-permute-start(f32[1024,128]{1,0:T(8,128)S(1)} %pack.3), channel_id=1, source_target_pairs={{0,8},{4,12},{8,0},{12,4},{1,9},{5,13},{9,1},{13,5},{2,10},{6,14},... | collective-permute-start | bytes 1572872 | tf_op jit(solution)/shard_map/ppermute | solution.py:343
  14.5 4.2 %collective-permute-start.1 = (f32[112,128]{1,0:T(8,128)S(1)}, f32[112,128]{1,0:T(8,128)S(1)}, u32[]{:S(2)}, u32[]{:S(2)}) collective-permute-start(f32[112,128]{1,0:T(8,128)S(1)} %source_panels.1), channel_id=1, source_target_pairs={{0,2},{2,0},{1,3},{3,1},{4,6},{6,4},{5,7},{7,5},{8,10},{10,8},{9,1... | collective-permute-start | bytes 172040 | tf_op jit(solution)/shard_map/ppermute | solution.py:24
  23.9 28.1 %collective-permute-start.2 = (f32[768,128]{1,0:T(8,128)S(1)}, f32[768,128]{1,0:T(8,128)S(1)}, u32[]{:S(2)}, u32[]{:S(2)}) collective-permute-start(f32[768,128]{1,0:T(8,128)S(1)} %source_chunk.1), channel_id=1, source_target_pairs={{0,12},{4,8},{8,4},{12,0},{1,13},{5,9},{9,5},{13,1},{2,14},{6,10},... | collective-permute-start | bytes 1179656 | tf_op jit(solution)/shard_map/ppermute | solution.py:353
  31.4 4.1 %collective-permute-start.4 = (f32[80,128]{1,0:T(8,128)S(1)}, f32[80,128]{1,0:T(8,128)S(1)}, u32[]{:S(2)}, u32[]{:S(2)}) collective-permute-start(f32[80,128]{1,0:T(8,128)S(1)} %arrived_panels.2), channel_id=1, source_target_pairs={{0,2},{2,0},{1,3},{3,1},{4,6},{6,4},{5,7},{7,5},{8,10},{10,8},{9,1... | collective-permute-start | bytes 122888 | tf_op jit(solution)/shard_map/ppermute | solution.py:24
  46.0 4.0 %collective-permute-start.6 = (f32[64,128]{1,0:T(8,128)S(1)}, f32[64,128]{1,0:T(8,128)S(1)}, u32[]{:S(2)}, u32[]{:S(2)}) collective-permute-start(f32[64,128]{1,0:T(8,128)S(1)} %arrived_panels.3), channel_id=1, source_target_pairs={{0,2},{2,0},{1,3},{3,1},{4,6},{6,4},{5,7},{7,5},{8,10},{10,8},{9,1... | collective-permute-start | bytes 98312 | tf_op jit(solution)/shard_map/ppermute | solution.py:24

commit v10 on v9

--- a/solution.py
+++ b/solution.py
@@ -330,11 +330,17 @@
     pairs = {k: exchange_pairs(basins, k) for k in range(basins)}
 
     far = basins - 1
-    cut = max(SUB // sizes.tiles, members // 4)
+    align = SUB // sizes.tiles
+    cut = max(align, members // 4)
     late = Piece(far, cut, members, sizes)
     head = Piece(far, 0, cut, sizes)
     near = [Piece(k, 0, members, sizes) for k in range(1, basins // 2)]
-    across = [Piece(k, 0, members, sizes) for k in range(basins // 2, far)]
+    most = members - align
+    across = [
+        Piece(k, start, stop, sizes)
+        for k in range(basins // 2, far)
+        for start, stop in ((0, most), (most, members))
+    ]
 
     first = pack_with_codes(x, head, pltpu.with_memory_space_constraint(codes, pltpu.HBM))
     far_codes = lax.ppermute(first, "basin", pairs[far])

time: 53 us -> 60.5 us (1.14)
  waiting for transfers between devices: 19.5 us -> 25.1 us
  starting transfers between devices: 14.6 us -> 15.6 us
  Pallas kernels: 18.5 us -> 19.3 us
    ppermute x2 -> x3, waiting for transfers between devices: 9.88 us -> 15.5 us  [local(): arrived[piece] = lax.ppermute(pack(x, piece), 'basin', pairs[piece.k])]
    ppermute x2 -> x3, starting transfers between devices: 0.7 us -> 1.72 us  [local(): arrived[piece] = lax.ppermute(pack(x, piece), 'basin', pairs[piece.k])]
    pallas_call x2 -> x3, Pallas kernels: 2.11 us -> 2.93 us  [pack(): pl.pallas_call(body, out_shape=piece.shape(), in_specs=[HBM], out_specs=V...]
  transfers between devices with their start and end apart: 7 -> 8, of which waited for: 6 -> 6; matrix products, arithmetic and copies ran while one was open for 0% -> 0% of each run, Pallas kernels for 32% -> 29%
where the time goes in v10:
time: 60.5 us; the launch traced here: 60.2 us
  waiting for transfers between devices  25.1 us (41%)
  Pallas kernels  19.3 us (32%)
  starting transfers between devices  15.6 us (26%)
    ppermute x3, waiting for transfers between devices, local(): arrived[piece] = lax.ppermute(pack(x, piece), 'basin', pairs[piece.k])  15.5 us
    ppermute x3, waiting for transfers between devices, from_behind(): lax.ppermute(value, axis, [(i, (i + 1) % count) for i in range(count)])  7.41 us
    ppermute x1, starting transfers between devices, local(): far_codes = lax.ppermute(first, 'basin', pairs[far])  5.11 us
    ppermute x3, starting transfers between devices, from_behind(): lax.ppermute(value, axis, [(i, (i + 1) % count) for i in range(count)])  4.88 us
    pallas_call x2, Pallas kernels, arrived_result(): pl.pallas_call(body, out_shape=pieces[0].sizes.result(), in_specs=[VMEM]...  3.91 us
    ppermute x1, starting transfers between devices, local(): lax.ppermute(source_chunk(x, late, far_codes, inflow), 'basin', pairs[far])  3.88 us
    pallas_call x1, Pallas kernels, source_panels(): pl.pallas_call(body, out_shape=jax.ShapeDtypeStruct((starts[-1], ROWS), j...  3.33 us
    pallas_call x1, Pallas kernels, own_result(): pl.pallas_call(body, out_shape=piece.sizes.result(), in_specs=[HBM, VMEM,...  2.97 us
  transfers between devices with their start and end apart: 8, of which 6 were waited for; matrix products, arithmetic and copies ran while one was open for 0% of the time, Pallas kernels for 29%

profile of v10, /device:TPU:0, one launch (start us, length us, event | category | flops | bytes accessed | tf_op | source)
XLA Modules:
  0.0 60.2 jit_solution(4383816281315917299)
XLA Ops:
  0.0 0.9 %pack_with_codes.1 = f32[320,128]{1,0:T(8,128)S(1)} custom-call(f32[16,256,128]{2,1,0:T(8,128)} %bitcast.10, s32[64,128]{1,0:T(8,128)} %bitcast.3), custom_call_target="tpu_custom_call" | custom-call | flops 32768 | bytes 32768 | tf_op jit(solution)/shard_map/pack_with_codes/pallas_call | solution.py:154
  0.9 0.0 copy-start
  1.0 5.1 %collective-permute-start = (f32[320,128]{1,0:T(8,128)S(1)}, f32[320,128]{1,0:T(8,128)S(1)}, u32[]{:S(2)}, u32[]{:S(2)}) collective-permute-start(f32[320,128]{1,0:T(8,128)S(1)} %pack_with_codes.1), channel_id=1, source_target_pairs={{0,12},{4,8},{8,4},{12,0},{1,13},{5,9},{9,5},{13,1},{2,14},{6,10},... | collective-permute-start | bytes 491528 | tf_op jit(solution)/shard_map/ppermute | solution.py:346
  6.1 1.0 %pack.3 = f32[1024,128]{1,0:T(8,128)S(1)} custom-call(f32[16,256,128]{2,1,0:T(8,128)} %bitcast.11), custom_call_target="tpu_custom_call" | custom-call | flops 131072 | bytes 131072 | tf_op jit(solution)/shard_map/pack/pallas_call | solution.py:130
  7.1 0.1 collective-permute-start.3
  7.2 1.0 %pack.4 = f32[896,128]{1,0:T(8,128)S(1)} custom-call(f32[16,256,128]{2,1,0:T(8,128)} %bitcast.12), custom_call_target="tpu_custom_call" | custom-call | flops 114688 | bytes 114688 | tf_op jit(solution)/shard_map/pack/pallas_call | solution.py:130
  8.3 0.6 %collective-permute-start.5 = (f32[896,128]{1,0:T(8,128)S(1)}, f32[896,128]{1,0:T(8,128)S(1)}, u32[]{:S(2)}, u32[]{:S(2)}) collective-permute-start(f32[896,128]{1,0:T(8,128)S(1)} %pack.4), channel_id=1, source_target_pairs={{0,8},{4,12},{8,0},{12,4},{1,9},{5,13},{9,1},{13,5},{2,10},{6,14},... | collective-permute-start | bytes 1376264 | tf_op jit(solution)/shard_map/ppermute | solution.py:349
  8.9 2.3 %collective-permute-done.refs_0_.d_ref = f32[320,128]{1,0:T(8,128)S(1)} collective-permute-done((f32[320,128]{1,0:T(8,128)S(1)}, f32[320,128]{1,0:T(8,128)S(1)}, u32[]{:S(2)}, u32[]{:S(2)}) %collective-permute-start) | collective-permute-done | bytes 163872 | tf_op jit(solution)/shard_map/ppermute | solution.py:346
  11.1 0.0 copy-done
  11.2 3.3 %source_panels.1 = f32[112,128]{1,0:T(8,128)S(1)} custom-call(f32[16,256,128]{2,1,0:T(8,128)} %bitcast.13, f32[320,128]{1,0:T(8,128)S(1)} %collective-permute-done.refs_0_.d_ref, s32[64,128]{1,0:T(8,128)S(1)} %bitcast.4), custom_call_target="tpu_custom_call" | custom-call | flops 229376 | bytes 229376 | tf_op jit(solution)/shard_map/source_panels/pallas_call | solution.py:187
  14.5 1.8 %collective-permute-start.1 = (f32[112,128]{1,0:T(8,128)S(1)}, f32[112,128]{1,0:T(8,128)S(1)}, u32[]{:S(2)}, u32[]{:S(2)}) collective-permute-start(f32[112,128]{1,0:T(8,128)S(1)} %source_panels.1), channel_id=1, source_target_pairs={{0,2},{2,0},{1,3},{3,1},{4,6},{6,4},{5,7},{7,5},{8,10},{10,8},{9,1... | collective-permute-start | bytes 172040 | tf_op jit(solution)/shard_map/ppermute | solution.py:24
  16.3 2.5 %collective-permute-done.1.in_ref = f32[112,128]{1,0:T(8,128)S(1)} collective-permute-done((f32[112,128]{1,0:T(8,128)S(1)}, f32[112,128]{1,0:T(8,128)S(1)}, u32[]{:S(2)}, u32[]{:S(2)}) %collective-permute-start.1) | collective-permute-done | bytes 57376 | tf_op jit(solution)/shard_map/ppermute | solution.py:24
  18.7 3.0 %own_result.1.refs_4_ = f32[4096,128]{1,0:T(8,128)} custom-call(f32[16,256,128]{2,1,0:T(8,128)} %bitcast.14, s32[64,128]{1,0:T(8,128)S(1)} %bitcast.5, f32[112,128]{1,0:T(8,128)S(1)} %collective-permute-done.1.in_ref), custom_call_target="tpu_custom_call" | custom-call | flops 131072 | bytes 131072 | tf_op jit(solution)/shard_map/own_result/pallas_call | solution.py:263
  21.7 2.1 %source_chunk.1 = f32[768,128]{1,0:T(8,128)S(1)} custom-call(f32[16,256,128]{2,1,0:T(8,128)} %bitcast.15, f32[320,128]{1,0:T(8,128)S(1)} %collective-permute-done.refs_0_.d_ref, f32[112,128]{1,0:T(8,128)S(1)} %collective-permute-done.1.in_ref), custom_call_target="tpu_custom_call" | custom-call | flops 98304 | bytes 98304 | tf_op jit(solution)/shard_map/source_chunk/pallas_call | solution.py:209
  23.9 3.9 %collective-permute-start.2 = (f32[768,128]{1,0:T(8,128)S(1)}, f32[768,128]{1,0:T(8,128)S(1)}, u32[]{:S(2)}, u32[]{:S(2)}) collective-permute-start(f32[768,128]{1,0:T(8,128)S(1)} %source_chunk.1), channel_id=1, source_target_pairs={{0,12},{4,8},{8,4},{12,0},{1,13},{5,9},{9,5},{13,1},{2,14},{6,10},... | collective-permute-start | bytes 1179656 | tf_op jit(solution)/shard_map/ppermute | solution.py:359
  27.7 0.8 %pack.5 = f32[128,128]{1,0:T(8,128)S(1)} custom-call(f32[16,256,128]{2,1,0:T(8,128)} %bitcast.16), custom_call_target="tpu_custom_call" | custom-call | flops 16384 | bytes 16384 | tf_op jit(solution)/shard_map/pack/pallas_call | solution.py:130
  28.6 1.0 %collective-permute-start.6 = (f32[128,128]{1,0:T(8,128)S(1)}, f32[128,128]{1,0:T(8,128)S(1)}, u32[]{:S(2)}, u32[]{:S(2)}) collective-permute-start(f32[128,128]{1,0:T(8,128)S(1)} %pack.5), channel_id=1, source_target_pairs={{0,8},{4,12},{8,0},{12,4},{1,9},{5,13},{9,1},{13,5},{2,10},{6,14},... | collective-permute-start | bytes 196616 | tf_op jit(solution)/shard_map/ppermute | solution.py:349
  29.6 0.7 %collective-permute-done.3.refs_1_ = f32[1024,128]{1,0:T(8,128)S(1)} collective-permute-done((f32[1024,128]{1,0:T(8,128)S(1)}, f32[1024,128]{1,0:T(8,128)S(1)}, u32[]{:S(2)}, u32[]{:S(2)}) %collective-permute-start.3) | collective-permute-done | bytes 524320 | tf_op jit(solution)/shard_map/ppermute | solution.py:349
  30.3 1.2 %arrived_panels.2 = f32[80,128]{1,0:T(8,128)S(1)} custom-call(f32[320,128]{1,0:T(8,128)S(1)} %collective-permute-done.refs_0_.d_ref, f32[1024,128]{1,0:T(8,128)S(1)} %collective-permute-done.3.refs_1_, s32[64,128]{1,0:T(8,128)S(1)} %bitcast.6), custom_call_target="tpu_custom_call" | custom-call | flops 163840 | bytes 163840 | tf_op jit(solution)/shard_map/arrived_panels/pallas_call | solution.py:242
  31.4 1.6 %collective-permute-start.4 = (f32[80,128]{1,0:T(8,128)S(1)}, f32[80,128]{1,0:T(8,128)S(1)}, u32[]{:S(2)}, u32[]{:S(2)}) collective-permute-start(f32[80,128]{1,0:T(8,128)S(1)} %arrived_panels.2), channel_id=1, source_target_pairs={{0,2},{2,0},{1,3},{3,1},{4,6},{6,4},{5,7},{7,5},{8,10},{10,8},{9,1... | collective-permute-start | bytes 122888 | tf_op jit(solution)/shard_map/ppermute | solution.py:24
  33.0 2.5 %collective-permute-done.4.refs_3_ = f32[80,128]{1,0:T(8,128)S(1)} collective-permute-done((f32[80,128]{1,0:T(8,128)S(1)}, f32[80,128]{1,0:T(8,128)S(1)}, u32[]{:S(2)}, u32[]{:S(2)}) %collective-permute-start.4) | collective-permute-done | bytes 40992 | tf_op jit(solution)/shard_map/ppermute | solution.py:24
  35.5 2.0 %arrived_result.2.refs_4_ = f32[4096,128]{1,0:T(8,128)} custom-call(f32[320,128]{1,0:T(8,128)S(1)} %collective-permute-done.refs_0_.d_ref, f32[1024,128]{1,0:T(8,128)S(1)} %collective-permute-done.3.refs_1_, s32[64,128]{1,0:T(8,128)S(1)} %bitcast.7, f32[80,128]{1,0:T(8,128)S(1)} %collective-permute-done.4.refs_3_, ...), custom_call_target="tpu_custom_call", output_to_operand_aliasing={{}: (4, {})} | custom-call | flops 163840 | bytes 163840 | tf_op jit(solution)/shard_map/arrived_result/pallas_call | solution.py:290
  37.5 14.8 %collective-permute-done.6.refs_1_ = f32[128,128]{1,0:T(8,128)S(1)} collective-permute-done((f32[128,128]{1,0:T(8,128)S(1)}, f32[128,128]{1,0:T(8,128)S(1)}, u32[]{:S(2)}, u32[]{:S(2)}) %collective-permute-start.6) | collective-permute-done | bytes 65568 | tf_op jit(solution)/shard_map/ppermute | solution.py:349
  52.3 0.0 collective-permute-done.5.refs_0_
  52.3 1.2 %arrived_panels.3 = f32[64,128]{1,0:T(8,128)S(1)} custom-call(f32[896,128]{1,0:T(8,128)S(1)} %collective-permute-done.5.refs_0_, f32[128,128]{1,0:T(8,128)S(1)} %collective-permute-done.6.refs_1_, s32[64,128]{1,0:T(8,128)S(1)} %bitcast.8), custom_call_target="tpu_custom_call" | custom-call | flops 131072 | bytes 131072 | tf_op jit(solution)/shard_map/arrived_panels/pallas_call | solution.py:242
  53.5 1.6 %collective-permute-start.7 = (f32[64,128]{1,0:T(8,128)S(1)}, f32[64,128]{1,0:T(8,128)S(1)}, u32[]{:S(2)}, u32[]{:S(2)}) collective-permute-start(f32[64,128]{1,0:T(8,128)S(1)} %arrived_panels.3), channel_id=1, source_target_pairs={{0,2},{2,0},{1,3},{3,1},{4,6},{6,4},{5,7},{7,5},{8,10},{10,8},{9,1... | collective-permute-start | bytes 98312 | tf_op jit(solution)/shard_map/ppermute | solution.py:24
  55.0 2.4 %collective-permute-done.7.refs_3_ = f32[64,128]{1,0:T(8,128)S(1)} collective-permute-done((f32[64,128]{1,0:T(8,128)S(1)}, f32[64,128]{1,0:T(8,128)S(1)}, u32[]{:S(2)}, u32[]{:S(2)}) %collective-permute-start.7) | collective-permute-done | bytes 32800 | tf_op jit(solution)/shard_map/ppermute | solution.py:24
  57.5 1.9 %arrived_result.3._ = f32[4096,128]{1,0:T(8,128)} custom-call(f32[896,128]{1,0:T(8,128)S(1)} %collective-permute-done.5.refs_0_, f32[128,128]{1,0:T(8,128)S(1)} %collective-permute-done.6.refs_1_, s32[64,128]{1,0:T(8,128)S(1)} %bitcast.9, f32[64,128]{1,0:T(8,128)S(1)} %collective-permute-done.7.refs_3_, ...), custom_call_target="tpu_custom_call", output_to_operand_aliasing={{}: (4, {})} | custom-call | flops 131072 | bytes 131072 | tf_op jit(solution)/shard_map/arrived_result/pallas_call | solution.py:290
  59.4 0.0 collective-permute-done.2.x_ref
  59.4 0.8 %place_chunk.1 = f32[4096,128]{1,0:T(8,128)} custom-call(f32[768,128]{1,0:T(8,128)S(1)} %collective-permute-done.2.x_ref, f32[4096,128]{1,0:T(8,128)} %arrived_result.3._), custom_call_target="tpu_custom_call", output_to_operand_aliasing={{}: (1, {})} | custom-call | flops 98304 | bytes 98304 | tf_op jit(solution)/shard_map/place_chunk/pallas_call | solution.py:310
Async XLA Ops:
  0.9 10.2 %copy-start = (s32[4,1,2048]{2,1,0:T(1,128)S(1)}, s32[4,1,2048]{2,1,0:T(1,128)}, u32[]{:S(2)}) copy-start(s32[4,1,2048]{2,1,0:T(1,128)} %param.3) | copy-start | bytes 98308
  1.0 10.2 %collective-permute-start = (f32[320,128]{1,0:T(8,128)S(1)}, f32[320,128]{1,0:T(8,128)S(1)}, u32[]{:S(2)}, u32[]{:S(2)}) collective-permute-start(f32[320,128]{1,0:T(8,128)S(1)} %pack_with_codes.1), channel_id=1, source_target_pairs={{0,12},{4,8},{8,4},{12,0},{1,13},{5,9},{9,5},{13,1},{2,14},{6,10},... | collective-permute-start | bytes 491528 | tf_op jit(solution)/shard_map/ppermute | solution.py:346
  7.1 23.2 %collective-permute-start.3 = (f32[1024,128]{1,0:T(8,128)S(1)}, f32[1024,128]{1,0:T(8,128)S(1)}, u32[]{:S(2)}, u32[]{:S(2)}) collective-permute-start(f32[1024,128]{1,0:T(8,128)S(1)} %pack.3), channel_id=1, source_target_pairs={{0,4},{4,0},{8,12},{12,8},{1,5},{5,1},{9,13},{13,9},{2,6},{6,2},{1... | collective-permute-start | bytes 1572872 | tf_op jit(solution)/shard_map/ppermute | solution.py:349
  8.3 44.0 %collective-permute-start.5 = (f32[896,128]{1,0:T(8,128)S(1)}, f32[896,128]{1,0:T(8,128)S(1)}, u32[]{:S(2)}, u32[]{:S(2)}) collective-permute-start(f32[896,128]{1,0:T(8,128)S(1)} %pack.4), channel_id=1, source_target_pairs={{0,8},{4,12},{8,0},{12,4},{1,9},{5,13},{9,1},{13,5},{2,10},{6,14},... | collective-permute-start | bytes 1376264 | tf_op jit(solution)/shard_map/ppermute | solution.py:349
  14.5 4.2 %collective-permute-start.1 = (f32[112,128]{1,0:T(8,128)S(1)}, f32[112,128]{1,0:T(8,128)S(1)}, u32[]{:S(2)}, u32[]{:S(2)}) collective-permute-start(f32[112,128]{1,0:T(8,128)S(1)} %source_panels.1), channel_id=1, source_target_pairs={{0,2},{2,0},{1,3},{3,1},{4,6},{6,4},{5,7},{7,5},{8,10},{10,8},{9,1... | collective-permute-start | bytes 172040 | tf_op jit(solution)/shard_map/ppermute | solution.py:24
  23.9 35.5 %collective-permute-start.2 = (f32[768,128]{1,0:T(8,128)S(1)}, f32[768,128]{1,0:T(8,128)S(1)}, u32[]{:S(2)}, u32[]{:S(2)}) collective-permute-start(f32[768,128]{1,0:T(8,128)S(1)} %source_chunk.1), channel_id=1, source_target_pairs={{0,12},{4,8},{8,4},{12,0},{1,13},{5,9},{9,5},{13,1},{2,14},{6,10},... | collective-permute-start | bytes 1179656 | tf_op jit(solution)/shard_map/ppermute | solution.py:359
  28.6 23.7 %collective-permute-start.6 = (f32[128,128]{1,0:T(8,128)S(1)}, f32[128,128]{1,0:T(8,128)S(1)}, u32[]{:S(2)}, u32[]{:S(2)}) collective-permute-start(f32[128,128]{1,0:T(8,128)S(1)} %pack.5), channel_id=1, source_target_pairs={{0,8},{4,12},{8,0},{12,4},{1,9},{5,13},{9,1},{13,5},{2,10},{6,14},... | collective-permute-start | bytes 196616 | tf_op jit(solution)/shard_map/ppermute | solution.py:349
  31.4 4.1 %collective-permute-start.4 = (f32[80,128]{1,0:T(8,128)S(1)}, f32[80,128]{1,0:T(8,128)S(1)}, u32[]{:S(2)}, u32[]{:S(2)}) collective-permute-start(f32[80,128]{1,0:T(8,128)S(1)} %arrived_panels.2), channel_id=1, source_target_pairs={{0,2},{2,0},{1,3},{3,1},{4,6},{6,4},{5,7},{7,5},{8,10},{10,8},{9,1... | collective-permute-start | bytes 122888 | tf_op jit(solution)/shard_map/ppermute | solution.py:24
  53.5 4.0 %collective-permute-start.7 = (f32[64,128]{1,0:T(8,128)S(1)}, f32[64,128]{1,0:T(8,128)S(1)}, u32[]{:S(2)}, u32[]{:S(2)}) collective-permute-start(f32[64,128]{1,0:T(8,128)S(1)} %arrived_panels.3), channel_id=1, source_target_pairs={{0,2},{2,0},{1,3},{3,1},{4,6},{6,4},{5,7},{7,5},{8,10},{10,8},{9,1... | collective-permute-start | bytes 98312 | tf_op jit(solution)/shard_map/ppermute | solution.py:24

commit v11 on v9

--- a/solution.py
+++ b/solution.py
@@ -45,8 +45,24 @@
 
     def place(self, o_ref):
         sizes = self.sizes
-        start = (partner(self.k) * sizes.members + self.first) * sizes.per_member
-        return o_ref.at[pl.ds(start, self.rows)]
+        start = (partner(self.k) * sizes.members + self.first) * sizes.tiles
+        return o_ref.at[pl.ds(start, self.count)]
+
+    def leave(self, x_ref, o_ref, sem):
+        rows = x_ref.reshape(self.count, self.sizes.columns, ROWS)
+        return pltpu.make_async_copy(rows, self.place(o_ref), sem)
+
+    def leave_halves(self, x_ref, o_ref, sems):
+        rows = x_ref.reshape(self.count, self.sizes.columns, ROWS)
+        half = self.sizes.columns // 2
+        return [
+            pltpu.make_async_copy(
+                rows.at[:, pl.ds(i * half, half)],
+                self.place(o_ref).at[:, pl.ds(i * half, half)],
+                sems.at[i],
+            )
+            for i in range(2)
+        ]
 
 
 class Sizes:
@@ -55,38 +71,53 @@
         self.per_member = tiles * columns
 
     def result(self):
-        rows = self.basins * self.members * self.per_member
-        return jax.ShapeDtypeStruct((rows, ROWS), jnp.float32)
-
-
-def column_masks(d_ref, col, sizes):
+        count = self.basins * self.members * self.tiles
+        return jax.ShapeDtypeStruct((count, self.columns, ROWS), jnp.float32)
+
+
+def column_offsets(d_ref, col, sizes):
     codes = d_ref[pl.ds(col, sizes.tiles, sizes.columns), :]
     codes = jnp.concatenate([codes] * (SUB // sizes.tiles), axis=0)
     lane = lax.broadcasted_iota(jnp.int32, codes.shape, 1)
     north = (codes == 1) & (lane > 0)
     south = (codes == 2) & (lane < ROWS - 1)
-    return north, south
-
-
-def advance(summed, north, south):
+    return jnp.where(north, -1, jnp.where(south, 1, 0))
+
+
+def composed(first, second):
+    above, below = pltpu.roll(second, 1, 1), pltpu.roll(second, ROWS - 1, 1)
+    return first + jnp.where(first == 0, second, jnp.where(first < 0, above, below))
+
+
+def advance(summed, offsets, reach):
     zero = jnp.zeros_like(summed)
-    up = pltpu.roll(jnp.where(north, summed, zero), ROWS - 1, 1)
-    down = pltpu.roll(jnp.where(south, summed, zero), 1, 1)
-    return jnp.where(north | south, zero, summed) + (up + down)
-
-
-def sweep(x_ref, d_ref, carried, o_ref, sizes):
-    for col in range(sizes.columns):
-        north, south = column_masks(d_ref, col, sizes)
+    moved = jnp.where(offsets == 0, summed, zero)
+    for by in range(1, reach + 1):
+        up = pltpu.roll(jnp.where(offsets == -by, summed, zero), ROWS - by, 1)
+        down = pltpu.roll(jnp.where(offsets == by, summed, zero), by, 1)
+        moved = moved + (up + down)
+    return moved
+
+
+def sweep(x_ref, d_ref, carried, o_ref, sizes, outflow=True, halfway=None):
+    carried = list(carried)
+    for col in range(0, sizes.columns, 2):
+        first, second = (column_offsets(d_ref, c, sizes) for c in (col, col + 1))
+        both = composed(first, second)
+        last = col + 2 == sizes.columns and not outflow
         for g in range(len(carried)):
-            rows = pl.ds(g * SUB * sizes.columns + col, SUB, sizes.columns)
-            summed = x_ref[rows, :]
+            at = g * SUB * sizes.columns + col
+            here, after = pl.ds(at, SUB, sizes.columns), pl.ds(at + 1, SUB, sizes.columns)
+            summed, water = x_ref[here, :], x_ref[after, :]
             if carried[g] is not None:
                 summed = summed + carried[g]
+            if not last:
+                carried[g] = advance(water, second, 1) + advance(summed, both, 2)
             if o_ref is not None:
-                o_ref[rows, :] = summed
-            if o_ref is None or col < sizes.columns - 1:
-                carried[g] = advance(summed, north, south)
+                o_ref[here, :] = summed
+                o_ref[after, :] = water + advance(summed, first, 1)
+        if halfway is not None and col + 2 == sizes.columns // 2:
+            halfway()
     return carried
 
 
@@ -204,7 +235,7 @@
         wait_all(copies)
         size = piece.sizes.per_member
         codes_ref = d_ref.at[pl.ds(codes.shape[0] - size, size)]
-        sweep(buf, codes_ref, registers(in_ref, 0, piece), o_ref, piece.sizes)
+        sweep(buf, codes_ref, registers(in_ref, 0, piece), o_ref, piece.sizes, outflow=False)
 
     return pl.pallas_call(
         body,
@@ -231,23 +262,53 @@
 def arrived_panels(chunks, pieces, codes, inflow):
     listed, starts = len(pieces), panel_starts(pieces)
     rows = sum(piece.rows for piece in pieces)
+    kept = inflow is None
 
     def body(*refs):
-        x_refs, d_ref, o_ref = refs[:listed], refs[listed], refs[-1]
-        in_ref = refs[listed + 1] if inflow is not None else None
-        for x_ref, piece, start in zip(x_refs, pieces, starts):
+        x_refs, d_ref = refs[:listed], refs[listed]
+        in_ref = None if kept else refs[listed + 1]
+        o_ref = refs[listed + 1 + (not kept)]
+        row_refs = refs[listed + 2 :] if kept else [None] * listed
+        for x_ref, row_ref, piece, start in zip(x_refs, row_refs, pieces, starts):
             carried = registers(in_ref, start, piece)
-            store_registers(o_ref, start, sweep(x_ref, d_ref, carried, None, piece.sizes))
-
-    return pl.pallas_call(
-        body,
-        out_shape=jax.ShapeDtypeStruct((starts[-1], ROWS), jnp.float32),
-        in_specs=[VMEM] * (listed + 1 + (inflow is not None)),
-        out_specs=VMEM,
+            store_registers(o_ref, start, sweep(x_ref, d_ref, carried, row_ref, piece.sizes))
+
+    out = pl.pallas_call(
+        body,
+        out_shape=[jax.ShapeDtypeStruct((starts[-1], ROWS), jnp.float32)]
+        + [piece.shape() for piece in pieces if kept],
+        in_specs=[VMEM] * (listed + 1 + (not kept)),
+        out_specs=[VMEM] * (1 + listed * kept),
         compiler_params=params(2 * rows),
         cost_estimate=cost(rows),
         name="arrived_panels",
-    )(*chunks, codes, *([inflow] if inflow is not None else []))
+    )(*chunks, codes, *([] if kept else [inflow]))
+    return out[0], out[1:]
+
+
+def head_result(chunks, pieces, result):
+    listed = len(pieces)
+
+    def body(*refs):
+        x_refs, o_ref, sem = refs[:listed], refs[listed + 1], refs[-1]
+
+        @pl.when(lax.axis_index("chain") == 0)
+        def _():
+            copies = [piece.leave(x_refs[i], o_ref, sem.at[i]) for i, piece in enumerate(pieces)]
+            start_all(copies)
+            wait_all(copies)
+
+    return pl.pallas_call(
+        body,
+        out_shape=pieces[0].sizes.result(),
+        in_specs=[VMEM] * listed + [HBM],
+        out_specs=HBM,
+        scratch_shapes=[pltpu.SemaphoreType.DMA((listed,))],
+        input_output_aliases={listed: 0},
+        compiler_params=params(sum(piece.rows for piece in pieces)),
+        cost_estimate=cost(sum(piece.rows for piece in pieces)),
+        name="head_result",
+    )(*chunks, result)
 
 
 def own_result(x, piece, codes, inflow, start):
@@ -255,8 +316,8 @@
         copies = piece.gather(x_ref, buf, sem)
         start_all(copies)
         wait_all(copies)
-        sweep(buf, d_ref, registers(in_ref, start, piece), out, piece.sizes)
-        copy = pltpu.make_async_copy(out, piece.place(o_ref), out_sem)
+        sweep(buf, d_ref, registers(in_ref, start, piece), out, piece.sizes, outflow=False)
+        copy = piece.leave(out, o_ref, out_sem)
         copy.start()
         copy.wait()
 
@@ -280,12 +341,19 @@
     def body(*refs):
         x_refs, d_ref, in_ref, o_ref = refs[:listed], refs[listed], refs[listed + 1], refs[listed + 3]
         outs, sem = refs[listed + 4 : -1], refs[-1]
-        copies = []
-        for i, piece in enumerate(pieces):
-            sweep(x_refs[i], d_ref, registers(in_ref, starts[i], piece), outs[i], piece.sizes)
-            copies.append(pltpu.make_async_copy(outs[i], piece.place(o_ref), sem.at[i]))
-            copies[i].start()
-        wait_all(copies)
+
+        @pl.when(lax.axis_index("chain") > 0)
+        def _():
+            copies = []
+            for i, piece in enumerate(pieces):
+                halves = piece.leave_halves(outs[i], o_ref, sem.at[i])
+                carried = registers(in_ref, starts[i], piece)
+                sweep(
+                    x_refs[i], d_ref, carried, outs[i], piece.sizes, outflow=False, halfway=halves[0].start
+                )
+                halves[1].start()
+                copies += halves
+            wait_all(copies)
 
     return pl.pallas_call(
         body,
@@ -293,7 +361,7 @@
         in_specs=[VMEM] * (listed + 2) + [HBM],
         out_specs=HBM,
         scratch_shapes=[pltpu.VMEM((piece.rows, ROWS), jnp.float32) for piece in pieces]
-        + [pltpu.SemaphoreType.DMA((listed,))],
+        + [pltpu.SemaphoreType.DMA((listed, 2))],
         input_output_aliases={listed + 2: 0},
         compiler_params=params(2 * rows),
         cost_estimate=cost(rows),
@@ -303,7 +371,7 @@
 
 def place_chunk(chunk, piece, result):
     def body(x_ref, _, o_ref, sem):
-        copy = pltpu.make_async_copy(x_ref, piece.place(o_ref), sem)
+        copy = piece.leave(x_ref, o_ref, sem)
         copy.start()
         copy.wait()
 
@@ -354,11 +422,13 @@
     for group in ([head] + near, across):
         chunks = [arrived[piece] for piece in group]
         result, chunks = lax.optimization_barrier((result, chunks))
-        inflow = None
-        for _ in range(chain - 1):
-            inflow = from_behind(arrived_panels(chunks, group, codes, inflow), "chain")
-        if inflow is None:
-            inflow = jnp.zeros((panel_starts(group)[-1], ROWS), jnp.float32)
+        panel, rows = arrived_panels(chunks, group, codes, None)
+        inflow = panel
+        for step in range(chain - 1):
+            inflow = from_behind(panel, "chain")
+            if step < chain - 2:
+                panel, _ = arrived_panels(chunks, group, codes, inflow)
+        result = head_result(rows, group, result)
         result = arrived_result(chunks, group, codes, inflow, result)
     result = place_chunk(finished, late, result)
     return result.reshape(basins * members, sizes.tiles, 1, cell_count)

time: 53 us -> 50.9 us (0.960)
  Pallas kernels: 18.5 us -> 14.5 us
  waiting for transfers between devices: 19.5 us -> 21.2 us
    pallas_call x2, Pallas kernels: 3.91 us -> 0.05 us  [arrived_result(): pl.pallas_call(body, out_shape=pieces[0].sizes.result(), in_specs=[VMEM]...]
    ppermute x2, waiting for transfers between devices: 9.88 us -> 13.2 us  [local(): arrived[piece] = lax.ppermute(pack(x, piece), 'basin', pairs[piece.k])]
    ppermute x3, waiting for transfers between devices: 7.41 us -> 5.74 us  [from_behind(): lax.ppermute(value, axis, [(i, (i + 1) % count) for i in range(count)])]
    pallas_call x2 -> x4, Pallas kernels: 2.32 us -> 3.67 us  [the longest x2 2.02 us: arrived_panels(): pl.pallas_call(body, out_shape=[jax.ShapeDtypeStruct((starts[-1], ROWS),...]
    pallas_call x1, Pallas kernels: 3.33 us -> 2.58 us  [source_panels(): pl.pallas_call(body, out_shape=jax.ShapeDtypeStruct((starts[-1], ROWS), j...]
  transfers between devices with their start and end apart: 7 -> 7, of which waited for: 6 -> 6; matrix products, arithmetic and copies ran while one was open for 0% -> 0% of each run, Pallas kernels for 32% -> 25%
where the time goes in v11:
time: 50.9 us; the launch traced here: 50.4 us
  waiting for transfers between devices  21.2 us (42%)
  starting transfers between devices  14.6 us (29%)
  Pallas kernels  14.5 us (28%)
    ppermute x2, waiting for transfers between devices, local(): arrived[piece] = lax.ppermute(pack(x, piece), 'basin', pairs[piece.k])  13.2 us
    ppermute x3, waiting for transfers between devices, from_behind(): lax.ppermute(value, axis, [(i, (i + 1) % count) for i in range(count)])  5.74 us
    ppermute x1, starting transfers between devices, local(): far_codes = lax.ppermute(first, 'basin', pairs[far])  5.11 us
    ppermute x3, starting transfers between devices, from_behind(): lax.ppermute(value, axis, [(i, (i + 1) % count) for i in range(count)])  4.88 us
    ppermute x1, starting transfers between devices, local(): lax.ppermute(source_chunk(x, late, far_codes, inflow), 'basin', pairs[far])  3.88 us
    pallas_call x1, Pallas kernels, own_result(): pl.pallas_call(body, out_shape=piece.sizes.result(), in_specs=[HBM, VMEM,...  2.6 us
    pallas_call x1, Pallas kernels, source_panels(): pl.pallas_call(body, out_shape=jax.ShapeDtypeStruct((starts[-1], ROWS), j...  2.58 us
    ppermute x1, waiting for transfers between devices, local(): far_codes = lax.ppermute(first, 'basin', pairs[far])  2.24 us
  transfers between devices with their start and end apart: 7, of which 6 were waited for; matrix products, arithmetic and copies ran while one was open for 0% of the time, Pallas kernels for 25%

profile of v11, /device:TPU:0, one launch (start us, length us, event | category | flops | bytes accessed | tf_op | source)
XLA Modules:
  0.0 50.4 jit_solution(8433493190774619923)
XLA Ops:
  0.0 0.9 %pack_with_codes.1 = f32[320,128]{1,0:T(8,128)S(1)} custom-call(f32[16,256,128]{2,1,0:T(8,128)} %bitcast.10, s32[64,128]{1,0:T(8,128)} %bitcast.3), custom_call_target="tpu_custom_call" | custom-call | flops 32768 | bytes 32768 | tf_op jit(solution)/shard_map/pack_with_codes/pallas_call | solution.py:185
  0.9 0.0 copy-start
  1.0 5.1 %collective-permute-start = (f32[320,128]{1,0:T(8,128)S(1)}, f32[320,128]{1,0:T(8,128)S(1)}, u32[]{:S(2)}, u32[]{:S(2)}) collective-permute-start(f32[320,128]{1,0:T(8,128)S(1)} %pack_with_codes.1), channel_id=1, source_target_pairs={{0,12},{4,8},{8,4},{12,0},{1,13},{5,9},{9,5},{13,1},{2,14},{6,10},... | collective-permute-start | bytes 491528 | tf_op jit(solution)/shard_map/ppermute | solution.py:408
  6.1 1.0 %pack.2 = f32[1024,128]{1,0:T(8,128)S(1)} custom-call(f32[16,256,128]{2,1,0:T(8,128)} %bitcast.11), custom_call_target="tpu_custom_call" | custom-call | flops 131072 | bytes 131072 | tf_op jit(solution)/shard_map/pack/pallas_call | solution.py:161
  7.1 0.1 collective-permute-start.3
  7.2 1.1 %pack.3 = f32[1024,128]{1,0:T(8,128)S(1)} custom-call(f32[16,256,128]{2,1,0:T(8,128)} %bitcast.12), custom_call_target="tpu_custom_call" | custom-call | flops 131072 | bytes 131072 | tf_op jit(solution)/shard_map/pack/pallas_call | solution.py:161
  8.3 0.6 %collective-permute-start.5 = (f32[1024,128]{1,0:T(8,128)S(1)}, f32[1024,128]{1,0:T(8,128)S(1)}, u32[]{:S(2)}, u32[]{:S(2)}) collective-permute-start(f32[1024,128]{1,0:T(8,128)S(1)} %pack.3), channel_id=1, source_target_pairs={{0,8},{4,12},{8,0},{12,4},{1,9},{5,13},{9,1},{13,5},{2,10},{6,14},... | collective-permute-start | bytes 1572872 | tf_op jit(solution)/shard_map/ppermute | solution.py:411
  8.9 2.2 %collective-permute-done.refs_0_.d_ref = f32[320,128]{1,0:T(8,128)S(1)} collective-permute-done((f32[320,128]{1,0:T(8,128)S(1)}, f32[320,128]{1,0:T(8,128)S(1)}, u32[]{:S(2)}, u32[]{:S(2)}) %collective-permute-start) | collective-permute-done | bytes 163872 | tf_op jit(solution)/shard_map/ppermute | solution.py:408
  11.1 0.0 copy-done
  11.2 2.6 %source_panels.1 = f32[112,128]{1,0:T(8,128)S(1)} custom-call(f32[16,256,128]{2,1,0:T(8,128)} %bitcast.13, f32[320,128]{1,0:T(8,128)S(1)} %collective-permute-done.refs_0_.d_ref, s32[64,128]{1,0:T(8,128)S(1)} %bitcast.4), custom_call_target="tpu_custom_call" | custom-call | flops 229376 | bytes 229376 | tf_op jit(solution)/shard_map/source_panels/pallas_call | solution.py:218
  13.7 1.8 %collective-permute-start.1 = (f32[112,128]{1,0:T(8,128)S(1)}, f32[112,128]{1,0:T(8,128)S(1)}, u32[]{:S(2)}, u32[]{:S(2)}) collective-permute-start(f32[112,128]{1,0:T(8,128)S(1)} %source_panels.1), channel_id=1, source_target_pairs={{0,2},{2,0},{1,3},{3,1},{4,6},{6,4},{5,7},{7,5},{8,10},{10,8},{9,1... | collective-permute-start | bytes 172040 | tf_op jit(solution)/shard_map/ppermute | solution.py:24
  15.5 2.5 %collective-permute-done.1.in_ref = f32[112,128]{1,0:T(8,128)S(1)} collective-permute-done((f32[112,128]{1,0:T(8,128)S(1)}, f32[112,128]{1,0:T(8,128)S(1)}, u32[]{:S(2)}, u32[]{:S(2)}) %collective-permute-start.1) | collective-permute-done | bytes 57376 | tf_op jit(solution)/shard_map/ppermute | solution.py:24
  18.0 2.6 %own_result.1.refs_2_ = f32[256,16,128]{2,1,0:T(8,128)} custom-call(f32[16,256,128]{2,1,0:T(8,128)} %bitcast.14, s32[64,128]{1,0:T(8,128)S(1)} %bitcast.5, f32[112,128]{1,0:T(8,128)S(1)} %collective-permute-done.1.in_ref), custom_call_target="tpu_custom_call" | custom-call | flops 131072 | bytes 131072 | tf_op jit(solution)/shard_map/own_result/pallas_call | solution.py:324
  20.6 1.8 %source_chunk.1 = f32[768,128]{1,0:T(8,128)S(1)} custom-call(f32[16,256,128]{2,1,0:T(8,128)} %bitcast.15, f32[320,128]{1,0:T(8,128)S(1)} %collective-permute-done.refs_0_.d_ref, f32[112,128]{1,0:T(8,128)S(1)} %collective-permute-done.1.in_ref), custom_call_target="tpu_custom_call" | custom-call | flops 98304 | bytes 98304 | tf_op jit(solution)/shard_map/source_chunk/pallas_call | solution.py:240
  22.4 3.9 %collective-permute-start.2 = (f32[768,128]{1,0:T(8,128)S(1)}, f32[768,128]{1,0:T(8,128)S(1)}, u32[]{:S(2)}, u32[]{:S(2)}) collective-permute-start(f32[768,128]{1,0:T(8,128)S(1)} %source_chunk.1), channel_id=1, source_target_pairs={{0,12},{4,8},{8,4},{12,0},{1,13},{5,9},{9,5},{13,1},{2,14},{6,10},... | collective-permute-start | bytes 1179656 | tf_op jit(solution)/shard_map/ppermute | solution.py:421
  26.3 4.0 %collective-permute-done.3.refs_1_ = f32[1024,128]{1,0:T(8,128)S(1)} collective-permute-done((f32[1024,128]{1,0:T(8,128)S(1)}, f32[1024,128]{1,0:T(8,128)S(1)}, u32[]{:S(2)}, u32[]{:S(2)}) %collective-permute-start.3) | collective-permute-done | bytes 524320 | tf_op jit(solution)/shard_map/ppermute | solution.py:411
  30.3 1.3 %arrived_panels.2 = (f32[80,128]{1,0:T(8,128)S(1)}, f32[256,128]{1,0:T(8,128)S(1)}, f32[1024,128]{1,0:T(8,128)S(1)}) custom-call(f32[320,128]{1,0:T(8,128)S(1)} %collective-permute-done.refs_0_.d_ref, f32[1024,128]{1,0:T(8,128)S(1)} %collective-permute-done.3.refs_1_, s32[64,128]{1,0:T(8,128)S(1)} %bitcast.6), custom_call_target="tpu_custom_call" | custom-call | flops 163840 | bytes 163840 | tf_op jit(solution)/shard_map/arrived_panels/pallas_call | solution.py:276
  31.6 1.6 %collective-permute-start.4 = (f32[80,128]{1,0:T(8,128)S(1)}, f32[80,128]{1,0:T(8,128)S(1)}, u32[]{:S(2)}, u32[]{:S(2)}) collective-permute-start(f32[80,128]{1,0:T(8,128)S(1)} %get-tuple-element.21), channel_id=1, source_target_pairs={{0,2},{2,0},{1,3},{3,1},{4,6},{6,4},{5,7},{7,5},{8,10},{10,8},{9,1... | collective-permute-start | bytes 122888 | tf_op jit(solution)/shard_map/ppermute | solution.py:24
  33.1 0.9 %head_result.2.refs_4_ = f32[256,16,128]{2,1,0:T(8,128)} custom-call(f32[256,128]{1,0:T(8,128)S(1)} %get-tuple-element.22.refs_0_, f32[1024,128]{1,0:T(8,128)S(1)} %get-tuple-element.23.refs_1_, f32[256,16,128]{2,1,0:T(8,128)} %own_result.1.refs_2_), custom_call_target="tpu_custom_call", output_to_operand_aliasing={{}: (2, {})} | custom-call | flops 163840 | bytes 163840 | tf_op jit(solution)/shard_map/head_result/pallas_call | solution.py:301
  34.0 1.6 %collective-permute-done.4.refs_3_ = f32[80,128]{1,0:T(8,128)S(1)} collective-permute-done((f32[80,128]{1,0:T(8,128)S(1)}, f32[80,128]{1,0:T(8,128)S(1)}, u32[]{:S(2)}, u32[]{:S(2)}) %collective-permute-start.4) | collective-permute-done | bytes 40992 | tf_op jit(solution)/shard_map/ppermute | solution.py:24
  35.7 9.2 %collective-permute-done.5.refs_0_ = f32[1024,128]{1,0:T(8,128)S(1)} collective-permute-done((f32[1024,128]{1,0:T(8,128)S(1)}, f32[1024,128]{1,0:T(8,128)S(1)}, u32[]{:S(2)}, u32[]{:S(2)}) %collective-permute-start.5) | collective-permute-done | bytes 524320 | tf_op jit(solution)/shard_map/ppermute | solution.py:411
  44.8 0.7 %arrived_panels.3 = (f32[64,128]{1,0:T(8,128)S(1)}, f32[1024,128]{1,0:T(8,128)S(1)}) custom-call(f32[1024,128]{1,0:T(8,128)S(1)} %collective-permute-done.5.refs_0_, s32[64,128]{1,0:T(8,128)S(1)} %bitcast.8), custom_call_target="tpu_custom_call" | custom-call | flops 131072 | bytes 131072 | tf_op jit(solution)/shard_map/arrived_panels/pallas_call | solution.py:276
  45.6 1.6 %collective-permute-start.6 = (f32[64,128]{1,0:T(8,128)S(1)}, f32[64,128]{1,0:T(8,128)S(1)}, u32[]{:S(2)}, u32[]{:S(2)}) collective-permute-start(f32[64,128]{1,0:T(8,128)S(1)} %get-tuple-element.26), channel_id=1, source_target_pairs={{0,2},{2,0},{1,3},{3,1},{4,6},{6,4},{5,7},{7,5},{8,10},{10,8},{9,1... | collective-permute-start | bytes 98312 | tf_op jit(solution)/shard_map/ppermute | solution.py:24
  47.1 0.8 %head_result.3.refs_3_ = f32[256,16,128]{2,1,0:T(8,128)} custom-call(f32[1024,128]{1,0:T(8,128)S(1)} %get-tuple-element.27.refs_0_, f32[256,16,128]{2,1,0:T(8,128)} %arrived_result.2.refs_1_), custom_call_target="tpu_custom_call", output_to_operand_aliasing={{}: (1, {})} | custom-call | flops 131072 | bytes 131072 | tf_op jit(solution)/shard_map/head_result/pallas_call | solution.py:301
  47.9 1.6 %collective-permute-done.6.refs_2_ = f32[64,128]{1,0:T(8,128)S(1)} collective-permute-done((f32[64,128]{1,0:T(8,128)S(1)}, f32[64,128]{1,0:T(8,128)S(1)}, u32[]{:S(2)}, u32[]{:S(2)}) %collective-permute-start.6) | collective-permute-done | bytes 32800 | tf_op jit(solution)/shard_map/ppermute | solution.py:24
  49.6 0.0 collective-permute-done.2.x_ref
  49.6 0.8 %place_chunk.1 = f32[256,16,128]{2,1,0:T(8,128)} custom-call(f32[768,128]{1,0:T(8,128)S(1)} %collective-permute-done.2.x_ref, f32[256,16,128]{2,1,0:T(8,128)} %arrived_result.3._), custom_call_target="tpu_custom_call", output_to_operand_aliasing={{}: (1, {})} | custom-call | flops 98304 | bytes 98304 | tf_op jit(solution)/shard_map/place_chunk/pallas_call | solution.py:378
  (2 shorter events, 0.1 us)
Async XLA Ops:
  0.9 10.2 %copy-start = (s32[4,1,2048]{2,1,0:T(1,128)S(1)}, s32[4,1,2048]{2,1,0:T(1,128)}, u32[]{:S(2)}) copy-start(s32[4,1,2048]{2,1,0:T(1,128)} %param.3) | copy-start | bytes 98308
  1.0 10.2 %collective-permute-start = (f32[320,128]{1,0:T(8,128)S(1)}, f32[320,128]{1,0:T(8,128)S(1)}, u32[]{:S(2)}, u32[]{:S(2)}) collective-permute-start(f32[320,128]{1,0:T(8,128)S(1)} %pack_with_codes.1), channel_id=1, source_target_pairs={{0,12},{4,8},{8,4},{12,0},{1,13},{5,9},{9,5},{13,1},{2,14},{6,10},... | collective-permute-start | bytes 491528 | tf_op jit(solution)/shard_map/ppermute | solution.py:408
  7.1 23.2 %collective-permute-start.3 = (f32[1024,128]{1,0:T(8,128)S(1)}, f32[1024,128]{1,0:T(8,128)S(1)}, u32[]{:S(2)}, u32[]{:S(2)}) collective-permute-start(f32[1024,128]{1,0:T(8,128)S(1)} %pack.2), channel_id=1, source_target_pairs={{0,4},{4,0},{8,12},{12,8},{1,5},{5,1},{9,13},{13,9},{2,6},{6,2},{1... | collective-permute-start | bytes 1572872 | tf_op jit(solution)/shard_map/ppermute | solution.py:411
  8.3 36.6 %collective-permute-start.5 = (f32[1024,128]{1,0:T(8,128)S(1)}, f32[1024,128]{1,0:T(8,128)S(1)}, u32[]{:S(2)}, u32[]{:S(2)}) collective-permute-start(f32[1024,128]{1,0:T(8,128)S(1)} %pack.3), channel_id=1, source_target_pairs={{0,8},{4,12},{8,0},{12,4},{1,9},{5,13},{9,1},{13,5},{2,10},{6,14},... | collective-permute-start | bytes 1572872 | tf_op jit(solution)/shard_map/ppermute | solution.py:411
  13.7 4.2 %collective-permute-start.1 = (f32[112,128]{1,0:T(8,128)S(1)}, f32[112,128]{1,0:T(8,128)S(1)}, u32[]{:S(2)}, u32[]{:S(2)}) collective-permute-start(f32[112,128]{1,0:T(8,128)S(1)} %source_panels.1), channel_id=1, source_target_pairs={{0,2},{2,0},{1,3},{3,1},{4,6},{6,4},{5,7},{7,5},{8,10},{10,8},{9,1... | collective-permute-start | bytes 172040 | tf_op jit(solution)/shard_map/ppermute | solution.py:24
  22.4 27.2 %collective-permute-start.2 = (f32[768,128]{1,0:T(8,128)S(1)}, f32[768,128]{1,0:T(8,128)S(1)}, u32[]{:S(2)}, u32[]{:S(2)}) collective-permute-start(f32[768,128]{1,0:T(8,128)S(1)} %source_chunk.1), channel_id=1, source_target_pairs={{0,12},{4,8},{8,4},{12,0},{1,13},{5,9},{9,5},{13,1},{2,14},{6,10},... | collective-permute-start | bytes 1179656 | tf_op jit(solution)/shard_map/ppermute | solution.py:421
  31.6 4.1 %collective-permute-start.4 = (f32[80,128]{1,0:T(8,128)S(1)}, f32[80,128]{1,0:T(8,128)S(1)}, u32[]{:S(2)}, u32[]{:S(2)}) collective-permute-start(f32[80,128]{1,0:T(8,128)S(1)} %get-tuple-element.21), channel_id=1, source_target_pairs={{0,2},{2,0},{1,3},{3,1},{4,6},{6,4},{5,7},{7,5},{8,10},{10,8},{9,1... | collective-permute-start | bytes 122888 | tf_op jit(solution)/shard_map/ppermute | solution.py:24
  45.6 4.0 %collective-permute-start.6 = (f32[64,128]{1,0:T(8,128)S(1)}, f32[64,128]{1,0:T(8,128)S(1)}, u32[]{:S(2)}, u32[]{:S(2)}) collective-permute-start(f32[64,128]{1,0:T(8,128)S(1)} %get-tuple-element.26), channel_id=1, source_target_pairs={{0,2},{2,0},{1,3},{3,1},{4,6},{6,4},{5,7},{7,5},{8,10},{10,8},{9,1... | collective-permute-start | bytes 98312 | tf_op jit(solution)/shard_map/ppermute | solution.py:24

commit v12 on v11

--- a/solution.py
+++ b/solution.py
@@ -170,13 +170,14 @@
     )(x)
 
 
-def pack_with_codes(x, piece, codes):
-    code_rows = codes.shape[0]
-
+def pack_with_codes(x, piece, codes, code_rows):
     def body(x_ref, d_ref, o_ref, buf, sem, code_sem):
         copies = piece.gather(x_ref, o_ref, sem)
         start_all(copies)
-        copy = pltpu.make_async_copy(d_ref, buf, code_sem)
+        shares = codes.shape[0] // code_rows
+        share = lax.axis_index("mem") if shares > 1 else 0
+        mine = d_ref.at[pl.ds(pl.multiple_of(share * code_rows, code_rows), code_rows)]
+        copy = pltpu.make_async_copy(mine, buf, code_sem)
         copy.start()
         copy.wait()
         o_ref[pl.ds(piece.rows, code_rows), :] = buf[...].astype(jnp.float32)
@@ -188,7 +189,7 @@
         in_specs=[HBM, HBM],
         out_specs=VMEM,
         scratch_shapes=[
-            pltpu.VMEM(codes.shape, codes.dtype),
+            pltpu.VMEM((code_rows, ROWS), codes.dtype),
             pltpu.SemaphoreType.DMA,
             pltpu.SemaphoreType.DMA,
         ],
@@ -404,9 +405,11 @@
     near = [Piece(k, 0, members, sizes) for k in range(1, basins // 2)]
     across = [Piece(k, 0, members, sizes) for k in range(basins // 2, far)]
 
-    first = pack_with_codes(x, head, pltpu.with_memory_space_constraint(codes, pltpu.HBM))
-    far_codes = lax.ppermute(first, "basin", pairs[far])
-    arrived = {head: far_codes}
+    code_rows = sizes.per_member // lax.axis_size("mem")
+    pinned = pltpu.with_memory_space_constraint(codes, pltpu.HBM)
+    first = lax.ppermute(pack_with_codes(x, head, pinned, code_rows), "basin", pairs[far])
+    arrived = {head: first}
+    far_codes = lax.all_gather(first[head.rows :], "mem", axis=0, tiled=True)
     for piece in across + near:
         arrived[piece] = lax.ppermute(pack(x, piece), "basin", pairs[piece.k])
 

time: 50.9 us -> 50.2 us (0.986)
  waiting for transfers between devices: 21.2 us -> 18.3 us
  blocking collectives: 0 us -> 1.82 us
    ppermute x2, waiting for transfers between devices: 13.2 us -> 10.8 us  [local(): arrived[piece] = lax.ppermute(pack(x, piece), 'basin', pairs[piece.k])]
    all_gather x0 -> x1, blocking collectives: none -> 1.82 us  [local(): far_codes = lax.all_gather(first[head.rows:], 'mem', axis=0, tiled=True)]
  transfers between devices with their start and end apart: 7 -> 7, of which waited for: 6 -> 6; matrix products, arithmetic and copies ran while one was open for 0% -> 0% of each run, Pallas kernels for 25% -> 26%
where the time goes in v12:
time: 50.2 us; the launch traced here: 49.5 us
  waiting for transfers between devices  18.3 us (36%)
  starting transfers between devices  14.7 us (29%)
  Pallas kernels  14.5 us (29%)
  blocking collectives  1.82 us (4%)
    ppermute x2, waiting for transfers between devices, local(): arrived[piece] = lax.ppermute(pack(x, piece), 'basin', pairs[piece.k])  10.8 us
    ppermute x3, waiting for transfers between devices, from_behind(): lax.ppermute(value, axis, [(i, (i + 1) % count) for i in range(count)])  5.64 us
    ppermute x1, starting transfers between devices, local(): lax.ppermute(pack_with_codes(x, head, pinned, code_rows), 'basin', pairs[...  5.11 us
    ppermute x3, starting transfers between devices, from_behind(): lax.ppermute(value, axis, [(i, (i + 1) % count) for i in range(count)])  4.98 us
    ppermute x1, starting transfers between devices, local(): lax.ppermute(source_chunk(x, late, far_codes, inflow), 'basin', pairs[far])  3.88 us
    pallas_call x1, Pallas kernels, own_result(): pl.pallas_call(body, out_shape=piece.sizes.result(), in_specs=[HBM, VMEM,...  2.6 us
    pallas_call x1, Pallas kernels, source_panels(): pl.pallas_call(body, out_shape=jax.ShapeDtypeStruct((starts[-1], ROWS), j...  2.58 us
    pallas_call x2, Pallas kernels, pack(): pl.pallas_call(body, out_shape=piece.shape(), in_specs=[HBM], out_specs=V...  2.11 us
  transfers between devices with their start and end apart: 7, of which 6 were waited for; matrix products, arithmetic and copies ran while one was open for 0% of the time, Pallas kernels for 26%

profile of v12, /device:TPU:0, one launch (start us, length us, event | category | flops | bytes accessed | tf_op | source)
XLA Modules:
  0.0 49.5 jit_solution(11096921429354615864)
XLA Ops:
  0.0 0.9 %pack_with_codes.1 = f32[288,128]{1,0:T(8,128)S(1)} custom-call(f32[16,256,128]{2,1,0:T(8,128)} %bitcast.10, s32[64,128]{1,0:T(8,128)} %bitcast.3), custom_call_target="tpu_custom_call" | custom-call | flops 32768 | bytes 32768 | tf_op jit(solution)/shard_map/pack_with_codes/pallas_call | solution.py:186
  0.9 0.0 copy-start
  1.0 5.1 %collective-permute-start = (f32[288,128]{1,0:T(8,128)S(1)}, f32[288,128]{1,0:T(8,128)S(1)}, u32[]{:S(2)}, u32[]{:S(2)}) collective-permute-start(f32[288,128]{1,0:T(8,128)S(1)} %pack_with_codes.1), channel_id=1, source_target_pairs={{0,12},{4,8},{8,4},{12,0},{1,13},{5,9},{9,5},{13,1},{2,14},{6,10},... | collective-permute-start | bytes 442376 | tf_op jit(solution)/shard_map/ppermute | solution.py:410
  6.1 1.0 %pack.2 = f32[1024,128]{1,0:T(8,128)S(1)} custom-call(f32[16,256,128]{2,1,0:T(8,128)} %bitcast.11), custom_call_target="tpu_custom_call" | custom-call | flops 131072 | bytes 131072 | tf_op jit(solution)/shard_map/pack/pallas_call | solution.py:161
  7.1 0.1 collective-permute-start.3
  7.2 1.1 %pack.3 = f32[1024,128]{1,0:T(8,128)S(1)} custom-call(f32[16,256,128]{2,1,0:T(8,128)} %bitcast.12), custom_call_target="tpu_custom_call" | custom-call | flops 131072 | bytes 131072 | tf_op jit(solution)/shard_map/pack/pallas_call | solution.py:161
  8.3 0.6 %collective-permute-start.5 = (f32[1024,128]{1,0:T(8,128)S(1)}, f32[1024,128]{1,0:T(8,128)S(1)}, u32[]{:S(2)}, u32[]{:S(2)}) collective-permute-start(f32[1024,128]{1,0:T(8,128)S(1)} %pack.3), channel_id=1, source_target_pairs={{0,8},{4,12},{8,0},{12,4},{1,9},{5,13},{9,1},{13,5},{2,10},{6,14},... | collective-permute-start | bytes 1572872 | tf_op jit(solution)/shard_map/ppermute | solution.py:414
  8.9 1.9 %collective-permute-done.refs_0_ = f32[288,128]{1,0:T(8,128)S(1)} collective-permute-done((f32[288,128]{1,0:T(8,128)S(1)}, f32[288,128]{1,0:T(8,128)S(1)}, u32[]{:S(2)}, u32[]{:S(2)}) %collective-permute-start) | collective-permute-done | bytes 147488 | tf_op jit(solution)/shard_map/ppermute | solution.py:410
  10.8 1.8 %all_gather.3.refs_0_.d_ref = f32[64,128]{1,0:T(8,128)S(1)} all-gather(f32[32,128]{1,0:T(8,128)S(1)} %slice.4), channel_id=1, replica_groups=mesh['grp'=2,'basin'=4,'chain'=2,'mem'=2] {'mem'}, dimensions={0}, use_global_device_ids=true | all-gather | bytes 49152 | tf_op jit(solution)/shard_map/all_gather | solution.py:412
  12.6 0.0 copy-done
  12.6 2.6 %source_panels.1 = f32[112,128]{1,0:T(8,128)S(1)} custom-call(f32[16,256,128]{2,1,0:T(8,128)} %bitcast.13, f32[64,128]{1,0:T(8,128)S(1)} %all_gather.3.refs_0_.d_ref, s32[64,128]{1,0:T(8,128)S(1)} %bitcast.4), custom_call_target="tpu_custom_call" | custom-call | flops 229376 | bytes 229376 | tf_op jit(solution)/shard_map/source_panels/pallas_call | solution.py:219
  15.2 1.8 %collective-permute-start.1 = (f32[112,128]{1,0:T(8,128)S(1)}, f32[112,128]{1,0:T(8,128)S(1)}, u32[]{:S(2)}, u32[]{:S(2)}) collective-permute-start(f32[112,128]{1,0:T(8,128)S(1)} %source_panels.1), channel_id=1, source_target_pairs={{0,2},{2,0},{1,3},{3,1},{4,6},{6,4},{5,7},{7,5},{8,10},{10,8},{9,1... | collective-permute-start | bytes 172040 | tf_op jit(solution)/shard_map/ppermute | solution.py:24
  17.0 2.5 %collective-permute-done.1.in_ref = f32[112,128]{1,0:T(8,128)S(1)} collective-permute-done((f32[112,128]{1,0:T(8,128)S(1)}, f32[112,128]{1,0:T(8,128)S(1)}, u32[]{:S(2)}, u32[]{:S(2)}) %collective-permute-start.1) | collective-permute-done | bytes 57376 | tf_op jit(solution)/shard_map/ppermute | solution.py:24
  19.4 2.6 %own_result.1.refs_2_ = f32[256,16,128]{2,1,0:T(8,128)} custom-call(f32[16,256,128]{2,1,0:T(8,128)} %bitcast.14, s32[64,128]{1,0:T(8,128)S(1)} %bitcast.5, f32[112,128]{1,0:T(8,128)S(1)} %collective-permute-done.1.in_ref), custom_call_target="tpu_custom_call" | custom-call | flops 131072 | bytes 131072 | tf_op jit(solution)/shard_map/own_result/pallas_call | solution.py:325
  22.1 1.8 %source_chunk.1 = f32[768,128]{1,0:T(8,128)S(1)} custom-call(f32[16,256,128]{2,1,0:T(8,128)} %bitcast.15, f32[64,128]{1,0:T(8,128)S(1)} %all_gather.3.refs_0_.d_ref, f32[112,128]{1,0:T(8,128)S(1)} %collective-permute-done.1.in_ref), custom_call_target="tpu_custom_call" | custom-call | flops 98304 | bytes 98304 | tf_op jit(solution)/shard_map/source_chunk/pallas_call | solution.py:241
  23.8 3.9 %collective-permute-start.2 = (f32[768,128]{1,0:T(8,128)S(1)}, f32[768,128]{1,0:T(8,128)S(1)}, u32[]{:S(2)}, u32[]{:S(2)}) collective-permute-start(f32[768,128]{1,0:T(8,128)S(1)} %source_chunk.1), channel_id=1, source_target_pairs={{0,12},{4,8},{8,4},{12,0},{1,13},{5,9},{9,5},{13,1},{2,14},{6,10},... | collective-permute-start | bytes 1179656 | tf_op jit(solution)/shard_map/ppermute | solution.py:424
  27.7 2.6 %collective-permute-done.3.refs_1_ = f32[1024,128]{1,0:T(8,128)S(1)} collective-permute-done((f32[1024,128]{1,0:T(8,128)S(1)}, f32[1024,128]{1,0:T(8,128)S(1)}, u32[]{:S(2)}, u32[]{:S(2)}) %collective-permute-start.3) | collective-permute-done | bytes 524320 | tf_op jit(solution)/shard_map/ppermute | solution.py:414
  30.3 1.3 %arrived_panels.2 = (f32[80,128]{1,0:T(8,128)S(1)}, f32[256,128]{1,0:T(8,128)S(1)}, f32[1024,128]{1,0:T(8,128)S(1)}) custom-call(f32[288,128]{1,0:T(8,128)S(1)} %collective-permute-done.refs_0_, f32[1024,128]{1,0:T(8,128)S(1)} %collective-permute-done.3.refs_1_, s32[64,128]{1,0:T(8,128)S(1)} %bitcast.6), custom_call_target="tpu_custom_call" | custom-call | flops 163840 | bytes 163840 | tf_op jit(solution)/shard_map/arrived_panels/pallas_call | solution.py:277
  31.6 1.7 %collective-permute-start.4 = (f32[80,128]{1,0:T(8,128)S(1)}, f32[80,128]{1,0:T(8,128)S(1)}, u32[]{:S(2)}, u32[]{:S(2)}) collective-permute-start(f32[80,128]{1,0:T(8,128)S(1)} %get-tuple-element.21), channel_id=1, source_target_pairs={{0,2},{2,0},{1,3},{3,1},{4,6},{6,4},{5,7},{7,5},{8,10},{10,8},{9,1... | collective-permute-start | bytes 122888 | tf_op jit(solution)/shard_map/ppermute | solution.py:24
  33.3 0.9 %head_result.2.refs_4_ = f32[256,16,128]{2,1,0:T(8,128)} custom-call(f32[256,128]{1,0:T(8,128)S(1)} %get-tuple-element.22.refs_0_, f32[1024,128]{1,0:T(8,128)S(1)} %get-tuple-element.23.refs_1_, f32[256,16,128]{2,1,0:T(8,128)} %own_result.1.refs_2_), custom_call_target="tpu_custom_call", output_to_operand_aliasing={{}: (2, {})} | custom-call | flops 163840 | bytes 163840 | tf_op jit(solution)/shard_map/head_result/pallas_call | solution.py:302
  34.1 1.5 %collective-permute-done.4.refs_3_ = f32[80,128]{1,0:T(8,128)S(1)} collective-permute-done((f32[80,128]{1,0:T(8,128)S(1)}, f32[80,128]{1,0:T(8,128)S(1)}, u32[]{:S(2)}, u32[]{:S(2)}) %collective-permute-start.4) | collective-permute-done | bytes 40992 | tf_op jit(solution)/shard_map/ppermute | solution.py:24
  35.7 8.2 %collective-permute-done.5.refs_0_ = f32[1024,128]{1,0:T(8,128)S(1)} collective-permute-done((f32[1024,128]{1,0:T(8,128)S(1)}, f32[1024,128]{1,0:T(8,128)S(1)}, u32[]{:S(2)}, u32[]{:S(2)}) %collective-permute-start.5) | collective-permute-done | bytes 524320 | tf_op jit(solution)/shard_map/ppermute | solution.py:414
  43.9 0.7 %arrived_panels.3 = (f32[64,128]{1,0:T(8,128)S(1)}, f32[1024,128]{1,0:T(8,128)S(1)}) custom-call(f32[1024,128]{1,0:T(8,128)S(1)} %collective-permute-done.5.refs_0_, s32[64,128]{1,0:T(8,128)S(1)} %bitcast.8), custom_call_target="tpu_custom_call" | custom-call | flops 131072 | bytes 131072 | tf_op jit(solution)/shard_map/arrived_panels/pallas_call | solution.py:277
  44.7 1.6 %collective-permute-start.6 = (f32[64,128]{1,0:T(8,128)S(1)}, f32[64,128]{1,0:T(8,128)S(1)}, u32[]{:S(2)}, u32[]{:S(2)}) collective-permute-start(f32[64,128]{1,0:T(8,128)S(1)} %get-tuple-element.26), channel_id=1, source_target_pairs={{0,2},{2,0},{1,3},{3,1},{4,6},{6,4},{5,7},{7,5},{8,10},{10,8},{9,1... | collective-permute-start | bytes 98312 | tf_op jit(solution)/shard_map/ppermute | solution.py:24
  46.3 0.8 %head_result.3.refs_3_ = f32[256,16,128]{2,1,0:T(8,128)} custom-call(f32[1024,128]{1,0:T(8,128)S(1)} %get-tuple-element.27.refs_0_, f32[256,16,128]{2,1,0:T(8,128)} %arrived_result.2.refs_1_), custom_call_target="tpu_custom_call", output_to_operand_aliasing={{}: (1, {})} | custom-call | flops 131072 | bytes 131072 | tf_op jit(solution)/shard_map/head_result/pallas_call | solution.py:302
  47.1 1.6 %collective-permute-done.6.refs_2_ = f32[64,128]{1,0:T(8,128)S(1)} collective-permute-done((f32[64,128]{1,0:T(8,128)S(1)}, f32[64,128]{1,0:T(8,128)S(1)}, u32[]{:S(2)}, u32[]{:S(2)}) %collective-permute-start.6) | collective-permute-done | bytes 32800 | tf_op jit(solution)/shard_map/ppermute | solution.py:24
  48.7 0.0 collective-permute-done.2.x_ref
  48.7 0.8 %place_chunk.1 = f32[256,16,128]{2,1,0:T(8,128)} custom-call(f32[768,128]{1,0:T(8,128)S(1)} %collective-permute-done.2.x_ref, f32[256,16,128]{2,1,0:T(8,128)} %arrived_result.3._), custom_call_target="tpu_custom_call", output_to_operand_aliasing={{}: (1, {})} | custom-call | flops 98304 | bytes 98304 | tf_op jit(solution)/shard_map/place_chunk/pallas_call | solution.py:379
  (3 shorter events, 0.1 us)
Async XLA Ops:
  0.9 11.7 %copy-start = (s32[4,1,2048]{2,1,0:T(1,128)S(1)}, s32[4,1,2048]{2,1,0:T(1,128)}, u32[]{:S(2)}) copy-start(s32[4,1,2048]{2,1,0:T(1,128)} %param.3) | copy-start | bytes 98308
  1.0 9.8 %collective-permute-start = (f32[288,128]{1,0:T(8,128)S(1)}, f32[288,128]{1,0:T(8,128)S(1)}, u32[]{:S(2)}, u32[]{:S(2)}) collective-permute-start(f32[288,128]{1,0:T(8,128)S(1)} %pack_with_codes.1), channel_id=1, source_target_pairs={{0,12},{4,8},{8,4},{12,0},{1,13},{5,9},{9,5},{13,1},{2,14},{6,10},... | collective-permute-start | bytes 442376 | tf_op jit(solution)/shard_map/ppermute | solution.py:410
  7.1 23.2 %collective-permute-start.3 = (f32[1024,128]{1,0:T(8,128)S(1)}, f32[1024,128]{1,0:T(8,128)S(1)}, u32[]{:S(2)}, u32[]{:S(2)}) collective-permute-start(f32[1024,128]{1,0:T(8,128)S(1)} %pack.2), channel_id=1, source_target_pairs={{0,4},{4,0},{8,12},{12,8},{1,5},{5,1},{9,13},{13,9},{2,6},{6,2},{1... | collective-permute-start | bytes 1572872 | tf_op jit(solution)/shard_map/ppermute | solution.py:414
  8.3 35.7 %collective-permute-start.5 = (f32[1024,128]{1,0:T(8,128)S(1)}, f32[1024,128]{1,0:T(8,128)S(1)}, u32[]{:S(2)}, u32[]{:S(2)}) collective-permute-start(f32[1024,128]{1,0:T(8,128)S(1)} %pack.3), channel_id=1, source_target_pairs={{0,8},{4,12},{8,0},{12,4},{1,9},{5,13},{9,1},{13,5},{2,10},{6,14},... | collective-permute-start | bytes 1572872 | tf_op jit(solution)/shard_map/ppermute | solution.py:414
  15.2 4.2 %collective-permute-start.1 = (f32[112,128]{1,0:T(8,128)S(1)}, f32[112,128]{1,0:T(8,128)S(1)}, u32[]{:S(2)}, u32[]{:S(2)}) collective-permute-start(f32[112,128]{1,0:T(8,128)S(1)} %source_panels.1), channel_id=1, source_target_pairs={{0,2},{2,0},{1,3},{3,1},{4,6},{6,4},{5,7},{7,5},{8,10},{10,8},{9,1... | collective-permute-start | bytes 172040 | tf_op jit(solution)/shard_map/ppermute | solution.py:24
  23.8 24.9 %collective-permute-start.2 = (f32[768,128]{1,0:T(8,128)S(1)}, f32[768,128]{1,0:T(8,128)S(1)}, u32[]{:S(2)}, u32[]{:S(2)}) collective-permute-start(f32[768,128]{1,0:T(8,128)S(1)} %source_chunk.1), channel_id=1, source_target_pairs={{0,12},{4,8},{8,4},{12,0},{1,13},{5,9},{9,5},{13,1},{2,14},{6,10},... | collective-permute-start | bytes 1179656 | tf_op jit(solution)/shard_map/ppermute | solution.py:424
  31.6 4.1 %collective-permute-start.4 = (f32[80,128]{1,0:T(8,128)S(1)}, f32[80,128]{1,0:T(8,128)S(1)}, u32[]{:S(2)}, u32[]{:S(2)}) collective-permute-start(f32[80,128]{1,0:T(8,128)S(1)} %get-tuple-element.21), channel_id=1, source_target_pairs={{0,2},{2,0},{1,3},{3,1},{4,6},{6,4},{5,7},{7,5},{8,10},{10,8},{9,1... | collective-permute-start | bytes 122888 | tf_op jit(solution)/shard_map/ppermute | solution.py:24
  44.7 4.0 %collective-permute-start.6 = (f32[64,128]{1,0:T(8,128)S(1)}, f32[64,128]{1,0:T(8,128)S(1)}, u32[]{:S(2)}, u32[]{:S(2)}) collective-permute-start(f32[64,128]{1,0:T(8,128)S(1)} %get-tuple-element.26), channel_id=1, source_target_pairs={{0,2},{2,0},{1,3},{3,1},{4,6},{6,4},{5,7},{7,5},{8,10},{10,8},{9,1... | collective-permute-start | bytes 98312 | tf_op jit(solution)/shard_map/ppermute | solution.py:24

commit v13 on v12

--- a/solution.py
+++ b/solution.py
@@ -152,20 +152,26 @@
     return pl.CostEstimate(flops=rows * ROWS, bytes_accessed=rows * ROWS, transcendentals=0)
 
 
-def pack(x, piece):
-    def body(x_ref, o_ref, sem):
-        copies = piece.gather(x_ref, o_ref, sem)
-        start_all(copies)
-        wait_all(copies)
-
-    return pl.pallas_call(
-        body,
-        out_shape=piece.shape(),
+def pack(x, pieces):
+    listed = len(pieces)
+    rows = sum(piece.rows for piece in pieces)
+
+    def body(x_ref, *refs):
+        o_refs, sem = refs[:-1], refs[-1]
+        copies = [piece.gather(x_ref, o_refs[i], sem.at[i]) for i, piece in enumerate(pieces)]
+        for c in copies:
+            start_all(c)
+        for c in copies:
+            wait_all(c)
+
+    return pl.pallas_call(
+        body,
+        out_shape=[piece.shape() for piece in pieces],
         in_specs=[HBM],
-        out_specs=VMEM,
-        scratch_shapes=[pltpu.SemaphoreType.DMA],
-        compiler_params=params(piece.rows),
-        cost_estimate=cost(piece.rows),
+        out_specs=[VMEM] * listed,
+        scratch_shapes=[pltpu.SemaphoreType.DMA((listed,))],
+        compiler_params=params(rows),
+        cost_estimate=cost(rows),
         name="pack",
     )(x)
 
@@ -410,8 +416,8 @@
     first = lax.ppermute(pack_with_codes(x, head, pinned, code_rows), "basin", pairs[far])
     arrived = {head: first}
     far_codes = lax.all_gather(first[head.rows :], "mem", axis=0, tiled=True)
-    for piece in across + near:
-        arrived[piece] = lax.ppermute(pack(x, piece), "basin", pairs[piece.k])
+    for piece, chunk in zip(across + near, pack(x, across + near)):
+        arrived[piece] = lax.ppermute(chunk, "basin", pairs[piece.k])
 
     own = Piece(0, 0, members, sizes)
     source, source_codes, inflow = [late, own], [far_codes, codes], None

time: 50.2 us -> 50.2 us (level)
  waiting for transfers between devices: 18.3 us -> 19.5 us
  Pallas kernels: 14.5 us -> 13.6 us
    ppermute x1, waiting for transfers between devices: 1.89 us -> 2.84 us  [local(): lax.ppermute(pack_with_codes(x, head, pinned, code_rows), 'basin', pairs[...]
    pallas_call x2 -> x1, Pallas kernels: 2.11 us -> 1.22 us  [pack(): pl.pallas_call(body, out_shape=[piece.shape() for piece in pieces], in_sp...]
  transfers between devices with their start and end apart: 7 -> 7, of which waited for: 6 -> 6; matrix products, arithmetic and copies ran while one was open for 0% -> 0% of each run, Pallas kernels for 26% -> 24%
where the time goes in v13:
time: 50.2 us; the launch traced here: 49.7 us
  waiting for transfers between devices  19.5 us (39%)
  starting transfers between devices  14.6 us (29%)
  Pallas kernels  13.6 us (27%)
  blocking collectives  1.82 us (4%)
    ppermute x2, waiting for transfers between devices, local(): arrived[piece] = lax.ppermute(chunk, 'basin', pairs[piece.k])  11 us
    ppermute x3, waiting for transfers between devices, from_behind(): lax.ppermute(value, axis, [(i, (i + 1) % count) for i in range(count)])  5.65 us
    ppermute x1, starting transfers between devices, local(): lax.ppermute(pack_with_codes(x, head, pinned, code_rows), 'basin', pairs[...  5.11 us
    ppermute x3, starting transfers between devices, from_behind(): lax.ppermute(value, axis, [(i, (i + 1) % count) for i in range(count)])  4.98 us
    ppermute x1, starting transfers between devices, local(): lax.ppermute(source_chunk(x, late, far_codes, inflow), 'basin', pairs[far])  3.88 us
    ppermute x1, waiting for transfers between devices, local(): lax.ppermute(pack_with_codes(x, head, pinned, code_rows), 'basin', pairs[...  2.84 us
    pallas_call x1, Pallas kernels, own_result(): pl.pallas_call(body, out_shape=piece.sizes.result(), in_specs=[HBM, VMEM,...  2.6 us
    pallas_call x1, Pallas kernels, source_panels(): pl.pallas_call(body, out_shape=jax.ShapeDtypeStruct((starts[-1], ROWS), j...  2.58 us
  transfers between devices with their start and end apart: 7, of which 6 were waited for; matrix products, arithmetic and copies ran while one was open for 0% of the time, Pallas kernels for 24%

profile of v13, /device:TPU:0, one launch (start us, length us, event | category | flops | bytes accessed | tf_op | source)
XLA Modules:
  0.0 49.7 jit_solution(17942695189071260413)
XLA Ops:
  0.0 0.0 copy-start
  0.0 0.9 %pack_with_codes.1 = f32[288,128]{1,0:T(8,128)S(1)} custom-call(f32[16,256,128]{2,1,0:T(8,128)} %bitcast.10, s32[64,128]{1,0:T(8,128)} %bitcast.3), custom_call_target="tpu_custom_call" | custom-call | flops 32768 | bytes 32768 | tf_op jit(solution)/shard_map/pack_with_codes/pallas_call | solution.py:192
  1.0 5.1 %collective-permute-start = (f32[288,128]{1,0:T(8,128)S(1)}, f32[288,128]{1,0:T(8,128)S(1)}, u32[]{:S(2)}, u32[]{:S(2)}) collective-permute-start(f32[288,128]{1,0:T(8,128)S(1)} %pack_with_codes.1), channel_id=1, source_target_pairs={{0,12},{4,8},{8,4},{12,0},{1,13},{5,9},{9,5},{13,1},{2,14},{6,10},... | collective-permute-start | bytes 442376 | tf_op jit(solution)/shard_map/ppermute | solution.py:416
  6.1 1.2 %pack.1 = (f32[1024,128]{1,0:T(8,128)S(1)}, f32[1024,128]{1,0:T(8,128)S(1)}) custom-call(f32[16,256,128]{2,1,0:T(8,128)} %bitcast.11), custom_call_target="tpu_custom_call" | custom-call | flops 262144 | bytes 262144 | tf_op jit(solution)/shard_map/pack/pallas_call | solution.py:167
  7.3 0.1 collective-permute-start.3
  7.4 0.6 %collective-permute-start.5 = (f32[1024,128]{1,0:T(8,128)S(1)}, f32[1024,128]{1,0:T(8,128)S(1)}, u32[]{:S(2)}, u32[]{:S(2)}) collective-permute-start(f32[1024,128]{1,0:T(8,128)S(1)} %get-tuple-element.28), channel_id=1, source_target_pairs={{0,8},{4,12},{8,0},{12,4},{1,9},{5,13},{9,1},{13,5},{2,10},{6,14},... | collective-permute-start | bytes 1572872 | tf_op jit(solution)/shard_map/ppermute | solution.py:420
  8.0 2.8 %collective-permute-done.refs_0_ = f32[288,128]{1,0:T(8,128)S(1)} collective-permute-done((f32[288,128]{1,0:T(8,128)S(1)}, f32[288,128]{1,0:T(8,128)S(1)}, u32[]{:S(2)}, u32[]{:S(2)}) %collective-permute-start) | collective-permute-done | bytes 147488 | tf_op jit(solution)/shard_map/ppermute | solution.py:416
  10.8 1.8 %all_gather.3.refs_0_.d_ref = f32[64,128]{1,0:T(8,128)S(1)} all-gather(f32[32,128]{1,0:T(8,128)S(1)} %slice.4), channel_id=1, replica_groups=mesh['grp'=2,'basin'=4,'chain'=2,'mem'=2] {'mem'}, dimensions={0}, use_global_device_ids=true | all-gather | bytes 49152 | tf_op jit(solution)/shard_map/all_gather | solution.py:418
  12.6 0.0 copy-done
  12.6 2.6 %source_panels.1 = f32[112,128]{1,0:T(8,128)S(1)} custom-call(f32[16,256,128]{2,1,0:T(8,128)} %bitcast.12, f32[64,128]{1,0:T(8,128)S(1)} %all_gather.3.refs_0_.d_ref, s32[64,128]{1,0:T(8,128)S(1)} %bitcast.4), custom_call_target="tpu_custom_call" | custom-call | flops 229376 | bytes 229376 | tf_op jit(solution)/shard_map/source_panels/pallas_call | solution.py:225
  15.2 1.8 %collective-permute-start.1 = (f32[112,128]{1,0:T(8,128)S(1)}, f32[112,128]{1,0:T(8,128)S(1)}, u32[]{:S(2)}, u32[]{:S(2)}) collective-permute-start(f32[112,128]{1,0:T(8,128)S(1)} %source_panels.1), channel_id=1, source_target_pairs={{0,2},{2,0},{1,3},{3,1},{4,6},{6,4},{5,7},{7,5},{8,10},{10,8},{9,1... | collective-permute-start | bytes 172040 | tf_op jit(solution)/shard_map/ppermute | solution.py:24
  17.0 2.5 %collective-permute-done.1.in_ref = f32[112,128]{1,0:T(8,128)S(1)} collective-permute-done((f32[112,128]{1,0:T(8,128)S(1)}, f32[112,128]{1,0:T(8,128)S(1)}, u32[]{:S(2)}, u32[]{:S(2)}) %collective-permute-start.1) | collective-permute-done | bytes 57376 | tf_op jit(solution)/shard_map/ppermute | solution.py:24
  19.4 2.6 %own_result.1.refs_2_ = f32[256,16,128]{2,1,0:T(8,128)} custom-call(f32[16,256,128]{2,1,0:T(8,128)} %bitcast.13, s32[64,128]{1,0:T(8,128)S(1)} %bitcast.5, f32[112,128]{1,0:T(8,128)S(1)} %collective-permute-done.1.in_ref), custom_call_target="tpu_custom_call" | custom-call | flops 131072 | bytes 131072 | tf_op jit(solution)/shard_map/own_result/pallas_call | solution.py:331
  22.1 1.8 %source_chunk.1 = f32[768,128]{1,0:T(8,128)S(1)} custom-call(f32[16,256,128]{2,1,0:T(8,128)} %bitcast.14, f32[64,128]{1,0:T(8,128)S(1)} %all_gather.3.refs_0_.d_ref, f32[112,128]{1,0:T(8,128)S(1)} %collective-permute-done.1.in_ref), custom_call_target="tpu_custom_call" | custom-call | flops 98304 | bytes 98304 | tf_op jit(solution)/shard_map/source_chunk/pallas_call | solution.py:247
  23.8 3.9 %collective-permute-start.2 = (f32[768,128]{1,0:T(8,128)S(1)}, f32[768,128]{1,0:T(8,128)S(1)}, u32[]{:S(2)}, u32[]{:S(2)}) collective-permute-start(f32[768,128]{1,0:T(8,128)S(1)} %source_chunk.1), channel_id=1, source_target_pairs={{0,12},{4,8},{8,4},{12,0},{1,13},{5,9},{9,5},{13,1},{2,14},{6,10},... | collective-permute-start | bytes 1179656 | tf_op jit(solution)/shard_map/ppermute | solution.py:430
  27.7 2.7 %collective-permute-done.3.refs_1_ = f32[1024,128]{1,0:T(8,128)S(1)} collective-permute-done((f32[1024,128]{1,0:T(8,128)S(1)}, f32[1024,128]{1,0:T(8,128)S(1)}, u32[]{:S(2)}, u32[]{:S(2)}) %collective-permute-start.3) | collective-permute-done | bytes 524320 | tf_op jit(solution)/shard_map/ppermute | solution.py:420
  30.4 1.3 %arrived_panels.2 = (f32[80,128]{1,0:T(8,128)S(1)}, f32[256,128]{1,0:T(8,128)S(1)}, f32[1024,128]{1,0:T(8,128)S(1)}) custom-call(f32[288,128]{1,0:T(8,128)S(1)} %collective-permute-done.refs_0_, f32[1024,128]{1,0:T(8,128)S(1)} %collective-permute-done.3.refs_1_, s32[64,128]{1,0:T(8,128)S(1)} %bitcast.6), custom_call_target="tpu_custom_call" | custom-call | flops 163840 | bytes 163840 | tf_op jit(solution)/shard_map/arrived_panels/pallas_call | solution.py:283
  31.7 1.7 %collective-permute-start.4 = (f32[80,128]{1,0:T(8,128)S(1)}, f32[80,128]{1,0:T(8,128)S(1)}, u32[]{:S(2)}, u32[]{:S(2)}) collective-permute-start(f32[80,128]{1,0:T(8,128)S(1)} %get-tuple-element.24), channel_id=1, source_target_pairs={{0,2},{2,0},{1,3},{3,1},{4,6},{6,4},{5,7},{7,5},{8,10},{10,8},{9,1... | collective-permute-start | bytes 122888 | tf_op jit(solution)/shard_map/ppermute | solution.py:24
  33.4 0.9 %head_result.2.refs_4_ = f32[256,16,128]{2,1,0:T(8,128)} custom-call(f32[256,128]{1,0:T(8,128)S(1)} %get-tuple-element.25.refs_0_, f32[1024,128]{1,0:T(8,128)S(1)} %get-tuple-element.26.refs_1_, f32[256,16,128]{2,1,0:T(8,128)} %own_result.1.refs_2_), custom_call_target="tpu_custom_call", output_to_operand_aliasing={{}: (2, {})} | custom-call | flops 163840 | bytes 163840 | tf_op jit(solution)/shard_map/head_result/pallas_call | solution.py:308
  34.2 1.5 %collective-permute-done.4.refs_3_ = f32[80,128]{1,0:T(8,128)S(1)} collective-permute-done((f32[80,128]{1,0:T(8,128)S(1)}, f32[80,128]{1,0:T(8,128)S(1)}, u32[]{:S(2)}, u32[]{:S(2)}) %collective-permute-start.4) | collective-permute-done | bytes 40992 | tf_op jit(solution)/shard_map/ppermute | solution.py:24
  35.8 8.3 %collective-permute-done.5.refs_0_ = f32[1024,128]{1,0:T(8,128)S(1)} collective-permute-done((f32[1024,128]{1,0:T(8,128)S(1)}, f32[1024,128]{1,0:T(8,128)S(1)}, u32[]{:S(2)}, u32[]{:S(2)}) %collective-permute-start.5) | collective-permute-done | bytes 524320 | tf_op jit(solution)/shard_map/ppermute | solution.py:420
  44.1 0.7 %arrived_panels.3 = (f32[64,128]{1,0:T(8,128)S(1)}, f32[1024,128]{1,0:T(8,128)S(1)}) custom-call(f32[1024,128]{1,0:T(8,128)S(1)} %collective-permute-done.5.refs_0_, s32[64,128]{1,0:T(8,128)S(1)} %bitcast.8), custom_call_target="tpu_custom_call" | custom-call | flops 131072 | bytes 131072 | tf_op jit(solution)/shard_map/arrived_panels/pallas_call | solution.py:283
  44.9 1.6 %collective-permute-start.6 = (f32[64,128]{1,0:T(8,128)S(1)}, f32[64,128]{1,0:T(8,128)S(1)}, u32[]{:S(2)}, u32[]{:S(2)}) collective-permute-start(f32[64,128]{1,0:T(8,128)S(1)} %get-tuple-element.30), channel_id=1, source_target_pairs={{0,2},{2,0},{1,3},{3,1},{4,6},{6,4},{5,7},{7,5},{8,10},{10,8},{9,1... | collective-permute-start | bytes 98312 | tf_op jit(solution)/shard_map/ppermute | solution.py:24
  46.4 0.8 %head_result.3.refs_3_ = f32[256,16,128]{2,1,0:T(8,128)} custom-call(f32[1024,128]{1,0:T(8,128)S(1)} %get-tuple-element.31.refs_0_, f32[256,16,128]{2,1,0:T(8,128)} %arrived_result.2.refs_1_), custom_call_target="tpu_custom_call", output_to_operand_aliasing={{}: (1, {})} | custom-call | flops 131072 | bytes 131072 | tf_op jit(solution)/shard_map/head_result/pallas_call | solution.py:308
  47.2 1.6 %collective-permute-done.6.refs_2_ = f32[64,128]{1,0:T(8,128)S(1)} collective-permute-done((f32[64,128]{1,0:T(8,128)S(1)}, f32[64,128]{1,0:T(8,128)S(1)}, u32[]{:S(2)}, u32[]{:S(2)}) %collective-permute-start.6) | collective-permute-done | bytes 32800 | tf_op jit(solution)/shard_map/ppermute | solution.py:24
  48.9 0.0 collective-permute-done.2.x_ref
  48.9 0.8 %place_chunk.1 = f32[256,16,128]{2,1,0:T(8,128)} custom-call(f32[768,128]{1,0:T(8,128)S(1)} %collective-permute-done.2.x_ref, f32[256,16,128]{2,1,0:T(8,128)} %arrived_result.3._), custom_call_target="tpu_custom_call", output_to_operand_aliasing={{}: (1, {})} | custom-call | flops 98304 | bytes 98304 | tf_op jit(solution)/shard_map/place_chunk/pallas_call | solution.py:385
  (3 shorter events, 0.1 us)
Async XLA Ops:
  0.0 12.6 %copy-start = (s32[4,1,2048]{2,1,0:T(1,128)S(1)}, s32[4,1,2048]{2,1,0:T(1,128)}, u32[]{:S(2)}) copy-start(s32[4,1,2048]{2,1,0:T(1,128)} %param.3) | copy-start | bytes 98308
  1.0 9.8 %collective-permute-start = (f32[288,128]{1,0:T(8,128)S(1)}, f32[288,128]{1,0:T(8,128)S(1)}, u32[]{:S(2)}, u32[]{:S(2)}) collective-permute-start(f32[288,128]{1,0:T(8,128)S(1)} %pack_with_codes.1), channel_id=1, source_target_pairs={{0,12},{4,8},{8,4},{12,0},{1,13},{5,9},{9,5},{13,1},{2,14},{6,10},... | collective-permute-start | bytes 442376 | tf_op jit(solution)/shard_map/ppermute | solution.py:416
  7.3 23.1 %collective-permute-start.3 = (f32[1024,128]{1,0:T(8,128)S(1)}, f32[1024,128]{1,0:T(8,128)S(1)}, u32[]{:S(2)}, u32[]{:S(2)}) collective-permute-start(f32[1024,128]{1,0:T(8,128)S(1)} %get-tuple-element.21), channel_id=1, source_target_pairs={{0,4},{4,0},{8,12},{12,8},{1,5},{5,1},{9,13},{13,9},{2,6},{6,2},{1... | collective-permute-start | bytes 1572872 | tf_op jit(solution)/shard_map/ppermute | solution.py:420
  7.4 36.8 %collective-permute-start.5 = (f32[1024,128]{1,0:T(8,128)S(1)}, f32[1024,128]{1,0:T(8,128)S(1)}, u32[]{:S(2)}, u32[]{:S(2)}) collective-permute-start(f32[1024,128]{1,0:T(8,128)S(1)} %get-tuple-element.28), channel_id=1, source_target_pairs={{0,8},{4,12},{8,0},{12,4},{1,9},{5,13},{9,1},{13,5},{2,10},{6,14},... | collective-permute-start | bytes 1572872 | tf_op jit(solution)/shard_map/ppermute | solution.py:420
  15.2 4.2 %collective-permute-start.1 = (f32[112,128]{1,0:T(8,128)S(1)}, f32[112,128]{1,0:T(8,128)S(1)}, u32[]{:S(2)}, u32[]{:S(2)}) collective-permute-start(f32[112,128]{1,0:T(8,128)S(1)} %source_panels.1), channel_id=1, source_target_pairs={{0,2},{2,0},{1,3},{3,1},{4,6},{6,4},{5,7},{7,5},{8,10},{10,8},{9,1... | collective-permute-start | bytes 172040 | tf_op jit(solution)/shard_map/ppermute | solution.py:24
  23.8 25.0 %collective-permute-start.2 = (f32[768,128]{1,0:T(8,128)S(1)}, f32[768,128]{1,0:T(8,128)S(1)}, u32[]{:S(2)}, u32[]{:S(2)}) collective-permute-start(f32[768,128]{1,0:T(8,128)S(1)} %source_chunk.1), channel_id=1, source_target_pairs={{0,12},{4,8},{8,4},{12,0},{1,13},{5,9},{9,5},{13,1},{2,14},{6,10},... | collective-permute-start | bytes 1179656 | tf_op jit(solution)/shard_map/ppermute | solution.py:430
  31.7 4.1 %collective-permute-start.4 = (f32[80,128]{1,0:T(8,128)S(1)}, f32[80,128]{1,0:T(8,128)S(1)}, u32[]{:S(2)}, u32[]{:S(2)}) collective-permute-start(f32[80,128]{1,0:T(8,128)S(1)} %get-tuple-element.24), channel_id=1, source_target_pairs={{0,2},{2,0},{1,3},{3,1},{4,6},{6,4},{5,7},{7,5},{8,10},{10,8},{9,1... | collective-permute-start | bytes 122888 | tf_op jit(solution)/shard_map/ppermute | solution.py:24
  44.9 4.0 %collective-permute-start.6 = (f32[64,128]{1,0:T(8,128)S(1)}, f32[64,128]{1,0:T(8,128)S(1)}, u32[]{:S(2)}, u32[]{:S(2)}) collective-permute-start(f32[64,128]{1,0:T(8,128)S(1)} %get-tuple-element.30), channel_id=1, source_target_pairs={{0,2},{2,0},{1,3},{3,1},{4,6},{6,4},{5,7},{7,5},{8,10},{10,8},{9,1... | collective-permute-start | bytes 98312 | tf_op jit(solution)/shard_map/ppermute | solution.py:24

commit v14 on v12

--- a/solution.py
+++ b/solution.py
@@ -172,13 +172,13 @@
 
 def pack_with_codes(x, piece, codes, code_rows):
     def body(x_ref, d_ref, o_ref, buf, sem, code_sem):
-        copies = piece.gather(x_ref, o_ref, sem)
-        start_all(copies)
         shares = codes.shape[0] // code_rows
         share = lax.axis_index("mem") if shares > 1 else 0
         mine = d_ref.at[pl.ds(pl.multiple_of(share * code_rows, code_rows), code_rows)]
         copy = pltpu.make_async_copy(mine, buf, code_sem)
         copy.start()
+        copies = piece.gather(x_ref, o_ref, sem)
+        start_all(copies)
         copy.wait()
         o_ref[pl.ds(piece.rows, code_rows), :] = buf[...].astype(jnp.float32)
         wait_all(copies)

time: 50.2 us -> 50.2 us (level)
  no operation moved by 1% of the time
where the time goes in v14:
time: 50.2 us; the launch traced here: 49.5 us
  waiting for transfers between devices  18.3 us (36%)
  starting transfers between devices  14.7 us (29%)
  Pallas kernels  14.5 us (29%)
  blocking collectives  1.82 us (4%)
    ppermute x2, waiting for transfers between devices, local(): arrived[piece] = lax.ppermute(pack(x, piece), 'basin', pairs[piece.k])  10.8 us
    ppermute x3, waiting for transfers between devices, from_behind(): lax.ppermute(value, axis, [(i, (i + 1) % count) for i in range(count)])  5.64 us
    ppermute x1, starting transfers between devices, local(): lax.ppermute(pack_with_codes(x, head, pinned, code_rows), 'basin', pairs[...  5.11 us
    ppermute x3, starting transfers between devices, from_behind(): lax.ppermute(value, axis, [(i, (i + 1) % count) for i in range(count)])  4.98 us
    ppermute x1, starting transfers between devices, local(): lax.ppermute(source_chunk(x, late, far_codes, inflow), 'basin', pairs[far])  3.88 us
    pallas_call x1, Pallas kernels, own_result(): pl.pallas_call(body, out_shape=piece.sizes.result(), in_specs=[HBM, VMEM,...  2.6 us
    pallas_call x1, Pallas kernels, source_panels(): pl.pallas_call(body, out_shape=jax.ShapeDtypeStruct((starts[-1], ROWS), j...  2.58 us
    pallas_call x2, Pallas kernels, pack(): pl.pallas_call(body, out_shape=piece.shape(), in_specs=[HBM], out_specs=V...  2.11 us
  transfers between devices with their start and end apart: 7, of which 6 were waited for; matrix products, arithmetic and copies ran while one was open for 0% of the time, Pallas kernels for 26%

profile of v14, /device:TPU:0, one launch (start us, length us, event | category | flops | bytes accessed | tf_op | source)
XLA Modules:
  0.0 49.5 jit_solution(2559353752717587449)
XLA Ops:
  0.0 0.9 %pack_with_codes.1 = f32[288,128]{1,0:T(8,128)S(1)} custom-call(f32[16,256,128]{2,1,0:T(8,128)} %bitcast.10, s32[64,128]{1,0:T(8,128)} %bitcast.3), custom_call_target="tpu_custom_call" | custom-call | flops 32768 | bytes 32768 | tf_op jit(solution)/shard_map/pack_with_codes/pallas_call | solution.py:186
  0.9 0.0 copy-start
  1.0 5.1 %collective-permute-start = (f32[288,128]{1,0:T(8,128)S(1)}, f32[288,128]{1,0:T(8,128)S(1)}, u32[]{:S(2)}, u32[]{:S(2)}) collective-permute-start(f32[288,128]{1,0:T(8,128)S(1)} %pack_with_codes.1), channel_id=1, source_target_pairs={{0,12},{4,8},{8,4},{12,0},{1,13},{5,9},{9,5},{13,1},{2,14},{6,10},... | collective-permute-start | bytes 442376 | tf_op jit(solution)/shard_map/ppermute | solution.py:410
  6.1 1.0 %pack.2 = f32[1024,128]{1,0:T(8,128)S(1)} custom-call(f32[16,256,128]{2,1,0:T(8,128)} %bitcast.11), custom_call_target="tpu_custom_call" | custom-call | flops 131072 | bytes 131072 | tf_op jit(solution)/shard_map/pack/pallas_call | solution.py:161
  7.1 0.1 collective-permute-start.3
  7.2 1.1 %pack.3 = f32[1024,128]{1,0:T(8,128)S(1)} custom-call(f32[16,256,128]{2,1,0:T(8,128)} %bitcast.12), custom_call_target="tpu_custom_call" | custom-call | flops 131072 | bytes 131072 | tf_op jit(solution)/shard_map/pack/pallas_call | solution.py:161
  8.3 0.6 %collective-permute-start.5 = (f32[1024,128]{1,0:T(8,128)S(1)}, f32[1024,128]{1,0:T(8,128)S(1)}, u32[]{:S(2)}, u32[]{:S(2)}) collective-permute-start(f32[1024,128]{1,0:T(8,128)S(1)} %pack.3), channel_id=1, source_target_pairs={{0,8},{4,12},{8,0},{12,4},{1,9},{5,13},{9,1},{13,5},{2,10},{6,14},... | collective-permute-start | bytes 1572872 | tf_op jit(solution)/shard_map/ppermute | solution.py:414
  8.9 1.9 %collective-permute-done.refs_0_ = f32[288,128]{1,0:T(8,128)S(1)} collective-permute-done((f32[288,128]{1,0:T(8,128)S(1)}, f32[288,128]{1,0:T(8,128)S(1)}, u32[]{:S(2)}, u32[]{:S(2)}) %collective-permute-start) | collective-permute-done | bytes 147488 | tf_op jit(solution)/shard_map/ppermute | solution.py:410
  10.8 1.8 %all_gather.3.refs_0_.d_ref = f32[64,128]{1,0:T(8,128)S(1)} all-gather(f32[32,128]{1,0:T(8,128)S(1)} %slice.4), channel_id=1, replica_groups=mesh['grp'=2,'basin'=4,'chain'=2,'mem'=2] {'mem'}, dimensions={0}, use_global_device_ids=true | all-gather | bytes 49152 | tf_op jit(solution)/shard_map/all_gather | solution.py:412
  12.6 0.0 copy-done
  12.6 2.6 %source_panels.1 = f32[112,128]{1,0:T(8,128)S(1)} custom-call(f32[16,256,128]{2,1,0:T(8,128)} %bitcast.13, f32[64,128]{1,0:T(8,128)S(1)} %all_gather.3.refs_0_.d_ref, s32[64,128]{1,0:T(8,128)S(1)} %bitcast.4), custom_call_target="tpu_custom_call" | custom-call | flops 229376 | bytes 229376 | tf_op jit(solution)/shard_map/source_panels/pallas_call | solution.py:219
  15.2 1.8 %collective-permute-start.1 = (f32[112,128]{1,0:T(8,128)S(1)}, f32[112,128]{1,0:T(8,128)S(1)}, u32[]{:S(2)}, u32[]{:S(2)}) collective-permute-start(f32[112,128]{1,0:T(8,128)S(1)} %source_panels.1), channel_id=1, source_target_pairs={{0,2},{2,0},{1,3},{3,1},{4,6},{6,4},{5,7},{7,5},{8,10},{10,8},{9,1... | collective-permute-start | bytes 172040 | tf_op jit(solution)/shard_map/ppermute | solution.py:24
  17.0 2.5 %collective-permute-done.1.in_ref = f32[112,128]{1,0:T(8,128)S(1)} collective-permute-done((f32[112,128]{1,0:T(8,128)S(1)}, f32[112,128]{1,0:T(8,128)S(1)}, u32[]{:S(2)}, u32[]{:S(2)}) %collective-permute-start.1) | collective-permute-done | bytes 57376 | tf_op jit(solution)/shard_map/ppermute | solution.py:24
  19.4 2.6 %own_result.1.refs_2_ = f32[256,16,128]{2,1,0:T(8,128)} custom-call(f32[16,256,128]{2,1,0:T(8,128)} %bitcast.14, s32[64,128]{1,0:T(8,128)S(1)} %bitcast.5, f32[112,128]{1,0:T(8,128)S(1)} %collective-permute-done.1.in_ref), custom_call_target="tpu_custom_call" | custom-call | flops 131072 | bytes 131072 | tf_op jit(solution)/shard_map/own_result/pallas_call | solution.py:325
  22.1 1.8 %source_chunk.1 = f32[768,128]{1,0:T(8,128)S(1)} custom-call(f32[16,256,128]{2,1,0:T(8,128)} %bitcast.15, f32[64,128]{1,0:T(8,128)S(1)} %all_gather.3.refs_0_.d_ref, f32[112,128]{1,0:T(8,128)S(1)} %collective-permute-done.1.in_ref), custom_call_target="tpu_custom_call" | custom-call | flops 98304 | bytes 98304 | tf_op jit(solution)/shard_map/source_chunk/pallas_call | solution.py:241
  23.8 3.9 %collective-permute-start.2 = (f32[768,128]{1,0:T(8,128)S(1)}, f32[768,128]{1,0:T(8,128)S(1)}, u32[]{:S(2)}, u32[]{:S(2)}) collective-permute-start(f32[768,128]{1,0:T(8,128)S(1)} %source_chunk.1), channel_id=1, source_target_pairs={{0,12},{4,8},{8,4},{12,0},{1,13},{5,9},{9,5},{13,1},{2,14},{6,10},... | collective-permute-start | bytes 1179656 | tf_op jit(solution)/shard_map/ppermute | solution.py:424
  27.7 2.6 %collective-permute-done.3.refs_1_ = f32[1024,128]{1,0:T(8,128)S(1)} collective-permute-done((f32[1024,128]{1,0:T(8,128)S(1)}, f32[1024,128]{1,0:T(8,128)S(1)}, u32[]{:S(2)}, u32[]{:S(2)}) %collective-permute-start.3) | collective-permute-done | bytes 524320 | tf_op jit(solution)/shard_map/ppermute | solution.py:414
  30.3 1.3 %arrived_panels.2 = (f32[80,128]{1,0:T(8,128)S(1)}, f32[256,128]{1,0:T(8,128)S(1)}, f32[1024,128]{1,0:T(8,128)S(1)}) custom-call(f32[288,128]{1,0:T(8,128)S(1)} %collective-permute-done.refs_0_, f32[1024,128]{1,0:T(8,128)S(1)} %collective-permute-done.3.refs_1_, s32[64,128]{1,0:T(8,128)S(1)} %bitcast.6), custom_call_target="tpu_custom_call" | custom-call | flops 163840 | bytes 163840 | tf_op jit(solution)/shard_map/arrived_panels/pallas_call | solution.py:277
  31.6 1.7 %collective-permute-start.4 = (f32[80,128]{1,0:T(8,128)S(1)}, f32[80,128]{1,0:T(8,128)S(1)}, u32[]{:S(2)}, u32[]{:S(2)}) collective-permute-start(f32[80,128]{1,0:T(8,128)S(1)} %get-tuple-element.21), channel_id=1, source_target_pairs={{0,2},{2,0},{1,3},{3,1},{4,6},{6,4},{5,7},{7,5},{8,10},{10,8},{9,1... | collective-permute-start | bytes 122888 | tf_op jit(solution)/shard_map/ppermute | solution.py:24
  33.3 0.9 %head_result.2.refs_4_ = f32[256,16,128]{2,1,0:T(8,128)} custom-call(f32[256,128]{1,0:T(8,128)S(1)} %get-tuple-element.22.refs_0_, f32[1024,128]{1,0:T(8,128)S(1)} %get-tuple-element.23.refs_1_, f32[256,16,128]{2,1,0:T(8,128)} %own_result.1.refs_2_), custom_call_target="tpu_custom_call", output_to_operand_aliasing={{}: (2, {})} | custom-call | flops 163840 | bytes 163840 | tf_op jit(solution)/shard_map/head_result/pallas_call | solution.py:302
  34.1 1.5 %collective-permute-done.4.refs_3_ = f32[80,128]{1,0:T(8,128)S(1)} collective-permute-done((f32[80,128]{1,0:T(8,128)S(1)}, f32[80,128]{1,0:T(8,128)S(1)}, u32[]{:S(2)}, u32[]{:S(2)}) %collective-permute-start.4) | collective-permute-done | bytes 40992 | tf_op jit(solution)/shard_map/ppermute | solution.py:24
  35.7 8.2 %collective-permute-done.5.refs_0_ = f32[1024,128]{1,0:T(8,128)S(1)} collective-permute-done((f32[1024,128]{1,0:T(8,128)S(1)}, f32[1024,128]{1,0:T(8,128)S(1)}, u32[]{:S(2)}, u32[]{:S(2)}) %collective-permute-start.5) | collective-permute-done | bytes 524320 | tf_op jit(solution)/shard_map/ppermute | solution.py:414
  43.9 0.7 %arrived_panels.3 = (f32[64,128]{1,0:T(8,128)S(1)}, f32[1024,128]{1,0:T(8,128)S(1)}) custom-call(f32[1024,128]{1,0:T(8,128)S(1)} %collective-permute-done.5.refs_0_, s32[64,128]{1,0:T(8,128)S(1)} %bitcast.8), custom_call_target="tpu_custom_call" | custom-call | flops 131072 | bytes 131072 | tf_op jit(solution)/shard_map/arrived_panels/pallas_call | solution.py:277
  44.7 1.6 %collective-permute-start.6 = (f32[64,128]{1,0:T(8,128)S(1)}, f32[64,128]{1,0:T(8,128)S(1)}, u32[]{:S(2)}, u32[]{:S(2)}) collective-permute-start(f32[64,128]{1,0:T(8,128)S(1)} %get-tuple-element.26), channel_id=1, source_target_pairs={{0,2},{2,0},{1,3},{3,1},{4,6},{6,4},{5,7},{7,5},{8,10},{10,8},{9,1... | collective-permute-start | bytes 98312 | tf_op jit(solution)/shard_map/ppermute | solution.py:24
  46.3 0.8 %head_result.3.refs_3_ = f32[256,16,128]{2,1,0:T(8,128)} custom-call(f32[1024,128]{1,0:T(8,128)S(1)} %get-tuple-element.27.refs_0_, f32[256,16,128]{2,1,0:T(8,128)} %arrived_result.2.refs_1_), custom_call_target="tpu_custom_call", output_to_operand_aliasing={{}: (1, {})} | custom-call | flops 131072 | bytes 131072 | tf_op jit(solution)/shard_map/head_result/pallas_call | solution.py:302
  47.1 1.6 %collective-permute-done.6.refs_2_ = f32[64,128]{1,0:T(8,128)S(1)} collective-permute-done((f32[64,128]{1,0:T(8,128)S(1)}, f32[64,128]{1,0:T(8,128)S(1)}, u32[]{:S(2)}, u32[]{:S(2)}) %collective-permute-start.6) | collective-permute-done | bytes 32800 | tf_op jit(solution)/shard_map/ppermute | solution.py:24
  48.7 0.0 collective-permute-done.2.x_ref
  48.7 0.8 %place_chunk.1 = f32[256,16,128]{2,1,0:T(8,128)} custom-call(f32[768,128]{1,0:T(8,128)S(1)} %collective-permute-done.2.x_ref, f32[256,16,128]{2,1,0:T(8,128)} %arrived_result.3._), custom_call_target="tpu_custom_call", output_to_operand_aliasing={{}: (1, {})} | custom-call | flops 98304 | bytes 98304 | tf_op jit(solution)/shard_map/place_chunk/pallas_call | solution.py:379
  (3 shorter events, 0.1 us)
Async XLA Ops:
  0.9 11.7 %copy-start = (s32[4,1,2048]{2,1,0:T(1,128)S(1)}, s32[4,1,2048]{2,1,0:T(1,128)}, u32[]{:S(2)}) copy-start(s32[4,1,2048]{2,1,0:T(1,128)} %param.3) | copy-start | bytes 98308
  1.0 9.8 %collective-permute-start = (f32[288,128]{1,0:T(8,128)S(1)}, f32[288,128]{1,0:T(8,128)S(1)}, u32[]{:S(2)}, u32[]{:S(2)}) collective-permute-start(f32[288,128]{1,0:T(8,128)S(1)} %pack_with_codes.1), channel_id=1, source_target_pairs={{0,12},{4,8},{8,4},{12,0},{1,13},{5,9},{9,5},{13,1},{2,14},{6,10},... | collective-permute-start | bytes 442376 | tf_op jit(solution)/shard_map/ppermute | solution.py:410
  7.1 23.2 %collective-permute-start.3 = (f32[1024,128]{1,0:T(8,128)S(1)}, f32[1024,128]{1,0:T(8,128)S(1)}, u32[]{:S(2)}, u32[]{:S(2)}) collective-permute-start(f32[1024,128]{1,0:T(8,128)S(1)} %pack.2), channel_id=1, source_target_pairs={{0,4},{4,0},{8,12},{12,8},{1,5},{5,1},{9,13},{13,9},{2,6},{6,2},{1... | collective-permute-start | bytes 1572872 | tf_op jit(solution)/shard_map/ppermute | solution.py:414
  8.3 35.7 %collective-permute-start.5 = (f32[1024,128]{1,0:T(8,128)S(1)}, f32[1024,128]{1,0:T(8,128)S(1)}, u32[]{:S(2)}, u32[]{:S(2)}) collective-permute-start(f32[1024,128]{1,0:T(8,128)S(1)} %pack.3), channel_id=1, source_target_pairs={{0,8},{4,12},{8,0},{12,4},{1,9},{5,13},{9,1},{13,5},{2,10},{6,14},... | collective-permute-start | bytes 1572872 | tf_op jit(solution)/shard_map/ppermute | solution.py:414
  15.2 4.2 %collective-permute-start.1 = (f32[112,128]{1,0:T(8,128)S(1)}, f32[112,128]{1,0:T(8,128)S(1)}, u32[]{:S(2)}, u32[]{:S(2)}) collective-permute-start(f32[112,128]{1,0:T(8,128)S(1)} %source_panels.1), channel_id=1, source_target_pairs={{0,2},{2,0},{1,3},{3,1},{4,6},{6,4},{5,7},{7,5},{8,10},{10,8},{9,1... | collective-permute-start | bytes 172040 | tf_op jit(solution)/shard_map/ppermute | solution.py:24
  23.8 24.9 %collective-permute-start.2 = (f32[768,128]{1,0:T(8,128)S(1)}, f32[768,128]{1,0:T(8,128)S(1)}, u32[]{:S(2)}, u32[]{:S(2)}) collective-permute-start(f32[768,128]{1,0:T(8,128)S(1)} %source_chunk.1), channel_id=1, source_target_pairs={{0,12},{4,8},{8,4},{12,0},{1,13},{5,9},{9,5},{13,1},{2,14},{6,10},... | collective-permute-start | bytes 1179656 | tf_op jit(solution)/shard_map/ppermute | solution.py:424
  31.6 4.1 %collective-permute-start.4 = (f32[80,128]{1,0:T(8,128)S(1)}, f32[80,128]{1,0:T(8,128)S(1)}, u32[]{:S(2)}, u32[]{:S(2)}) collective-permute-start(f32[80,128]{1,0:T(8,128)S(1)} %get-tuple-element.21), channel_id=1, source_target_pairs={{0,2},{2,0},{1,3},{3,1},{4,6},{6,4},{5,7},{7,5},{8,10},{10,8},{9,1... | collective-permute-start | bytes 122888 | tf_op jit(solution)/shard_map/ppermute | solution.py:24
  44.7 4.0 %collective-permute-start.6 = (f32[64,128]{1,0:T(8,128)S(1)}, f32[64,128]{1,0:T(8,128)S(1)}, u32[]{:S(2)}, u32[]{:S(2)}) collective-permute-start(f32[64,128]{1,0:T(8,128)S(1)} %get-tuple-element.26), channel_id=1, source_target_pairs={{0,2},{2,0},{1,3},{3,1},{4,6},{6,4},{5,7},{7,5},{8,10},{10,8},{9,1... | collective-permute-start | bytes 98312 | tf_op jit(solution)/shard_map/ppermute | solution.py:24
